TPU v7x, 32 devices: a whole 2x2x4 slice. The times are simulated.
32 devices in a mesh: ctx: 8 (over z, y), uly: 4 (over x, core).
Axes of the slice: x: 2, y: 2, z: 4, core: 2. Of those that a mesh axis runs over, the one named last changes fastest.
Arguments:
- byte_embed: bfloat16 [24576, 768], P(('ctx', 'uly')), may hold values from -6 to 6
- query_weight: bfloat16 [768, 768], P(('ctx', 'uly')), may hold values from -0.109375 to 0.109375
- key_weight: bfloat16 [768, 768], P(('ctx', 'uly')), may hold values from -0.109375 to 0.109375
- value_weight: bfloat16 [768, 768], P(('ctx', 'uly')), may hold values from -0.21875 to 0.21875
- merge_weight: bfloat16 [768, 768], P(('ctx', 'uly')), may hold values from -0.625 to 0.625
- gate_weight: bfloat16 [768, 2048], P(('ctx', 'uly')), may hold values from -0.21875 to 0.21875
- up_weight: bfloat16 [768, 2048], P(('ctx', 'uly')), may hold values from -0.21875 to 0.21875
- down_weight: bfloat16 [2048, 768], P(('ctx', 'uly')), may hold values from -0.25 to 0.25
- conv_weight: float32 [5, 768], replicated, may hold values from -3 to 3
- score_weight: float32 [768], replicated, may hold values from -0.4375 to 0.4375
- attn_gain: float32 [768], replicated, may hold values from 0.1 to 1.9
- ffn_gain: float32 [768], replicated, may hold values from 0.1 to 1.9
- bias_table: float32 [32, 12], replicated, may hold values from -4 to 4
- doc_lengths: int32 [23], replicated, may hold values from 1 to 2048, as said below
- rel_bucket: int32 [2047], replicated, may hold values from 0 to 31
- out_grad: bfloat16 [12288, 768], P(('ctx', 'uly')), may hold values from -6 to 6
Outputs:
- layer_out: bfloat16 [12288, 768], P(('ctx', 'uly'))
- embed_grad: float32 [24576, 768], P(('ctx', 'uly'))
- query_grad: float32 [768, 768], P(('ctx', 'uly'))
- key_grad: float32 [768, 768], P(('ctx', 'uly'))
- value_grad: float32 [768, 768], P(('ctx', 'uly'))
- merge_grad: float32 [768, 768], P(('ctx', 'uly'))
- gate_grad: float32 [768, 2048], P(('ctx', 'uly'))
- up_grad: float32 [768, 2048], P(('ctx', 'uly'))
- down_grad: float32 [2048, 768], P(('ctx', 'uly'))
- conv_grad: float32 [5, 768], replicated
- score_grad: float32 [768], replicated
- attn_gain_grad: float32 [768], replicated
- ffn_gain_grad: float32 [768], replicated
- table_grad: float32 [32, 12], replicated
Inputs may be any that keep to these rules, and one draw needn't show every extreme that they name: `doc_lengths`: the documents lie end to end over the 24576 bytes in this order; the longest has exactly 2048 bytes; at every multiple of 3072 inside the stream a document of exactly 2048 bytes begins between 768 and 1280 bytes before it. `rel_bucket`: entry r is the bucket of the key-minus-query offset r - 1023.
All inputs are finite; a program needn't handle non-finite values.
Results may differ from a plain program's by a relative error of at most 0.02.
Values may be sent and summed in bfloat16 or wider, within the bound.
No kernel may reach another device: no remote copies, remote signals or barrier semaphores. Data moves between devices by JAX's collectives and lax.ppermute only.
A program may use at most 448 MiB of HBM per device.

v0:
```python
from functools import partial

import jax
import jax.numpy as jnp
from jax import lax
from jax.experimental import pallas as pl
from jax.experimental.pallas import tpu as pltpu
from jax.sharding import Mesh, PartitionSpec as P

HEADS = 12
HEAD_DIM = 64
NBUCK = 32
CONV = 5
DOC_TOK = 1024
TILE = 256
FORM = 16
PHASES = 12
EPS = 1e-06
BIG = 1e30
GELU_C = 0.7978845608028654
GELU_A = 0.044715

bf16 = jnp.bfloat16
f32 = jnp.float32
RING = ("ctx", "ux", "uc")
ULY = ("ux", "uc")
highest = lax.Precision.HIGHEST


def dot(left, right, dims=((1,), (0,))):
    return lax.dot_general(left, right, (dims, ((), ())), preferred_element_type=f32)


def kernel_call(body, outs, *, grid=(1,), ins, scratch=(), prefetch=0, out_specs=None, flops=0, moved=0, name=None):
    params = pltpu.CompilerParams(
        dimension_semantics=("arbitrary",) * len(grid), vmem_limit_bytes=56 << 20
    )
    return pl.pallas_call(
        body,
        out_shape=outs,
        grid_spec=pltpu.PrefetchScalarGridSpec(
            num_scalar_prefetch=prefetch,
            grid=grid,
            in_specs=ins,
            out_specs=out_specs,
            scratch_shapes=list(scratch),
        ),
        compiler_params=params,
        cost_estimate=pl.CostEstimate(flops=int(flops), bytes_accessed=int(moved), transcendentals=0),
        name=name,
    )


def whole(shape, once=True):
    zeros = (0,) * len(shape)
    if once:
        return pl.BlockSpec(shape, lambda *a: zeros, pipeline_mode=pl.Buffered(1))
    return pl.BlockSpec(shape, lambda *a: zeros)


def struct(shape, dtype):
    return jax.ShapeDtypeStruct(shape, dtype)


def block_of(size, at):
    first = size * (at // size)
    return range(first, first + size)


def token_pairs(tok):
    found = set()
    for byte in (2 * tok, 2 * tok + 1):
        for size in range(1, 5):
            found |= set(block_of(size, byte))
    return sorted(found)


def mix_coefs(weights):
    coefs = {}
    for tok in range(PHASES // 2):
        for at in token_pairs(tok):
            total = None
            for byte in (2 * tok, 2 * tok + 1):
                for size in range(1, 5):
                    if at in block_of(size, byte):
                        term = weights[size - 1][byte] * (0.5 / size)
                        total = term if total is None else total + term
            coefs[tok, at] = total
    return coefs


def lane_chunks(feats):
    return [slice(128 * c, 128 * (c + 1)) for c in range(feats // 128)]


def fill_bytes(pad, lo, emb, hi):
    byte_count, feats = emb.shape
    chunks = lane_chunks(feats)
    for c, cols in enumerate(chunks):
        pad[c, 0:8, :] = lo[:, cols].astype(f32)
        pad[c, 8 + byte_count : 16 + byte_count, :] = hi[:, cols].astype(f32)

    def fill(t, _):
        at = pl.multiple_of(t * 32, 32)
        for c, cols in enumerate(chunks):
            pad[c, pl.ds(at + 8, 32), :] = emb[pl.ds(at, 32), cols].astype(f32)
        return 0

    lax.fori_loop(0, byte_count // 32, fill, 0)


def gbst_forward_kernel(lo, emb, hi, msk, cw, sw, gain, gb, nrm, conv, aw, pad, mix):
    byte_count, feats = emb.shape
    chunks = lane_chunks(feats)
    fill_bytes(pad, lo, emb, hi)
    lanes = lax.broadcasted_iota(jnp.int32, (8, 128), 1)

    def step(g, _):
        base = g * 8 * PHASES + 8
        rows = pl.ds(pl.multiple_of(8 * g, 8), 8)
        first = []
        for p in range(PHASES):
            mask = msk[pl.ds(base + p, 8, stride=PHASES), :]
            same = {k: mask[:, k : k + 1] for k in (0, 1, 3, 4)}
            dots = None
            for c, cols in enumerate(chunks):
                x = pad[c, pl.ds(base + p, 8, stride=PHASES), :] * cw[2:3, cols]
                for k in (0, 1, 3, 4):
                    x = x + pad[c, pl.ds(base + p + k - 2, 8, stride=PHASES), :] * same[k] * cw[k : k + 1, cols]
                conv[p, rows, cols] = x
                term = x * sw[:, cols]
                dots = term if dots is None else dots + term
            first.append(jnp.sum(dots, axis=1, keepdims=True))
        weights = [[None] * PHASES for _ in range(4)]
        packed = jnp.zeros((8, 128), f32)
        for p in range(PHASES):
            scores = []
            for size in range(1, 5):
                total = None
                for at in block_of(size, p):
                    total = first[at] if total is None else total + first[at]
                scores.append(total * (1.0 / size))
            top = jnp.maximum(jnp.maximum(scores[0], scores[1]), jnp.maximum(scores[2], scores[3]))
            exps = [jnp.exp(s - top) for s in scores]
            inv = 1.0 / (exps[0] + exps[1] + exps[2] + exps[3])
            for size in range(4):
                weights[size][p] = exps[size] * inv
                packed = jnp.where(lanes == 4 * p + size, weights[size][p], packed)
        aw[rows, :] = packed
        coefs = mix_coefs(weights)
        for tok in range(PHASES // 2):
            for c, cols in enumerate(chunks):
                out = None
                for at in token_pairs(tok):
                    term = coefs[tok, at] * conv[at, rows, cols]
                    out = term if out is None else out + term
                mix[c, pl.ds(g * 4 * PHASES + tok, 8, stride=PHASES // 2), :] = out
        return 0

    lax.fori_loop(0, byte_count // (8 * PHASES), step, 0)

    def norm(t, _):
        at = pl.multiple_of(t * 16, 16)
        v = jnp.concatenate([mix[c, pl.ds(at, 16), :] for c in range(len(chunks))], axis=1)
        r = lax.rsqrt(jnp.mean(v * v, axis=1, keepdims=True) + EPS)
        gb[pl.ds(at, 16), :] = v
        nrm[pl.ds(at, 16), :] = (v * r * gain[...]).astype(bf16)
        return 0

    lax.fori_loop(0, byte_count // 32, norm, 0)


def gbst_forward(lo, emb, hi, msk, cw, sw, gain):
    nb, d = emb.shape
    return kernel_call(
        gbst_forward_kernel,
        (
            struct((nb // 2, d), f32),
            struct((nb // 2, d), bf16),
            struct((PHASES, nb // PHASES, d), f32),
            struct((nb // PHASES, 128), f32),
        ),
        ins=[whole(x.shape) for x in (lo, emb, hi, msk, cw, sw, gain)],
        out_specs=(
            whole((nb // 2, d), False),
            whole((nb // 2, d), False),
            whole((PHASES, nb // PHASES, d), False),
            whole((nb // PHASES, 128), False),
        ),
        scratch=[pltpu.VMEM((d // 128, nb + 16, 128), f32), pltpu.VMEM((d // 128, nb // 2, 128), f32)],
        flops=60 * nb * d,
        moved=20 * nb * d,
        name="gbst_forward",
    )(lo, emb, hi, msk, cw, sw, gain)


def gbst_backward_kernel(keep, recv, gb, dmid, gain, conv, aw, lo, emb, hi, msk, cw, sw, eg, small, dtok, dconv, pad, acc):
    byte_count, feats = emb.shape
    chunks = lane_chunks(feats)
    acc[...] = jnp.zeros_like(acc)
    fill_bytes(pad, lo, emb, hi)
    for c in range(len(chunks)):
        dconv[c, 0:16, :] = jnp.zeros((16, 128), f32)
        dconv[c, 16 + byte_count : 32 + byte_count, :] = jnp.zeros((16, 128), f32)

    def norm(t, _):
        at = pl.multiple_of(t * 16, 16)
        e = keep[pl.ds(at, 16), :] + recv[pl.ds(at, 16), :].astype(f32)
        v = gb[pl.ds(at, 16), :]
        r = lax.rsqrt(jnp.mean(v * v, axis=1, keepdims=True) + EPS)
        ge = gain[...] * e
        m = jnp.mean(ge * v, axis=1, keepdims=True)
        out = dmid[pl.ds(at, 16), :] + r * ge - v * (r * r * r * m)
        for c, cols in enumerate(chunks):
            dtok[c, pl.ds(at, 16), :] = out[:, cols]
        part = e * v * r
        acc[48:56, :] = acc[48:56, :] + part[0:8] + part[8:16]
        return 0

    lax.fori_loop(0, byte_count // 32, norm, 0)

    def step(g, _):
        rows = pl.ds(pl.multiple_of(8 * g, 8), 8)
        half = PHASES // 2

        def tok_rows(tok, c):
            return dtok[c, pl.ds(g * 8 * half + tok, 8, stride=half), :]

        inner = {}
        for tok in range(half):
            toks = [tok_rows(tok, c) for c in range(len(chunks))]
            for at in token_pairs(tok):
                dots = None
                for c, cols in enumerate(chunks):
                    term = toks[c] * conv[at, rows, cols]
                    dots = term if dots is None else dots + term
                inner[tok, at] = jnp.sum(dots, axis=1, keepdims=True)
        tile = aw[rows, :]
        weights = [[tile[:, 4 * p + size : 4 * p + size + 1] for p in range(PHASES)] for size in range(4)]
        coefs = mix_coefs(weights)
        dsize = [[None] * PHASES for _ in range(4)]
        for p in range(PHASES):
            cs = []
            for size in range(1, 5):
                total = None
                for at in block_of(size, p):
                    total = inner[p // 2, at] if total is None else total + inner[p // 2, at]
                cs.append(total * (0.5 / size))
            mean = sum(weights[s][p] * cs[s] for s in range(4))
            for s in range(4):
                dsize[s][p] = weights[s][p] * (cs[s] - mean)
        slopes = []
        for at in range(PHASES):
            e = None
            for size in range(1, 5):
                for p in block_of(size, at):
                    term = dsize[size - 1][p] * (1.0 / size)
                    e = term if e is None else e + term
            slopes.append(e)
        for c, cols in enumerate(chunks):
            toks = [tok_rows(tok, c) for tok in range(half)]
            score = acc[40:48, cols]
            for at in range(PHASES):
                out = slopes[at] * sw[:, cols]
                for tok in range(half):
                    if (tok, at) in coefs:
                        out = out + coefs[tok, at] * toks[tok]
                dconv[c, pl.ds(g * 8 * PHASES + 16 + at, 8, stride=PHASES), :] = out
                score = score + slopes[at] * conv[at, rows, cols]
            acc[40:48, cols] = score
        return 0

    lax.fori_loop(0, byte_count // (8 * PHASES), step, 0)

    def taps(t, _):
        at = pl.multiple_of(t * 8, 8)
        mask = msk[pl.ds(at, 8), :]
        same = {k: mask[:, 4 - k : 5 - k] for k in (0, 1, 3, 4)}
        for c, cols in enumerate(chunks):
            x = pad[c, pl.ds(at, 8), :]
            out = None
            for k in range(CONV):
                z = dconv[c, pl.ds(at + 8 + 2 - k, 8), :]
                if k != 2:
                    z = z * same[k]
                term = z * cw[k : k + 1, cols]
                out = term if out is None else out + term
                acc[8 * k : 8 * k + 8, cols] = acc[8 * k : 8 * k + 8, cols] + z * x
            eg[pl.ds(at, 8), cols] = out
        return 0

    lax.fori_loop(0, (byte_count + 16) // 8, taps, 0)
    small[...] = jnp.zeros_like(small)
    for k in range(7):
        small[k : k + 1, :] = jnp.sum(acc[8 * k : 8 * k + 8, :], axis=0, keepdims=True)


def gbst_backward(keep, recv, gb, dmid, gain, conv, aw, lo, emb, hi, msk, cw, sw):
    nb, d = emb.shape
    args = (keep, recv, gb, dmid, gain, conv, aw, lo, emb, hi, msk, cw, sw)
    return kernel_call(
        gbst_backward_kernel,
        (struct((nb + 16, d), f32), struct((8, d), f32)),
        ins=[whole(x.shape) for x in args],
        out_specs=(whole((nb + 16, d), False), whole((8, d), False)),
        scratch=[
            pltpu.VMEM((d // 128, nb // 2, 128), f32),
            pltpu.VMEM((d // 128, nb + 32, 128), f32),
            pltpu.VMEM((d // 128, nb + 16, 128), f32),
            pltpu.VMEM((56, d), f32),
        ],
        flops=120 * nb * d,
        moved=24 * nb * d,
        name="gbst_backward",
    )(*args)


def halo_row(who, tok_dev, ext):
    return jnp.where(who >= 2, (who - 2) * tok_dev, ext - 2 * tok_dev + who * tok_dev)


def project_kernel(me, *refs):
    own, far, w, (q, k, v, wp) = refs[:4], refs[4:8], refs[8], refs[9:13]
    tok, _ = own[0].shape
    wide = TILE
    part = w.shape[1] // 3
    wp[...] = jnp.zeros_like(wp)
    for j in range(3):
        wp[:, wide * j : wide * j + part] = w[:, part * j : part * (j + 1)]
    ext = k.shape[0]
    left = (ext - q.shape[0]) // 2
    for rel in range(4):
        who = me[0] ^ rel
        out = dot(own[rel][...], wp[...]).astype(bf16)
        q[pl.ds(pl.multiple_of(who * tok, 128), tok), :] = out[:, :wide]
        at = pl.multiple_of(left + who * tok, 128)
        k[pl.ds(at, tok), :] = out[:, wide : 2 * wide]
        v[pl.ds(at, tok), :] = out[:, 2 * wide :]
        at = pl.multiple_of(halo_row(who, tok, ext), 128)
        out = dot(far[rel][...], wp[:, wide:]).astype(bf16)
        k[pl.ds(at, tok), :] = out[:, :wide]
        v[pl.ds(at, tok), :] = out[:, wide:]


def project(me, own, far, w):
    tok, d = own[0].shape
    rows, ext = 4 * tok, 8 * tok
    args = (*own, *far, w)
    return kernel_call(
        project_kernel,
        (
            struct((rows, TILE), bf16),
            struct((ext, TILE), bf16),
            struct((ext, TILE), bf16),
            struct((d, 3 * TILE), bf16),
        ),
        prefetch=1,
        ins=[whole(x.shape) for x in args],
        out_specs=(
            whole((rows, TILE), False),
            whole((ext, TILE), False),
            whole((ext, TILE), False),
            whole((d, 3 * TILE), False),
        ),
        flops=2 * ext * d * 3 * TILE,
        moved=2 * (ext * d + 2 * ext * TILE + d * d),
        name="project",
    )(me, *args)


def project_back_kernel(is_halo, me, dq, dk, dv, wp, keep0, keep2, send1, send3):
    tok = keep0.shape[0]
    ext = dk.shape[0]
    left = (ext - dq.shape[0]) // 2
    for rel, ref in ((3, send3), (1, send1), (2, keep2), (0, keep0)):
        who = me[0] ^ rel
        if is_halo:
            at = pl.multiple_of(halo_row(who, tok, ext), 128)
            out = dot(dk[pl.ds(at, tok), :], wp[:, TILE : 2 * TILE], ((1,), (1,)))
        else:
            at = pl.multiple_of(left + who * tok, 128)
            out = dot(dk[pl.ds(at, tok), :], wp[:, TILE : 2 * TILE], ((1,), (1,)))
            mine = pl.multiple_of(who * tok, 128)
            out = out + dot(dq[pl.ds(mine, tok), :], wp[:, :TILE], ((1,), (1,)))
        out = out + dot(dv[pl.ds(at, tok), :], wp[:, 2 * TILE :], ((1,), (1,)))
        ref[...] = out.astype(ref.dtype)


def project_back(is_halo, me, dq, dk, dv, wp):
    ext, d = dk.shape[0], wp.shape[0]
    tok = ext // 8
    args = (dq, dk, dv, wp)
    kinds = (f32, f32, bf16, bf16)
    return kernel_call(
        partial(project_back_kernel, is_halo),
        tuple(struct((tok, d), kind) for kind in kinds),
        prefetch=1,
        ins=[whole(x.shape) for x in args],
        out_specs=tuple(whole((tok, d), False) for _ in kinds),
        flops=2 * ext // 2 * d * 3 * TILE,
        moved=4 * ext * d,
        name="project_back",
    )(me, *args)


def project_grad_kernel(me, *refs):
    own, far, (dqt, dkt, dvt), out = refs[:4], refs[4:8], refs[8:11], refs[11]
    tok = own[0].shape[0]
    ext = dkt.shape[1]
    left = (ext - dqt.shape[1]) // 2
    part = dqt.shape[0]
    totals = [None] * 3
    for rel in range(4):
        who = me[0] ^ rel
        mine = pl.multiple_of(who * tok, 128)
        at = pl.multiple_of(left + who * tok, 128)
        edge = pl.multiple_of(halo_row(who, tok, ext), 128)
        terms = [
            dot(dqt[:, pl.ds(mine, tok)], own[rel][...]),
            dot(dkt[:, pl.ds(at, tok)], own[rel][...]) + dot(dkt[:, pl.ds(edge, tok)], far[rel][...]),
            dot(dvt[:, pl.ds(at, tok)], own[rel][...]) + dot(dvt[:, pl.ds(edge, tok)], far[rel][...]),
        ]
        totals = [t if s is None else s + t for s, t in zip(totals, terms)]
    for j in range(3):
        out[:, part * j : part * (j + 1)] = totals[j].T.astype(bf16)


def project_grad(me, own, far, dqt, dkt, dvt):
    tok, d = own[0].shape
    args = (*own, *far, dqt, dkt, dvt)
    return kernel_call(
        project_grad_kernel,
        struct((d, 3 * dqt.shape[0]), bf16),
        prefetch=1,
        ins=[whole(x.shape) for x in args],
        out_specs=whole((d, 3 * dqt.shape[0]), False),
        flops=2 * 8 * tok * d * 3 * dqt.shape[0],
        moved=2 * 12 * tok * d,
        name="project_grad",
    )(me, *args)


def bias_kernel(diag, out):
    at = pl.program_id(0)
    heads = diag.shape[0]
    seg = diag[:, pl.ds(pl.multiple_of(at * TILE, TILE), 2 * TILE)]
    for h in range(heads):
        rows = jnp.broadcast_to(seg[h : h + 1, :], (TILE, 2 * TILE))
        turned = pltpu.roll(rows, TILE + 1, axis=1, stride=1, stride_axis=0)
        out[0, TILE * h : TILE * (h + 1), :] = turned[:, :TILE]


def bias_tiles(diag):
    heads, width = diag.shape
    count = width // TILE - 1
    return kernel_call(
        bias_kernel,
        struct((count, heads * TILE, TILE), f32),
        grid=(count,),
        ins=[whole(diag.shape)],
        out_specs=pl.BlockSpec((1, heads * TILE, TILE), lambda i: (i, 0, 0)),
        moved=4 * count * heads * TILE * TILE,
        name="bias_tiles",
    )(diag)


def table_kernel(tiles, out):
    heads = out.shape[1]
    for h in range(heads):
        part = tiles[0, TILE * h : TILE * (h + 1), :]
        cur = jnp.concatenate([part, jnp.zeros_like(part)], axis=1)
        rows = TILE
        while rows > 8:
            rows //= 2
            cur = cur[:rows] + pltpu.roll(cur[rows:], 2 * TILE - rows, axis=1)
        total = cur[0:1]
        for i in range(1, 8):
            total = total + pltpu.roll(cur[i : i + 1], 2 * TILE - i, axis=1)
        out[0, h : h + 1, :] = pltpu.roll(total, TILE - 1, axis=1)


def table_sums(tiles):
    count, rows, _ = tiles.shape
    heads = rows // TILE
    return kernel_call(
        table_kernel,
        struct((count, heads, 2 * TILE), f32),
        grid=(count,),
        ins=[pl.BlockSpec((1, rows, TILE), lambda i: (i, 0, 0))],
        out_specs=pl.BlockSpec((1, heads, 2 * TILE), lambda i: (i, 0, 0)),
        moved=4 * count * rows * TILE,
        name="table_sums",
    )(tiles)


def lane_head(shape):
    return lax.broadcasted_iota(jnp.int32, shape, 1) // HEAD_DIM


def attend_kernel(heads, info, q, k, v, cq, ck, bias, oa, ob, oloc, lse, kx, q3, sc, mx, ls, ac):
    i = pl.program_id(0)
    grid = pl.num_programs(0)
    me = info[2 * grid]
    ext = k.shape[0]

    @pl.when(i == 0)
    def _():
        kx[...] = k[...] + ck[...]

    lo, hi = info[i], info[grid + i]
    away = (ext // TILE - grid) // 2
    where = lane_head((TILE, TILE))
    for h in range(heads):
        q3[TILE * h : TILE * (h + 1), :] = jnp.where(where == h, q[...], jnp.zeros_like(q[...])) + cq[...]
    mx[...] = jnp.full_like(mx, -jnp.inf)
    ls[...] = jnp.zeros_like(ls)
    ac[...] = jnp.zeros_like(ac)

    def scores(kt, _):
        at = pl.multiple_of(kt * TILE, TILE)
        s = dot(q3[...], kx[pl.ds(at, TILE), :], ((1,), (1,))) + bias[kt - i - away + 4]
        sc[kt - lo] = s
        mx[...] = jnp.maximum(mx[...], jnp.maximum(s[:, :128], s[:, 128:]))
        return 0

    lax.fori_loop(lo, hi, scores, 0)
    top = jnp.max(mx[...], axis=1, keepdims=True)

    def gather(kt, _):
        at = pl.multiple_of(kt * TILE, TILE)
        p = jnp.exp(sc[kt - lo] - top)
        ls[...] = ls[...] + p[:, :128] + p[:, 128:]
        ac[...] = ac[...] + dot(p.astype(bf16), v[pl.ds(at, TILE), :])
        return 0

    lax.fori_loop(lo, hi, gather, 0)
    total = jnp.sum(ls[...], axis=1, keepdims=True)
    inv = 1.0 / total
    logs = top + jnp.log(total)
    out = jnp.zeros((TILE, TILE), f32)
    kept = jnp.zeros((TILE, 128), f32)
    lane = lax.broadcasted_iota(jnp.int32, (TILE, 128), 1)
    for h in range(heads):
        rows = slice(TILE * h, TILE * (h + 1))
        out = jnp.where(where == h, ac[rows, :] * inv[rows], out)
        kept = jnp.where(lane == h, logs[rows], kept)
    lse[...] = kept
    oloc[...] = out.astype(bf16)
    turned = out.T.astype(bf16)
    per = oa.shape[1]
    for j in range(TILE // 128):
        chunk = i * (TILE // 128) + j
        rel = (chunk // per) ^ me
        piece = turned[: heads * HEAD_DIM, 128 * j : 128 * (j + 1)]

        @pl.when(rel < 2)
        def _():
            oa[rel, chunk % per] = piece

        @pl.when(rel >= 2)
        def _():
            ob[rel - 2, chunk % per] = piece


def attend(info, q, k, v, cq, ck, bias, heads, tok):
    rows, ext = q.shape[0], k.shape[0]
    grid = rows // TILE
    width = heads * HEAD_DIM
    sent = (2, tok // 128, width, 128)
    tile = pl.BlockSpec((TILE, TILE), lambda i, *_: (i, 0))
    return kernel_call(
        partial(attend_kernel, heads),
        (
            struct(sent, bf16),
            struct(sent, bf16),
            struct((rows, TILE), bf16),
            struct((rows, 128), f32),
        ),
        grid=(grid,),
        prefetch=1,
        ins=[tile, whole(k.shape), whole(v.shape), tile, whole(ck.shape), whole(bias.shape)],
        out_specs=(
            whole(sent, False),
            whole(sent, False),
            tile,
            pl.BlockSpec((TILE, 128), lambda i, *_: (i, 0)),
        ),
        scratch=[
            pltpu.VMEM((ext, TILE), bf16),
            pltpu.VMEM((heads * TILE, TILE), bf16),
            pltpu.VMEM((9, heads * TILE, TILE), f32),
            pltpu.VMEM((heads * TILE, 128), f32),
            pltpu.VMEM((heads * TILE, 128), f32),
            pltpu.VMEM((heads * TILE, TILE), f32),
        ],
        flops=4 * rows * 1280 * TILE * heads,
        moved=4 * bias.size + 8 * ext * TILE,
        name="attend",
    )(info, q, k, v, cq, ck, bias)


def attend_back_kernel(
    heads, info, q, k, v, cq, ck, bias, oloc, lse, d0, d2, d13,
    dq, dk, dv, dqt, dkt, dvt, tacc,
    kx, q3, g3, gall, dqa, dka, dva, qt, gt,
):
    i = pl.program_id(0)
    grid = pl.num_programs(0)
    me = info[2 * grid]
    ext = k.shape[0]
    per = d0.shape[0]
    width = heads * HEAD_DIM

    @pl.when(i == 0)
    def _():
        kx[...] = k[...] + ck[...]
        dka[...] = jnp.zeros_like(dka)
        dva[...] = jnp.zeros_like(dva)
        tacc[...] = jnp.zeros_like(tacc)
        for rel, piece in ((0, d0[...]), (2, d2[...]), (1, d13[0]), (3, d13[1])):
            gall[pl.ds((me ^ rel) * per, per)] = piece

    lo, hi = info[i], info[grid + i]
    away = (ext // TILE - grid) // 2
    where = lane_head((TILE, TILE))
    for j in range(TILE // 128):
        gt[:width, 128 * j : 128 * (j + 1)] = gall[i * (TILE // 128) + j]
    gt[width:, :] = jnp.zeros((TILE - width, TILE), bf16)
    grad = gt[...].astype(f32).T
    qt[...] = q[...].astype(f32).T.astype(bf16)
    prod = grad * oloc[...].astype(f32)
    deltas, logs = [], []
    for h in range(heads):
        rows = slice(TILE * h, TILE * (h + 1))
        q3[rows, :] = jnp.where(where == h, q[...], jnp.zeros_like(q[...])) + cq[...]
        g3[rows, :] = jnp.where(where == h, grad, 0.0).astype(bf16)
        deltas.append(jnp.sum(jnp.where(where == h, prod, 0.0), axis=1, keepdims=True))
        logs.append(lse[:, h : h + 1])
    delta = jnp.concatenate(deltas, axis=0)
    log = jnp.concatenate(logs, axis=0)
    dqa[...] = jnp.zeros_like(dqa)

    def step(kt, _):
        at = pl.ds(pl.multiple_of(kt * TILE, TILE), TILE)
        rel = kt - i - away + 4
        s = dot(q3[...], kx[at, :], ((1,), (1,))) + bias[rel]
        p = jnp.exp(s - log)
        dp = dot(g3[...], v[at, :], ((1,), (1,)))
        ds = p * (dp - delta)
        tacc[rel] = tacc[rel] + ds
        low = ds.astype(bf16)
        plow = p.astype(bf16)
        dqa[...] = dqa[...] + dot(low, k[at, :])
        for h in range(heads):
            rows = slice(TILE * h, TILE * (h + 1))
            head = slice(HEAD_DIM * h, HEAD_DIM * (h + 1))
            dka[head, at] = dka[head, at] + dot(qt[head, :], low[rows, :])
            dva[head, at] = dva[head, at] + dot(gt[head, :], plow[rows, :])
        return 0

    lax.fori_loop(lo, hi, step, 0)
    out = jnp.zeros((TILE, TILE), f32)
    for h in range(heads):
        out = jnp.where(where == h, dqa[TILE * h : TILE * (h + 1), :], out)
    dq[...] = out.astype(bf16)
    dqt[...] = out.T[:width].astype(bf16)

    @pl.when(i == grid - 1)
    def _():
        fill = jnp.zeros((TILE - width, TILE), f32)

        def turn(t, _):
            at = pl.ds(pl.multiple_of(t * TILE, TILE), TILE)
            for acc, flat, turned in ((dka, dkt, dk), (dva, dvt, dv)):
                part = acc[:, at]
                flat[:, at] = part.astype(bf16)
                turned[at, :] = jnp.concatenate([part, fill], axis=0).T.astype(bf16)
            return 0

        lax.fori_loop(0, ext // TILE, turn, 0)


def attend_back(info, q, k, v, cq, ck, bias, oloc, lse, d0, d2, d13, heads):
    rows, ext = q.shape[0], k.shape[0]
    grid = rows // TILE
    width = heads * HEAD_DIM
    per = d0.shape[0]
    tile = pl.BlockSpec((TILE, TILE), lambda i, *_: (i, 0))
    return kernel_call(
        partial(attend_back_kernel, heads),
        (
            struct((rows, TILE), bf16),
            struct((ext, TILE), bf16),
            struct((ext, TILE), bf16),
            struct((width, rows), bf16),
            struct((width, ext), bf16),
            struct((width, ext), bf16),
            struct(bias.shape, f32),
        ),
        grid=(grid,),
        prefetch=1,
        ins=[
            tile, whole(k.shape), whole(v.shape), tile, whole(ck.shape), whole(bias.shape),
            tile, pl.BlockSpec((TILE, 128), lambda i, *_: (i, 0)),
            whole(d0.shape), whole(d2.shape), whole(d13.shape),
        ],
        out_specs=(
            tile,
            whole((ext, TILE)),
            whole((ext, TILE)),
            pl.BlockSpec((width, TILE), lambda i, *_: (0, i)),
            whole((width, ext)),
            whole((width, ext)),
            whole(bias.shape),
        ),
        scratch=[
            pltpu.VMEM((ext, TILE), bf16),
            pltpu.VMEM((heads * TILE, TILE), bf16),
            pltpu.VMEM((heads * TILE, TILE), bf16),
            pltpu.VMEM((rows // 128, width, 128), bf16),
            pltpu.VMEM((heads * TILE, TILE), f32),
            pltpu.VMEM((width, ext), f32),
            pltpu.VMEM((width, ext), f32),
            pltpu.VMEM((TILE, TILE), bf16),
            pltpu.VMEM((TILE, TILE), bf16),
        ],
        flops=10 * rows * 1280 * TILE * heads,
        moved=8 * bias.size + 16 * ext * TILE,
        name="attend_back",
    )(info, q, k, v, cq, ck, bias, oloc, lse, d0, d2, d13)


def merge_rows(packed, src, part):
    span = FORM // 4
    low = 576 + 48 * part
    return packed[pl.ds(src * span, span), low : low + 48, :].reshape(48 * span, TILE)


def merge_kernel(me, a0, a2, a13, packed, gb, gain, mid, nrm):
    per = a0.shape[0]
    for t in range(per):
        rows = slice(128 * t, 128 * (t + 1))
        total = [gb[rows, TILE * part : TILE * (part + 1)] for part in range(3)]
        for rel, piece in ((0, a0[t]), (2, a2[t]), (1, a13[0, t]), (3, a13[1, t])):
            flat = piece.astype(f32).T.astype(bf16)
            for part in range(3):
                total[part] = total[part] + dot(flat, merge_rows(packed, me[0] ^ rel, part))
        v = jnp.concatenate(total, axis=1)
        mid[rows, :] = v
        r = lax.rsqrt(jnp.mean(v * v, axis=1, keepdims=True) + EPS)
        nrm[rows, :] = (v * r * gain[...]).astype(bf16)


def merge(me, a0, a2, a13, packed, gb, gain):
    tok, d = gb.shape
    args = (a0, a2, a13, packed, gb, gain)
    return kernel_call(
        merge_kernel,
        (struct((tok, d), f32), struct((tok, d), bf16)),
        prefetch=1,
        ins=[whole(x.shape) for x in args],
        out_specs=(whole((tok, d), False), whole((tok, d), False)),
        flops=2 * tok * d * d,
        moved=10 * tok * d + packed.size * 2,
        name="merge",
    )(me, *args)


def feed_kernel(na, nb, ga, gb, packed, oa, ob, da, db, hid, dg, du, nt, gr, osum, dsum):
    j = pl.program_id(0)
    tok = na.shape[0]

    @pl.when(j == 0)
    def _():
        nt[:tok, :] = na[...]
        nt[tok:, :] = nb[...]
        gr[:tok, :] = ga[...]
        gr[tok:, :] = gb[...]
        osum[...] = jnp.zeros_like(osum)
        dsum[...] = jnp.zeros_like(dsum)

    at = pl.multiple_of(48 * j, 16)
    wg = packed[:, pl.ds(at, 48), :].reshape(FORM * 48, TILE)
    wu = packed[:, pl.ds(192 + at, 48), :].reshape(FORM * 48, TILE)
    gate = dot(nt[...], wg)
    up = dot(nt[...], wu)
    dh = None
    wds = []
    for part in range(3):
        wd = packed[pl.ds(4 * j, 4), 384 + 64 * part : 448 + 64 * part, :].reshape(TILE, TILE)
        wds.append(wd)
        term = dot(gr[:, TILE * part : TILE * (part + 1)], wd, ((1,), (1,)))
        dh = term if dh is None else dh + term
    sq = gate * gate
    th = jnp.tanh(GELU_C * gate * (1.0 + GELU_A * sq))
    half = 0.5 * (1.0 + th)
    act = gate * half
    slope = half + 0.5 * gate * (1.0 - th * th) * (GELU_C * (1.0 + 3.0 * GELU_A * sq))
    h = (act * up).astype(bf16)
    g = (dh * up * slope).astype(bf16)
    u = (dh * act).astype(bf16)
    hid[...] = h
    dg[...] = g
    du[...] = u
    for part in range(3):
        cols = slice(TILE * part, TILE * (part + 1))
        osum[:, cols] = osum[:, cols] + dot(h, wds[part])
    dsum[...] = dsum[...] + dot(g, wg, ((1,), (1,))) + dot(u, wu, ((1,), (1,)))

    @pl.when(j == pl.num_programs(0) - 1)
    def _():
        oa[...] = osum[:tok, :]
        ob[...] = osum[tok:, :].astype(bf16)
        da[...] = dsum[:tok, :]
        db[...] = dsum[tok:, :].astype(bf16)


def feed(na, nb, ga, gb, packed, units):
    tok, d = na.shape
    args = (na, nb, ga, gb, packed)
    col = pl.BlockSpec((2 * tok, TILE), lambda j: (0, j))
    full = whole((tok, d))
    return kernel_call(
        feed_kernel,
        (
            struct((tok, d), f32), struct((tok, d), bf16), struct((tok, d), f32), struct((tok, d), bf16),
            struct((2 * tok, units), bf16), struct((2 * tok, units), bf16), struct((2 * tok, units), bf16),
        ),
        grid=(units // TILE,),
        ins=[whole(x.shape) for x in args],
        out_specs=(full, full, full, full, col, col, col),
        scratch=[
            pltpu.VMEM((2 * tok, d), bf16), pltpu.VMEM((2 * tok, d), bf16),
            pltpu.VMEM((2 * tok, d), f32), pltpu.VMEM((2 * tok, d), f32),
        ],
        flops=12 * 2 * tok * d * units,
        moved=2 * packed.size + 20 * tok * d + 12 * tok * units,
        name="feed",
    )(*args)


def middle_kernel(me, mid, da, db, oa, ob, og, gain, packed, layer, dmid, dlow, ga, gb, gsum):
    tok, d = mid.shape
    gsum[...] = jnp.zeros_like(gsum)

    def norm(t, _):
        at = pl.ds(pl.multiple_of(t * 16, 16), 16)
        v = mid[at, :]
        layer[at, :] = (v + oa[at, :] + ob[at, :].astype(f32)).astype(bf16)
        e = da[at, :] + db[at, :].astype(f32)
        r = lax.rsqrt(jnp.mean(v * v, axis=1, keepdims=True) + EPS)
        ge = gain[...] * e
        m = jnp.mean(ge * v, axis=1, keepdims=True)
        out = og[at, :].astype(f32) + r * ge - v * (r * r * r * m)
        dmid[at, :] = out
        dlow[at, :] = out.astype(bf16)
        part = e * v * r
        gsum[...] = gsum[...] + part[0:8] + part[8:16]
        return 0

    lax.fori_loop(0, tok // 16, norm, 0)
    for rel in range(4):
        out = None
        for part in range(3):
            cols = slice(TILE * part, TILE * (part + 1))
            term = dot(merge_rows(packed, me[0] ^ rel, part), dlow[:, cols], ((1,), (1,)))
            out = term if out is None else out + term
        low = out.astype(bf16)
        for t in range(tok // 128):
            ref = ga if rel < 2 else gb
            ref[rel % 2, t] = low[:, 128 * t : 128 * (t + 1)]


def middle(me, mid, da, db, oa, ob, og, gain, packed):
    tok, d = mid.shape
    args = (mid, da, db, oa, ob, og, gain, packed)
    sent = (2, tok // 128, d // 4, 128)
    shapes = [((tok, d), bf16), ((tok, d), f32), ((tok, d), bf16), (sent, bf16), (sent, bf16), ((8, d), f32)]
    return kernel_call(
        middle_kernel,
        tuple(struct(*s) for s in shapes),
        prefetch=1,
        ins=[whole(x.shape) for x in args],
        out_specs=tuple(whole(s[0], False) for s in shapes),
        flops=2 * tok * d * d,
        moved=30 * tok * d + packed.size * 2,
        name="middle",
    )(me, *args)


def merge_grad_kernel(me, a0, a2, a13, dlow, keep, send):
    per = a0.shape[0]
    width = a0.shape[1]
    half = keep.shape[1]
    core = me[0] % 2
    for rel in range(4):
        pieces = [(a0[t], a2[t], a13[0, t], a13[1, t])[(0, 2, 1, 3)[rel]] for t in range(per)]
        left = jnp.concatenate(pieces, axis=1)
        rows = pl.ds(pl.multiple_of((me[0] ^ rel) * width, 64), width)
        mine = dlow[:, pl.ds(pl.multiple_of(core * half, 128), half)]
        other = dlow[:, pl.ds(pl.multiple_of((1 - core) * half, 128), half)]
        keep[rows, :] = dot(left, mine)
        send[rows, :] = dot(left, other).astype(bf16)


def merge_grad(me, a0, a2, a13, dlow):
    tok, d = dlow.shape
    args = (a0, a2, a13, dlow)
    return kernel_call(
        merge_grad_kernel,
        (struct((d, d // 2), f32), struct((d, d // 2), bf16)),
        prefetch=1,
        ins=[whole(x.shape) for x in args],
        out_specs=(whole((d, d // 2), False), whole((d, d // 2), False)),
        flops=2 * tok * d * d,
        moved=4 * tok * d + 3 * d * d,
        name="merge_grad",
    )(me, *args)


def weight_kernel(na, nb, ga, gb, hid, dg, du, keep, recv, out, nt, gr):
    j = pl.program_id(0)
    tok, d = na.shape

    @pl.when(j == 0)
    def _():
        nt[:, :tok] = na[...].astype(f32).T.astype(bf16)
        nt[:, tok:] = nb[...].astype(f32).T.astype(bf16)
        gr[:tok, :] = ga[...]
        gr[tok:, :] = gb[...]
        total = (keep[...] + recv[...].astype(f32)).astype(bf16)
        for part in range(total.shape[1] // 128):
            low = 1152 + 48 * part
            out[:, low : low + 48, :] = total[:, 128 * part : 128 * (part + 1)].reshape(FORM, 48, 128)

    for base, ref in ((0, dg), (384, du)):
        grad = dot(nt[...], ref[...]).astype(bf16)
        for part in range(TILE // 128):
            at = pl.multiple_of(base + 48 * ((TILE // 128) * j + part), 16)
            out[:, pl.ds(at, 48), :] = grad[:, 128 * part : 128 * (part + 1)].reshape(FORM, 48, 128)
    turned = hid[...].astype(f32).T.astype(bf16)
    grad = dot(turned, gr[...]).astype(bf16)
    for part in range(d // 128):
        low = 768 + 64 * part
        out[pl.ds(4 * j, 4), low : low + 64, :] = grad[:, 128 * part : 128 * (part + 1)].reshape(4, 64, 128)


def weight_grads(na, nb, ga, gb, hid, dg, du, keep, recv):
    tok, d = na.shape
    units = hid.shape[1]
    args = (na, nb, ga, gb, hid, dg, du, keep, recv)
    col = pl.BlockSpec((2 * tok, TILE), lambda j: (0, j))
    shape = (FORM, 1296, 128)
    return kernel_call(
        weight_kernel,
        struct(shape, bf16),
        grid=(units // TILE,),
        ins=[whole(x.shape) for x in args[:4]] + [col, col, col] + [whole(keep.shape), whole(recv.shape)],
        out_specs=whole(shape),
        scratch=[pltpu.VMEM((d, 2 * tok), bf16), pltpu.VMEM((2 * tok, d), bf16)],
        flops=6 * 2 * tok * d * units,
        moved=12 * tok * units + 16 * tok * d,
        name="weight_grads",
    )(*args)


def regroup(stacked, parts, groups):
    count, _, width = stacked.shape
    if count == groups:
        return stacked
    pieces, low = [], 0
    for blocks, rows in parts:
        piece = stacked[:, low : low + blocks * rows].reshape(count, blocks, rows, width)
        low += blocks * rows
        piece = jnp.transpose(piece, (1, 0, 2, 3)).reshape(blocks, groups, count * rows // groups, width)
        pieces.append(jnp.transpose(piece, (1, 0, 2, 3)).reshape(groups, blocks * count * rows // groups, width))
    return jnp.concatenate(pieces, axis=1)


def to_blocks(mat, width):
    rows, cols = mat.shape
    return jnp.transpose(mat.reshape(rows, cols // width, width), (1, 0, 2)).reshape(-1, width)


def from_blocks(stacked, rows):
    blocks, width = stacked.shape[0] // rows, stacked.shape[1]
    return jnp.transpose(stacked.reshape(blocks, rows, width), (1, 0, 2)).reshape(rows, blocks * width)


def flip(x, bit):
    return lax.ppermute(x, ULY, [(i, i ^ bit) for i in range(4)])


def ordered(core, mine, theirs, axis):
    first = jnp.where(core == 0, mine, theirs)
    second = jnp.where(core == 0, theirs, mine)
    return jnp.concatenate([first, second], axis=axis)


def local(
    n_ctx,
    byte_embed,
    query_weight,
    key_weight,
    value_weight,
    merge_weight,
    gate_weight,
    up_weight,
    down_weight,
    conv_weight,
    score_weight,
    attn_gain,
    ffn_gain,
    bias_table,
    doc_lengths,
    rel_bucket,
    out_grad,
):
    nb, d = byte_embed.shape
    tok = out_grad.shape[0]
    n_dev = n_ctx * 4
    groups = n_ctx * 2
    rows_dev = query_weight.shape[0]
    down_dev = down_weight.shape[0]
    heads = HEADS // 4
    width = heads * HEAD_DIM
    group_len = tok * 4
    ext = 2 * group_len
    ff = gate_weight.shape[1]
    ctx_at = lax.axis_index("ctx")
    core = lax.axis_index("uc")
    uly_at = lax.axis_index(ULY)
    dev_at = lax.axis_index(RING)
    me = uly_at.astype(jnp.int32).reshape(1)

    up_pairs = [(i, i + 1) for i in range(n_dev - 1)]
    down_pairs = [(i + 1, i) for i in range(n_dev - 1)]
    lo = lax.ppermute(byte_embed[nb - 8 :], RING, up_pairs)
    hi = lax.ppermute(byte_embed[:8], RING, down_pairs)

    qkv_own = jnp.stack(
        [w.reshape(rows_dev, 4, width) for w in (query_weight, key_weight, value_weight)], axis=2
    ).reshape(rows_dev, 4, 3 * width)
    qkv_send = jnp.broadcast_to(
        jnp.transpose(qkv_own, (1, 0, 2))[None], (n_ctx, 4, rows_dev, 3 * width)
    ).reshape(n_dev, rows_dev, 3 * width)
    qkv_w = lax.all_to_all(qkv_send, RING, 0, 0, tiled=True).reshape(d, 3 * width)

    unit = ff // n_dev
    split = lambda w, at: lax.dynamic_index_in_dim(
        w.reshape(rows_dev, groups, 2, unit), at, 2, keepdims=False
    ).reshape(rows_dev, ff // 2)
    mine = jnp.concatenate([split(gate_weight, core), split(up_weight, core), merge_weight], axis=1)
    other = jnp.concatenate([split(gate_weight, 1 - core), split(up_weight, 1 - core), merge_weight], axis=1)
    theirs = flip(other, 1)
    both = ordered(core, mine, theirs, 0)
    packed_own = jnp.concatenate(
        [
            to_blocks(both[:, : ff // 2], TILE),
            to_blocks(both[:, ff // 2 : ff], TILE),
            to_blocks(down_weight, TILE),
            to_blocks(both[:, ff:], TILE),
        ],
        axis=0,
    )
    packed = lax.all_gather(packed_own, ("ctx", "ux"), axis=0, tiled=False)
    packed = packed.reshape(groups, packed_own.shape[0], TILE)
    packed = regroup(
        packed,
        ((4, 2 * rows_dev), (4, 2 * rows_dev), (3, down_dev), (3, 2 * rows_dev)),
        FORM,
    )
    grad_other = flip(out_grad, 1)

    count = doc_lengths.shape[0]
    order = lax.broadcasted_iota(jnp.int32, (count, count), 0)
    before = lax.broadcasted_iota(jnp.int32, (count, count), 1)
    starts = jnp.sum(jnp.where(before < order, doc_lengths[None, :], 0), axis=1)
    limit = jnp.sum(doc_lengths)

    def doc_of(places):
        found = jnp.sum((starts[None, :] <= places[:, None]).astype(jnp.int32), axis=1) - 1
        return jnp.where((places >= 0) & (places < limit), found, -1)

    byte_doc = doc_of(dev_at * nb - 16 + jnp.arange(nb + 32, dtype=jnp.int32))
    center = byte_doc[8 : nb + 24]
    msk = jnp.stack(
        [(byte_doc[8 + k - 2 : 8 + k - 2 + nb + 16] == center).astype(f32) for k in range(CONV)]
        + [jnp.zeros((nb + 16,), f32)] * (128 - CONV),
        axis=1,
    )
    tok_doc = doc_of(2 * (ctx_at * group_len - group_len // 2 + jnp.arange(ext, dtype=jnp.int32)))
    bits = count.bit_length()
    lane = jnp.arange(TILE, dtype=jnp.int32) - width
    bit_on = ((tok_doc[:, None] >> jnp.clip(lane // 2, 0, 31)[None, :]) & 1) == 1
    used = ((lane >= 0) & (lane < 2 * bits))[None, :]
    odd = (lane % 2 == 1)[None, :]
    code_k = jnp.where(used & (bit_on == odd), 1.0, 0.0).astype(bf16)
    code_q = jnp.where(used & (bit_on != odd), -BIG, 0.0).astype(bf16)[group_len // 2 : group_len // 2 + group_len]
    tiles = group_len // TILE
    first = ctx_at * group_len + TILE * jnp.arange(tiles, dtype=jnp.int32)
    begin = jnp.max(jnp.where(starts[None, :] <= 2 * first[:, None], starts[None, :], 0), axis=1)
    last = 2 * (first + TILE - 1)
    end = jnp.min(jnp.where(starts[None, :] > last[:, None], starts[None, :], limit), axis=1)
    shift = group_len // 2 - ctx_at * group_len
    tile_lo = jnp.clip(((begin + 1) // 2 + shift) // TILE, 0, ext // TILE)
    tile_hi = jnp.clip(((end - 1) // 2 + shift) // TILE + 1, 0, ext // TILE)
    info = jnp.concatenate([tile_lo, tile_hi, me]).astype(jnp.int32)

    rel_count = rel_bucket.shape[0]
    diag_len = 2 * DOC_TOK + 2 * TILE
    bucket = jnp.pad(rel_bucket, (TILE, diag_len - TILE - rel_count), constant_values=-1)
    onehot = (bucket[None, :] == jnp.arange(NBUCK, dtype=jnp.int32)[:, None]).astype(f32)
    table_here = lax.dynamic_slice_in_dim(bias_table, uly_at * heads, heads, 1)
    diag = lax.dot_general(table_here, onehot, (((0,), (0,)), ((), ())), precision=highest)
    bias = bias_tiles(diag)

    cw, sw = conv_weight, score_weight[None, :]
    gain_one, gain_two = attn_gain[None, :], ffn_gain[None, :]
    gbst, normed, conv, aw = gbst_forward(lo, byte_embed, hi, msk, cw, sw, gain_one)

    near = [(4 * c + u, 4 * (c + s) + u) for c in range(n_ctx) for u, s in ((0, -1), (1, -1), (2, 1), (3, 1)) if 0 <= c + s < n_ctx]
    far0 = lax.ppermute(normed, RING, near)
    own2 = flip(normed, 2)
    own1 = flip(normed, 1)
    own3 = flip(own2, 1)
    far2 = flip(far0, 2)
    far1 = flip(far0, 1)
    far3 = flip(far2, 1)
    own = (normed, own1, own2, own3)
    far = (far0, far1, far2, far3)
    q, k, v, wp = project(me, own, far, qkv_w)

    oa, ob, oloc, lse = attend(info, q, k, v, code_q, code_k, bias, heads, tok)
    got2 = flip(ob, 2)
    got1 = flip(jnp.stack([oa[1], got2[1]]), 1)
    att = (oa[0], got2[0], got1)
    mid, normed_two = merge(me, *att, packed, gbst, gain_two)

    normed_other = flip(normed_two, 1)
    out_a, out_b, dn_a, dn_b, hid, dgate, dup = feed(
        normed_two, normed_other, out_grad, grad_other, packed, ff // 2
    )
    dn_got = flip(dn_b, 1)
    out_got = flip(out_b, 1)
    layer_out, dmid, dlow, ga, gb2, ffn_sum = middle(
        me, mid, dn_a, dn_got, out_a, out_got, out_grad, gain_two, packed
    )
    back2 = flip(gb2, 2)
    keep_m, send_m = merge_grad(me, *att, dlow)
    recv_m = flip(send_m, 1)
    back1 = flip(jnp.stack([ga[1], back2[1]]), 1)
    grads = weight_grads(normed_two, normed_other, out_grad, grad_other, hid, dgate, dup, keep_m, recv_m)
    parts16 = ((8, 48), (8, 48), (6, 64), (3, 48))
    grads = regroup(grads, parts16, groups)
    summed = lax.psum_scatter(grads, ("ctx", "ux"), scatter_dimension=0, tiled=False)

    dq, dk, dv, dqt, dkt, dvt, tacc = attend_back(
        info, q, k, v, code_q, code_k, bias, oloc, lse, ga[0], back2[0], back1, heads
    )
    hk0, hk2, hs1, hs3 = project_back(True, me, dq, dk, dv, wp)
    h_got3 = flip(hs3, 1)
    h_mid = (hk2 + h_got3.astype(f32)).astype(bf16)
    h_got2 = flip(h_mid, 2)
    h_got1 = flip(hs1, 1)
    ok0, ok2, os1, os3 = project_back(False, me, dq, dk, dv, wp)
    o_got3 = flip(os3, 1)
    o_mid = (ok2 + o_got3.astype(f32)).astype(bf16)
    o_got2 = flip(o_mid, 2)
    o_got1 = flip(os1, 1)
    h_sum = (hk0 + h_got1.astype(f32) + h_got2.astype(f32)).astype(bf16)
    h_back = lax.ppermute(h_sum, RING, [(b, a) for a, b in near])
    o_sum = ok0 + o_got1.astype(f32) + o_got2.astype(f32)

    qkv_grad = project_grad(me, own, far, dqt, dkt, dvt)
    qkv_got = lax.all_to_all(qkv_grad.reshape(n_dev, rows_dev, 3 * width), RING, 0, 0, tiled=True)
    qkv_sum = jnp.sum(qkv_got.reshape(n_ctx, 4, rows_dev, 3, width).astype(f32), axis=0)
    qkv_sum = jnp.transpose(qkv_sum, (2, 1, 0, 3))
    query_grad, key_grad, value_grad = (
        qkv_sum[j].reshape(rows_dev, d) for j in range(3)
    )

    diag_parts = jnp.transpose(table_sums(tacc), (1, 0, 2))
    count_t = diag_parts.shape[1]
    low = diag_parts[:, :, :TILE].reshape(heads, count_t * TILE)
    high = diag_parts[:, :, TILE:].reshape(heads, count_t * TILE)
    diag_grad = jnp.pad(low, ((0, 0), (0, TILE))) + jnp.pad(high, ((0, 0), (TILE, 0)))
    table_local = lax.dot_general(onehot, diag_grad, (((1,), (1,)), ((), ())), precision=highest)
    table_grad = lax.dynamic_update_slice(jnp.zeros((NBUCK, HEADS), f32), table_local, (0, uly_at * heads))

    eg, small = gbst_backward(
        o_sum, h_back, gbst, dmid, gain_one, conv, aw, lo, byte_embed, hi, msk, cw, sw
    )
    from_prev = lax.ppermute(eg[nb + 8 :], RING, up_pairs)
    from_next = lax.ppermute(eg[:8], RING, down_pairs)
    main = eg[8 : nb + 8]
    embed_grad = jnp.concatenate(
        [main[:8] + from_prev, main[8 : nb - 8], main[nb - 8 :] + from_next], axis=0
    )

    rest = jnp.concatenate(
        [jnp.sum(ffn_sum, axis=0, keepdims=True), jnp.pad(table_grad.reshape(1, -1), ((0, 0), (0, d - NBUCK * HEADS)))],
        axis=0,
    )
    total = jnp.concatenate([small, jnp.pad(rest, ((0, 6), (0, 0)))], axis=0)
    for bit in (1, 2):
        total = total + flip(total, bit)
    bit = 1
    while bit < n_ctx:
        total = total + lax.ppermute(total, "ctx", [(i, i ^ bit) for i in range(n_ctx)])
        bit *= 2

    rows2 = 2 * rows_dev
    gate_b = from_blocks(summed[: 8 * rows2], rows2)
    up_b = from_blocks(summed[8 * rows2 : 16 * rows2], rows2)
    down_grad = from_blocks(summed[16 * rows2 : 16 * rows2 + 6 * down_dev], down_dev).astype(f32)
    merge_b = from_blocks(summed[16 * rows2 + 6 * down_dev :], rows2)
    three = jnp.concatenate([gate_b, up_b, merge_b], axis=1).reshape(2, rows_dev, -1)
    kept = lax.dynamic_index_in_dim(three, core, 0, keepdims=False)
    given = flip(lax.dynamic_index_in_dim(three, 1 - core, 0, keepdims=False), 1)
    even = jnp.where(core == 0, kept, given).astype(f32)
    odd_part = jnp.where(core == 0, given, kept).astype(f32)

    def units(low_col, cols):
        return jnp.stack(
            [x[:, low_col : low_col + cols].reshape(rows_dev, groups, unit) for x in (even, odd_part)], axis=2
        ).reshape(rows_dev, 2 * cols)

    gate_grad = units(0, ff // 2)
    up_grad = units(ff // 2, ff // 2)
    merge_g = jnp.concatenate([even[:, ff:], odd_part[:, ff:]], axis=1)
    return (
        layer_out,
        embed_grad,
        query_grad,
        key_grad,
        value_grad,
        merge_g,
        gate_grad,
        up_grad,
        down_grad,
        total[:CONV],
        total[5],
        total[6],
        total[8],
        total[9, : NBUCK * HEADS].reshape(NBUCK, HEADS),
    )


def solution(mesh):
    n_ctx = mesh.shape["ctx"]
    inner = Mesh(mesh.devices.reshape(n_ctx, 2, 2), RING)
    row = P(RING, None)
    return jax.shard_map(
        partial(local, n_ctx),
        mesh=inner,
        in_specs=(row,) * 8 + (P(),) * 7 + (row,),
        out_specs=(row,) * 9 + (P(),) * 5,
        check_vma=False,
    )
```

profile of v0, /device:TPU:1, one launch (start us, length us, event | category | flops | bytes accessed | tf_op | source)
XLA Modules:
  0.0 423.4 jit_solution(611376625285612053)
XLA Ops:
  24.3 6.8 %all-to-all-start = ((bf16[32,24,576]{2,1,0:T(8,128)(2,1)}), bf16[32,24,576]{2,1,0:T(8,128)(2,1)}, u32[]{:S(2)}, u32[]{:S(2)}) async-start(bf16[32,24,576]{2,1,0:T(8,128)(2,1)} %bitcast.2), calls=%async_computation | async-start | bytes 1966080 | tf_op jit(solution)/shard_map/all_to_all | solution.py:1047
  40.3 4.6 %stack.71.msk = f32[784,128]{1,0:T(8,128)} concatenate(f32[784,1]{1,0:T(8,128)S(1)} %reshape.249, f32[784,1]{1,0:T(8,128)S(1)} %reshape.250, f32[784,1]{1,0:T(8,128)S(1)} %eq.57, f32[784,1]{1,0:T(8,128)S(1)} %reshape.251, f32[784,1]{1,0:T(8,128)S(1)} %reshape.252, f32[784,1]{1,0:T(8,128)} %stack_broadcast_in_dim.3, f32[784,2]{1,0:T(8,128)} %stack.66, f32[784,8]{1,0:T(8,128)} %stack.67, ...), dimensions={1} | concatenate | bytes 802816 | tf_op jit(solution)/shard_map/stack | solution.py:1087
  46.1 10.1 %gbst_forward.1 = (f32[384,768]{1,0:T(8,128)}, bf16[384,768]{1,0:T(8,128)(2,1)}, f32[12,64,768]{2,1,0:T(8,128)}, f32[64,128]{1,0:T(8,128)}) custom-call(bf16[8,768]{1,0:T(8,128)(2,1)} %copy-done.19, bf16[768,768]{1,0:T(8,128)(2,1)} %emb.3, bf16[8,768]{1,0:T(8,128)(2,1)} %copy-done.18, f32[784,128]{1,0:T(8,128)} %stack.71.msk, f32[5,768]{1,0:T(8,128)} %cw.3, ...), custom_call_target="tpu_custom_call" | custom-call | flops 35389440 | bytes 11796480 | tf_op jit(solution)/shard_map/gbst_forward/pallas_call | solution.py:175
  58.6 6.6 %bias_tiles.1.bias = f32[9,768,256]{2,1,0:T(8,128)} custom-call(f32[3,2560]{1,0:T(4,128)} %fusion.2.diag), custom_call_target="tpu_custom_call" | custom-call | bytes 7077888 | tf_op jit(solution)/shard_map/bias_tiles/pallas_call | solution.py:456
  77.1 5.5 %collective-permute-done.3.refs_2_ = bf16[384,768]{1,0:T(8,128)(2,1)S(1)} collective-permute-done((bf16[384,768]{1,0:T(8,128)(2,1)S(1)}, bf16[384,768]{1,0:T(8,128)(2,1)S(1)}, u32[]{:S(2)}, u32[]{:S(2)}) %collective-permute-start.3) | collective-permute-done | bytes 589856 | tf_op jit(solution)/shard_map/ppermute | solution.py:991
  84.5 19.6 %collective-permute-done.7.refs_6_ = bf16[384,768]{1,0:T(8,128)(2,1)S(1)} collective-permute-done((bf16[384,768]{1,0:T(8,128)(2,1)S(1)}, bf16[384,768]{1,0:T(8,128)(2,1)S(1)}, u32[]{:S(2)}, u32[]{:S(2)}) %collective-permute-start.7) | collective-permute-done | bytes 589856 | tf_op jit(solution)/shard_map/ppermute | solution.py:991
  110.7 8.4 %project.1 = (bf16[1536,256]{1,0:T(8,128)(2,1)}, bf16[3072,256]{1,0:T(8,128)(2,1)}, bf16[3072,256]{1,0:T(8,128)(2,1)}, bf16[768,768]{1,0:T(8,128)(2,1)}) custom-call(s32[1]{0:T(128)} %bitcast.me, bf16[384,768]{1,0:T(8,128)(2,1)} %get-tuple-element.60.refs_0_, bf16[384,768]{1,0:T(8,128)(2,1)} %copy-done.34, bf16[384,768]{1,0:T(8,128)(2,1)} %copy-done.32, ...), custom_call_target="tpu_custom_call" | custom-call | flops 3623878656 | bytes 9043968 | tf_op jit(solution)/shard_map/project/pallas_call | solution.py:349
  119.0 25.5 %attend.1 = (bf16[2,3,192,128]{3,2,1,0:T(8,128)(2,1)}, bf16[2,3,192,128]{3,2,1,0:T(8,128)(2,1)}, bf16[1536,256]{1,0:T(8,128)(2,1)}, f32[1536,128]{1,0:T(8,128)}) custom-call(s32[13]{0:T(128)} %pad_add_fusion.info, bf16[1536,256]{1,0:T(8,128)(2,1)} %get-tuple-element.61.q, bf16[3072,256]{1,0:T(8,128)(2,1)} %get-tuple-element.62.k, ...), custom_call_target="tpu_custom_call" | custom-call | flops 6039797760 | bytes 13369344 | tf_op jit(solution)/shard_map/attend/pallas_call | solution.py:571
  148.5 5.8 %collective-permute-done.9 = bf16[2,3,192,128]{3,2,1,0:T(8,128)(2,1)S(1)} collective-permute-done((bf16[2,3,192,128]{3,2,1,0:T(8,128)(2,1)}, bf16[2,3,192,128]{3,2,1,0:T(8,128)(2,1)S(1)}, u32[]{:S(2)}, u32[]{:S(2)}) %collective-permute-start.9) | collective-permute-done | bytes 294944 | tf_op jit(solution)/shard_map/ppermute | solution.py:991
  157.8 5.3 %merge.1 = (f32[384,768]{1,0:T(8,128)}, bf16[384,768]{1,0:T(8,128)(2,1)}) custom-call(s32[1]{0:T(128)} %bitcast.me, bf16[3,192,128]{2,1,0:T(8,128)(2,1)} %get-tuple-element.216.a0, bf16[3,192,128]{2,1,0:T(8,128)(2,1)} %get-tuple-element.218.a2, bf16[2,3,192,128]{3,2,1,0:T(8,128)(2,1)} %copy-done.14, bf16[16,720,256]{2,1,0:T(8,128)(2,1)} %bitcast.60, ...), custom_call_target="tpu_custom_call" | custom-call | flops 452984832 | bytes 8847360 | tf_op jit(solution)/shard_map/merge/pallas_call | solution.py:757
  166.1 15.4 %feed.1 = (f32[384,768]{1,0:T(8,128)}, bf16[384,768]{1,0:T(8,128)(2,1)}, f32[384,768]{1,0:T(8,128)}, bf16[384,768]{1,0:T(8,128)(2,1)}, bf16[768,1024]{1,0:T(8,12...) custom-call(bf16[384,768]{1,0:T(8,128)(2,1)} %get-tuple-element.68.na, bf16[384,768]{1,0:T(8,128)(2,1)} %copy-done.8, ...), custom_call_target="tpu_custom_call" | custom-call | flops 7247757312 | bytes 16515072 | tf_op jit(solution)/shard_map/feed/pallas_call | solution.py:823
  185.4 8.7 %middle.1 = (bf16[384,768]{1,0:T(8,128)(2,1)}, f32[384,768]{1,0:T(8,128)}, bf16[384,768]{1,0:T(8,128)(2,1)}, bf16[2,3,192,128]{3,2,1,0:T(8,128)(2,1)}, bf16[2,3,...) custom-call(s32[1]{0:T(128)} %bitcast.me, f32[384,768]{1,0:T(8,128)} %get-tuple-element.67.mid, ...), custom_call_target="tpu_custom_call" | custom-call | flops 452984832 | bytes 14745600 | tf_op jit(solution)/shard_map/middle/pallas_call | solution.py:879
  200.6 10.4 %weight_grads.1 = bf16[16,1296,128]{2,1,0:T(8,128)(2,1)} custom-call(bf16[384,768]{1,0:T(8,128)(2,1)} %get-tuple-element.68.na, bf16[384,768]{1,0:T(8,128)(2,1)} %copy-done.8, bf16[384,768]{1,0:T(8,128)(2,1)} %ga.3, bf16[384,768]{1,0:T(8,128)(2,1)} %copy-done.7, bf16[768,1024]{1,0:T(8,128)(2,1)} %get-tuple-element.97.hid, ...), custom_call_target="tpu_custom_call" | custom-call | flops 3623878656 | bytes 9437184 | tf_op jit(solution)/shard_map/weight_grads/pallas_call | solution.py:954
  214.1 6.1 %collective-permute-done.16 = bf16[2,3,192,128]{3,2,1,0:T(8,128)(2,1)S(1)} collective-permute-done((bf16[2,3,192,128]{3,2,1,0:T(8,128)(2,1)S(1)}, bf16[2,3,192,128]{3,2,1,0:T(8,128)(2,1)S(1)}, u32[]{:S(2)}, u32[]{:S(2)}) %collective-permute-start.16) | collective-permute-done | bytes 294944 | tf_op jit(solution)/shard_map/ppermute | solution.py:991
  224.1 35.2 %attend_back.1 = (bf16[1536,256]{1,0:T(8,128)(2,1)}, bf16[3072,256]{1,0:T(8,128)(2,1)}, bf16[3072,256]{1,0:T(8,128)(2,1)}, bf16[192,1536]{1,0:T(8,128)(2,1)}, bf...) custom-call(s32[13]{0:T(128)} %pad_add_fusion.info, ...), custom_call_target="tpu_custom_call" | custom-call | flops 15099494400 | bytes 26738688 | tf_op jit(solution)/shard_map/attend_back/pallas_call | solution.py:689
  259.3 5.4 %project_back.3 = (f32[384,768]{1,0:T(8,128)}, f32[384,768]{1,0:T(8,128)}, bf16[384,768]{1,0:T(8,128)(2,1)}, bf16[384,768]{1,0:T(8,128)(2,1)}) custom-call(s32[1]{0:T(128)} %bitcast.me, bf16[1536,256]{1,0:T(8,128)(2,1)} %get-tuple-element.78.dq, bf16[3072,256]{1,0:T(8,128)(2,1)} %get-tuple-element.79.dk, bf16[3072,256]{1,0:T(8,128)(2,1)} %get-tuple-element.80.dv, ...), custom_call_target="tpu_custom_call" | custom-call | flops 1811939328 | bytes 9437184 | tf_op jit(solution)/shard_map/project_back/pallas_call | solution.py:394
  265.0 7.7 %project_grad.1 = bf16[768,576]{1,0:T(8,128)(2,1)} custom-call(s32[1]{0:T(128)} %bitcast.me, bf16[384,768]{1,0:T(8,128)(2,1)} %get-tuple-element.60.refs_0_, bf16[384,768]{1,0:T(8,128)(2,1)} %copy-done.34, bf16[384,768]{1,0:T(8,128)(2,1)} %copy-done.32, bf16[384,768]{1,0:T(8,128)(2,1)} %collective-permute-done.4.refs_3_, bf16[384,768]{1,0:T(8,128)(2,1)} %copy-done.31, ...), custom_call_target="tpu_custom_call" | custom-call | flops 2717908992 | bytes 7077888 | tf_op jit(solution)/shard_map/project_grad/pallas_call | solution.py:431
  272.8 22.7 %all-to-all-start.1 = ((bf16[32,24,576]{2,1,0:T(8,128)(2,1)}), bf16[32,24,576]{2,1,0:T(8,128)(2,1)}, u32[]{:S(2)}, u32[]{:S(2)}) async-start(bf16[32,24,576]{2,1,0:T(8,128)(2,1)} %bitcast.65), calls=%async_computation.1 | async-start | bytes 1966080 | tf_op jit(solution)/shard_map/all_to_all | solution.py:1176
  295.4 6.2 %project_back.2 = (f32[384,768]{1,0:T(8,128)}, f32[384,768]{1,0:T(8,128)}, bf16[384,768]{1,0:T(8,128)(2,1)}, bf16[384,768]{1,0:T(8,128)(2,1)}) custom-call(s32[1]{0:T(128)} %bitcast.me, bf16[1536,256]{1,0:T(8,128)(2,1)} %get-tuple-element.78.dq, bf16[3072,256]{1,0:T(8,128)(2,1)} %get-tuple-element.79.dk, bf16[3072,256]{1,0:T(8,128)(2,1)} %get-tuple-element.80.dv, ...), custom_call_target="tpu_custom_call" | custom-call | flops 1811939328 | bytes 9437184 | tf_op jit(solution)/shard_map/project_back/pallas_call | solution.py:394
  304.5 9.4 %table_sums.1 = f32[9,3,512]{2,1,0:T(4,128)} custom-call(f32[9,768,256]{2,1,0:T(8,128)} %get-tuple-element.105.tiles), custom_call_target="tpu_custom_call" | custom-call | bytes 7077888 | tf_op jit(solution)/shard_map/table_sums/pallas_call | solution.py:485
  315.7 8.7 %collective-permute-done.23 = bf16[384,768]{1,0:T(8,128)(2,1)S(1)} collective-permute-done((bf16[384,768]{1,0:T(8,128)(2,1)}, bf16[384,768]{1,0:T(8,128)(2,1)S(1)}, u32[]{:S(2)}, u32[]{:S(2)}) %collective-permute-start.23) | collective-permute-done | bytes 589856 | tf_op jit(solution)/shard_map/ppermute | solution.py:991
  334.6 6.1 %collective-permute-done.20 = bf16[384,768]{1,0:T(8,128)(2,1)S(1)} collective-permute-done((bf16[384,768]{1,0:T(8,128)(2,1)S(1)}, bf16[384,768]{1,0:T(8,128)(2,1)S(1)}, u32[]{:S(2)}, u32[]{:S(2)}) %collective-permute-start.20) | collective-permute-done | bytes 589856 | tf_op jit(solution)/shard_map/ppermute | solution.py:991
  341.8 11.4 %collective-permute-done.24.recv = bf16[384,768]{1,0:T(8,128)(2,1)S(1)} collective-permute-done((bf16[384,768]{1,0:T(8,128)(2,1)}, bf16[384,768]{1,0:T(8,128)(2,1)S(1)}, u32[]{:S(2)}, u32[]{:S(2)}) %collective-permute-start.24) | collective-permute-done | bytes 589856 | tf_op jit(solution)/shard_map/ppermute | solution.py:1172
  354.1 21.0 %gbst_backward.1 = (f32[784,768]{1,0:T(8,128)}, f32[8,768]{1,0:T(8,128)}) custom-call(f32[384,768]{1,0:T(8,128)} %convert_add_fusion.keep, bf16[384,768]{1,0:T(8,128)(2,1)} %copy-done.9, f32[384,768]{1,0:T(8,128)} %get-tuple-element.66.gb, f32[384,768]{1,0:T(8,128)} %get-tuple-element.90.dmid, f32[1,768]{1,0:T(1,128)} %broadcast_in_dim.91.gain, ...), custom_call_target="tpu_custom_call" | custom-call | flops 70778880 | bytes 14155776 | tf_op jit(solution)/shard_map/gbst_backward/pallas_call | solution.py:301
  (287 shorter events, 135.2 us)
Async XLA Ops:
  7.2 149.8 %all-gather.3.cloned.1.call-start = ((), (), s32[]{:S(2)}) async-start(), calls=%async_computation.4 | async-start | bytes 6266880 | tf_op jit(solution)/shard_map/all_gather | solution.py:1066
  15.6 29.3 %collective-permute-start.1 = (bf16[8,768]{1,0:T(8,128)(2,1)S(1)}, bf16[8,768]{1,0:T(8,128)(2,1)S(1)}, u32[]{:S(2)}, u32[]{:S(2)}) collective-permute-start(bf16[8,768]{1,0:T(8,128)(2,1)S(1)} %get-tuple-element.201), channel_id=1, source_target_pairs={{1,0},{2,1},{3,2},{4,3},{5,4},{6,5},{7,6},{8,7},{9,8},{10,9},{11,1... | collective-permute-start | bytes 36872 | tf_op jit(solution)/shard_map/ppermute | solution.py:1039
  17.7 27.3 %collective-permute-start = (bf16[8,768]{1,0:T(8,128)(2,1)S(1)}, bf16[8,768]{1,0:T(8,128)(2,1)S(1)}, u32[]{:S(2)}, u32[]{:S(2)}) collective-permute-start(bf16[8,768]{1,0:T(8,128)(2,1)S(1)} %get-tuple-element.202), channel_id=1, source_target_pairs={{0,1},{1,2},{2,3},{3,4},{4,5},{5,6},{6,7},{7,8},{8,9},{9,10},{10,1... | collective-permute-start | bytes 36872 | tf_op jit(solution)/shard_map/ppermute | solution.py:1038
  24.3 86.1 %all-to-all-start = ((bf16[32,24,576]{2,1,0:T(8,128)(2,1)}), bf16[32,24,576]{2,1,0:T(8,128)(2,1)}, u32[]{:S(2)}, u32[]{:S(2)}) async-start(bf16[32,24,576]{2,1,0:T(8,128)(2,1)} %bitcast.2), calls=%async_computation | async-start | bytes 1966080 | tf_op jit(solution)/shard_map/all_to_all | solution.py:1047
  31.1 373.2 %reduce-scatter.2.cloned.1.call-start = ((), (), s32[]{:S(2)}) async-start(), calls=%async_computation.3 | async-start | bytes 5640192 | tf_op jit(solution)/shard_map/reduce_scatter | solution.py:1156
  56.3 17.1 %collective-permute-start.5 = (bf16[384,768]{1,0:T(8,128)(2,1)}, bf16[384,768]{1,0:T(8,128)(2,1)S(1)}, u32[]{:S(2)}, u32[]{:S(2)}) collective-permute-start(bf16[384,768]{1,0:T(8,128)(2,1)} %get-tuple-element.60.refs_0_), channel_id=1, source_target_pairs={{2,6},{3,7},{4,0},{5,1},{6,10},{7,11},{8,4},{9,5},{10,14},{11,15},... | collective-permute-start | bytes 1769480 | tf_op jit(solution)/shard_map/ppermute | solution.py:1123
  66.2 16.4 %collective-permute-start.3 = (bf16[384,768]{1,0:T(8,128)(2,1)S(1)}, bf16[384,768]{1,0:T(8,128)(2,1)S(1)}, u32[]{:S(2)}, u32[]{:S(2)}) collective-permute-start(bf16[384,768]{1,0:T(8,128)(2,1)S(1)} %copy-done.30), channel_id=1, source_target_pairs={{0,2},{1,3},{2,0},{3,1},{4,6},{5,7},{6,4},{7,5},{8,10},{9,11},{10,... | collective-permute-start | bytes 1769480 | tf_op jit(solution)/shard_map/ppermute | solution.py:991
  73.4 30.7 %collective-permute-start.7 = (bf16[384,768]{1,0:T(8,128)(2,1)S(1)}, bf16[384,768]{1,0:T(8,128)(2,1)S(1)}, u32[]{:S(2)}, u32[]{:S(2)}) collective-permute-start(bf16[384,768]{1,0:T(8,128)(2,1)S(1)} %collective-permute-done.5.refs_4_), channel_id=1, source_target_pairs={{0,2},{1,3},{2,0},{3,1},{4,6},{5,7},{6,4},{7,5},{8,10},{9,11},{10,... | collective-permute-start | bytes 1769480 | tf_op jit(solution)/shard_map/ppermute | solution.py:991
  75.5 34.1 %collective-permute-start.2 = (bf16[384,768]{1,0:T(8,128)(2,1)S(1)}, bf16[384,768]{1,0:T(8,128)(2,1)S(1)}, u32[]{:S(2)}, u32[]{:S(2)}) collective-permute-start(bf16[384,768]{1,0:T(8,128)(2,1)S(1)} %copy-done.30), channel_id=1, source_target_pairs={{0,1},{1,0},{2,3},{3,2},{4,5},{5,4},{6,7},{7,6},{8,9},{9,8},{10,11... | collective-permute-start | bytes 1769480 | tf_op jit(solution)/shard_map/ppermute | solution.py:991
  77.0 32.6 %collective-permute-start.6 = (bf16[384,768]{1,0:T(8,128)(2,1)S(1)}, bf16[384,768]{1,0:T(8,128)(2,1)S(1)}, u32[]{:S(2)}, u32[]{:S(2)}) collective-permute-start(bf16[384,768]{1,0:T(8,128)(2,1)S(1)} %collective-permute-done.5.refs_4_), channel_id=1, source_target_pairs={{0,1},{1,0},{2,3},{3,2},{4,5},{5,4},{6,7},{7,6},{8,9},{9,8},{10,11... | collective-permute-start | bytes 1769480 | tf_op jit(solution)/shard_map/ppermute | solution.py:991
  82.5 27.9 %collective-permute-start.4 = (bf16[384,768]{1,0:T(8,128)(2,1)S(1)}, bf16[384,768]{1,0:T(8,128)(2,1)}, u32[]{:S(2)}, u32[]{:S(2)}) collective-permute-start(bf16[384,768]{1,0:T(8,128)(2,1)S(1)} %collective-permute-done.3.refs_2_), channel_id=1, source_target_pairs={{0,1},{1,0},{2,3},{3,2},{4,5},{5,4},{6,7},{7,6},{8,9},{9,8},{10,11... | collective-permute-start | bytes 1769480 | tf_op jit(solution)/shard_map/ppermute | solution.py:991
  144.5 9.9 %collective-permute-start.9 = (bf16[2,3,192,128]{3,2,1,0:T(8,128)(2,1)}, bf16[2,3,192,128]{3,2,1,0:T(8,128)(2,1)S(1)}, u32[]{:S(2)}, u32[]{:S(2)}) collective-permute-start(bf16[2,3,192,128]{3,2,1,0:T(8,128)(2,1)} %get-tuple-element.65), channel_id=1, source_target_pairs={{0,2},{1,3},{2,0},{3,1},{4,6},{5,7},{6,4},{7,5},{8,10},{9,11},{10,... | collective-permute-start | bytes 884744 | tf_op jit(solution)/shard_map/ppermute | solution.py:991
  155.8 7.7 %collective-permute-start.13 = (bf16[384,768]{1,0:T(8,128)(2,1)S(1)}, bf16[384,768]{1,0:T(8,128)(2,1)S(1)}, u32[]{:S(2)}, u32[]{:S(2)}) collective-permute-start(bf16[384,768]{1,0:T(8,128)(2,1)S(1)} %copy-done.2), channel_id=1, source_target_pairs={{0,1},{1,0},{2,3},{3,2},{4,5},{5,4},{6,7},{7,6},{8,9},{9,8},{10,11... | collective-permute-start | bytes 1769480 | tf_op jit(solution)/shard_map/ppermute | solution.py:991
  211.9 8.2 %collective-permute-start.16 = (bf16[2,3,192,128]{3,2,1,0:T(8,128)(2,1)S(1)}, bf16[2,3,192,128]{3,2,1,0:T(8,128)(2,1)S(1)}, u32[]{:S(2)}, u32[]{:S(2)}) collective-permute-start(bf16[2,3,192,128]{3,2,1,0:T(8,128)(2,1)S(1)} %copy-done.36), channel_id=1, source_target_pairs={{0,2},{1,3},{2,0},{3,1},{4,6},{5,7},{6,4},{7,5},{8,10},{9,11},{10,... | collective-permute-start | bytes 884744 | tf_op jit(solution)/shard_map/ppermute | solution.py:991
  264.7 37.4 %collective-permute-start.22 = (bf16[384,768]{1,0:T(8,128)(2,1)}, bf16[384,768]{1,0:T(8,128)(2,1)S(1)}, u32[]{:S(2)}, u32[]{:S(2)}) collective-permute-start(bf16[384,768]{1,0:T(8,128)(2,1)} %get-tuple-element.89), channel_id=1, source_target_pairs={{0,1},{1,0},{2,3},{3,2},{4,5},{5,4},{6,7},{7,6},{8,9},{9,8},{10,11... | collective-permute-start | bytes 1769480 | tf_op jit(solution)/shard_map/ppermute | solution.py:991
  272.8 104.5 %all-to-all-start.1 = ((bf16[32,24,576]{2,1,0:T(8,128)(2,1)}), bf16[32,24,576]{2,1,0:T(8,128)(2,1)}, u32[]{:S(2)}, u32[]{:S(2)}) async-start(bf16[32,24,576]{2,1,0:T(8,128)(2,1)} %bitcast.65), calls=%async_computation.1 | async-start | bytes 1966080 | tf_op jit(solution)/shard_map/all_to_all | solution.py:1176
  301.7 13.8 %collective-permute-start.19 = (bf16[384,768]{1,0:T(8,128)(2,1)}, bf16[384,768]{1,0:T(8,128)(2,1)S(1)}, u32[]{:S(2)}, u32[]{:S(2)}) collective-permute-start(bf16[384,768]{1,0:T(8,128)(2,1)} %get-tuple-element.85), channel_id=1, source_target_pairs={{0,1},{1,0},{2,3},{3,2},{4,5},{5,4},{6,7},{7,6},{8,9},{9,8},{10,11... | collective-permute-start | bytes 1769480 | tf_op jit(solution)/shard_map/ppermute | solution.py:991
  301.9 13.8 %collective-permute-start.21 = (bf16[384,768]{1,0:T(8,128)(2,1)}, bf16[384,768]{1,0:T(8,128)(2,1)S(1)}, u32[]{:S(2)}, u32[]{:S(2)}) collective-permute-start(bf16[384,768]{1,0:T(8,128)(2,1)} %get-tuple-element.87), channel_id=1, source_target_pairs={{0,1},{1,0},{2,3},{3,2},{4,5},{5,4},{6,7},{7,6},{8,9},{9,8},{10,11... | collective-permute-start | bytes 1769480 | tf_op jit(solution)/shard_map/ppermute | solution.py:991
  303.1 21.3 %collective-permute-start.23 = (bf16[384,768]{1,0:T(8,128)(2,1)}, bf16[384,768]{1,0:T(8,128)(2,1)S(1)}, u32[]{:S(2)}, u32[]{:S(2)}) collective-permute-start(bf16[384,768]{1,0:T(8,128)(2,1)} %add_convert_fusion.1), channel_id=1, source_target_pairs={{0,2},{1,3},{2,0},{3,1},{4,6},{5,7},{6,4},{7,5},{8,10},{9,11},{10,... | collective-permute-start | bytes 1769480 | tf_op jit(solution)/shard_map/ppermute | solution.py:991
  314.0 20.6 %collective-permute-start.18 = (bf16[384,768]{1,0:T(8,128)(2,1)}, bf16[384,768]{1,0:T(8,128)(2,1)S(1)}, u32[]{:S(2)}, u32[]{:S(2)}) collective-permute-start(bf16[384,768]{1,0:T(8,128)(2,1)} %get-tuple-element.83), channel_id=1, source_target_pairs={{0,1},{1,0},{2,3},{3,2},{4,5},{5,4},{6,7},{7,6},{8,9},{9,8},{10,11... | collective-permute-start | bytes 1769480 | tf_op jit(solution)/shard_map/ppermute | solution.py:991
  315.6 25.0 %collective-permute-start.20 = (bf16[384,768]{1,0:T(8,128)(2,1)S(1)}, bf16[384,768]{1,0:T(8,128)(2,1)S(1)}, u32[]{:S(2)}, u32[]{:S(2)}) collective-permute-start(bf16[384,768]{1,0:T(8,128)(2,1)S(1)} %add_convert_fusion.2), channel_id=1, source_target_pairs={{0,2},{1,3},{2,0},{3,1},{4,6},{5,7},{6,4},{7,5},{8,10},{9,11},{10,... | collective-permute-start | bytes 1769480 | tf_op jit(solution)/shard_map/ppermute | solution.py:991
  327.5 25.8 %collective-permute-start.24 = (bf16[384,768]{1,0:T(8,128)(2,1)}, bf16[384,768]{1,0:T(8,128)(2,1)S(1)}, u32[]{:S(2)}, u32[]{:S(2)}) collective-permute-start(bf16[384,768]{1,0:T(8,128)(2,1)} %add_convert_fusion), channel_id=1, source_target_pairs={{6,2},{7,3},{0,4},{1,5},{10,6},{11,7},{4,8},{5,9},{14,10},{15,11},... | collective-permute-start | bytes 1769480 | tf_op jit(solution)/shard_map/ppermute | solution.py:1172
  376.5 8.7 %collective-permute-start.29 = (f32[16,768]{1,0:T(8,128)}, f32[16,768]{1,0:T(8,128)}, u32[]{:S(2)}, u32[]{:S(2)}) collective-permute-start(f32[16,768]{1,0:T(8,128)} %select_maximum_fusion), channel_id=1, source_target_pairs={{0,1},{1,0},{2,3},{3,2},{4,5},{5,4},{6,7},{7,6},{8,9},{9,8},{10,11... | collective-permute-start | bytes 147464 | tf_op jit(solution)/shard_map/ppermute | solution.py:991
  388.8 9.6 %collective-permute-start.26 = (f32[8,768]{1,0:T(8,128)S(1)}, f32[8,768]{1,0:T(8,128)S(1)}, u32[]{:S(2)}, u32[]{:S(2)}) collective-permute-start(f32[8,768]{1,0:T(8,128)S(1)} %get-tuple-element.200), channel_id=1, source_target_pairs={{1,0},{2,1},{3,2},{4,3},{5,4},{6,5},{7,6},{8,7},{9,8},{10,9},{11,1... | collective-permute-start | bytes 73736 | tf_op jit(solution)/shard_map/ppermute | solution.py:1195
  (53 other events, 376.8 us)
Sparse Core Ops, SparseCore 0:
  15.0 118.1 all-gather.2
  211.1 171.5 reduce-scatter.1
where the time goes:
time: 431 us; the launch traced here: 423 us
  Pallas kernels  179 us (42%)
  waiting for transfers between devices  78 us (18%)
  starting transfers between devices  77.6 us (18%)
  local copies, waits for them, and re-layouts  49.4 us (11%)
  other arithmetic  22.4 us (5%)
  between operations  15.5 us (4%)
    ppermute x25, waiting for transfers between devices, flip(): return lax.ppermute(x, ULY, [(i, i ^ bit) for i in range(4)])  60.7 us
    pallas_call x1, Pallas kernels, attend_back(): kernel_call(partial(attend_back_kernel, heads), (struct((rows, TILE), bf1...  35.2 us
    ppermute x25, starting transfers between devices, flip(): return lax.ppermute(x, ULY, [(i, i ^ bit) for i in range(4)])  26.9 us
    pallas_call x1, Pallas kernels, attend(): kernel_call(partial(attend_kernel, heads), (struct(sent, bf16), struct(se...  25.5 us
    all_to_all x1, starting transfers between devices, local(): lax.all_to_all(qkv_grad.reshape(n_dev, rows_dev, 3 * width), RING, 0, 0,...  22.7 us
    pallas_call x1, Pallas kernels, gbst_backward(): kernel_call(gbst_backward_kernel, (struct((nb + 16, d), f32), struct((8,...  21 us
    pallas_call x1, Pallas kernels, feed(): kernel_call(feed_kernel, (struct((tok, d), f32), struct((tok, d), bf16),...  15.4 us
    pallas_call x2, Pallas kernels, project_back(): kernel_call(partial(project_back_kernel, is_halo), tuple((struct((tok, d)...  11.6 us
  transfers between devices with their start and end apart: 38, of which 17 were waited for; matrix products, arithmetic and copies ran while one was open for 12% of the time, Pallas kernels for 33%

commit v1 on v0

v1 whole, which is shorter than its diff:
```python
from functools import partial

import jax
import jax.numpy as jnp
from jax import lax
from jax.experimental import pallas as pl
from jax.experimental.pallas import tpu as pltpu
from jax.sharding import Mesh, PartitionSpec as P

HEADS = 12
HEAD_DIM = 64
NBUCK = 32
CONV = 5
DOC_TOK = 1024
TILE = 256
FORM = 16
PHASES = 12
EPS = 1e-06
BIG = 1e30
GELU_C = 0.7978845608028654
GELU_A = 0.044715

bf16 = jnp.bfloat16
f32 = jnp.float32
RING = ("ctx", "ux", "uc")
ULY = ("ux", "uc")
highest = lax.Precision.HIGHEST


def dot(left, right, dims=((1,), (0,))):
    return lax.dot_general(left, right, (dims, ((), ())), preferred_element_type=f32)


def kernel_call(body, outs, *, grid=(1,), ins, scratch=(), prefetch=0, out_specs=None, flops=0, moved=0, vmem=40, name=None):
    params = pltpu.CompilerParams(
        dimension_semantics=("arbitrary",) * len(grid), vmem_limit_bytes=vmem << 20
    )
    return pl.pallas_call(
        body,
        out_shape=outs,
        grid_spec=pltpu.PrefetchScalarGridSpec(
            num_scalar_prefetch=prefetch,
            grid=grid,
            in_specs=ins,
            out_specs=out_specs,
            scratch_shapes=list(scratch),
        ),
        compiler_params=params,
        cost_estimate=pl.CostEstimate(flops=int(flops), bytes_accessed=int(moved), transcendentals=0),
        name=name,
    )


def whole(shape, once=True):
    zeros = (0,) * len(shape)
    if once:
        return pl.BlockSpec(shape, lambda *a: zeros, pipeline_mode=pl.Buffered(1))
    return pl.BlockSpec(shape, lambda *a: zeros)


def in_hbm(*arrays):
    return tuple(pltpu.with_memory_space_constraint(x, pltpu.HBM) for x in arrays)


def struct(shape, dtype):
    return jax.ShapeDtypeStruct(shape, dtype)


def block_of(size, at):
    first = size * (at // size)
    return range(first, first + size)


def token_pairs(tok):
    found = set()
    for byte in (2 * tok, 2 * tok + 1):
        for size in range(1, 5):
            found |= set(block_of(size, byte))
    return sorted(found)


def mix_coefs(weights):
    coefs = {}
    for tok in range(PHASES // 2):
        for at in token_pairs(tok):
            total = None
            for byte in (2 * tok, 2 * tok + 1):
                for size in range(1, 5):
                    if at in block_of(size, byte):
                        term = weights[size - 1][byte] * (0.5 / size)
                        total = term if total is None else total + term
            coefs[tok, at] = total
    return coefs


def lane_chunks(feats):
    return [slice(128 * c, 128 * (c + 1)) for c in range(feats // 128)]


def fill_bytes(pad, lo, emb, hi):
    byte_count, feats = emb.shape
    chunks = lane_chunks(feats)
    for c, cols in enumerate(chunks):
        pad[c, 0:8, :] = lo[:, cols].astype(f32)
        pad[c, 8 + byte_count : 16 + byte_count, :] = hi[:, cols].astype(f32)

    def fill(t, _):
        at = pl.multiple_of(t * 32, 32)
        for c, cols in enumerate(chunks):
            pad[c, pl.ds(at + 8, 32), :] = emb[pl.ds(at, 32), cols].astype(f32)
        return 0

    lax.fori_loop(0, byte_count // 32, fill, 0)


def gbst_forward_kernel(lo, emb, hi, msk, cw, sw, gain, gb, nrm, conv, aw, pad, mix):
    byte_count, feats = emb.shape
    chunks = lane_chunks(feats)
    fill_bytes(pad, lo, emb, hi)
    lanes = lax.broadcasted_iota(jnp.int32, (8, 128), 1)

    def step(g, _):
        base = g * 8 * PHASES + 8
        rows = pl.ds(pl.multiple_of(8 * g, 8), 8)
        first = []
        for p in range(PHASES):
            mask = msk[pl.ds(base + p, 8, stride=PHASES), :]
            same = {k: jnp.broadcast_to(mask[:, k : k + 1], (8, 128)) for k in (0, 1, 3, 4)}
            dots = None
            for c, cols in enumerate(chunks):
                x = pad[c, pl.ds(base + p, 8, stride=PHASES), :] * cw[2:3, cols]
                for k in (0, 1, 3, 4):
                    x = x + pad[c, pl.ds(base + p + k - 2, 8, stride=PHASES), :] * same[k] * cw[k : k + 1, cols]
                conv[p, rows, cols] = x
                term = x * sw[:, cols]
                dots = term if dots is None else dots + term
            first.append(jnp.broadcast_to(jnp.sum(dots, axis=1, keepdims=True), (8, 128)))
        weights = [[None] * PHASES for _ in range(4)]
        packed = jnp.zeros((8, 128), f32)
        for p in range(PHASES):
            scores = []
            for size in range(1, 5):
                total = None
                for at in block_of(size, p):
                    total = first[at] if total is None else total + first[at]
                scores.append(total * (1.0 / size))
            top = jnp.maximum(jnp.maximum(scores[0], scores[1]), jnp.maximum(scores[2], scores[3]))
            exps = [jnp.exp(s - top) for s in scores]
            inv = 1.0 / (exps[0] + exps[1] + exps[2] + exps[3])
            for size in range(4):
                weights[size][p] = exps[size] * inv
                packed = jnp.where(lanes == 4 * p + size, weights[size][p], packed)
        aw[rows, :] = packed
        coefs = mix_coefs(weights)
        for tok in range(PHASES // 2):
            for c, cols in enumerate(chunks):
                out = None
                for at in token_pairs(tok):
                    term = coefs[tok, at] * conv[at, rows, cols]
                    out = term if out is None else out + term
                mix[c, pl.ds(g * 4 * PHASES + tok, 8, stride=PHASES // 2), :] = out
        return 0

    lax.fori_loop(0, byte_count // (8 * PHASES), step, 0)

    def norm(t, _):
        at = pl.multiple_of(t * 16, 16)
        v = jnp.concatenate([mix[c, pl.ds(at, 16), :] for c in range(len(chunks))], axis=1)
        r = lax.rsqrt(jnp.mean(v * v, axis=1, keepdims=True) + EPS)
        gb[pl.ds(at, 16), :] = v
        nrm[pl.ds(at, 16), :] = (v * r * gain[...]).astype(bf16)
        return 0

    lax.fori_loop(0, byte_count // 32, norm, 0)


def gbst_forward(lo, emb, hi, msk, cw, sw, gain):
    nb, d = emb.shape
    return kernel_call(
        gbst_forward_kernel,
        (
            struct((nb // 2, d), f32),
            struct((nb // 2, d), bf16),
            struct((PHASES, nb // PHASES, d), f32),
            struct((nb // PHASES, 128), f32),
        ),
        ins=[whole(x.shape) for x in (lo, emb, hi, msk, cw, sw, gain)],
        out_specs=(
            whole((nb // 2, d)),
            whole((nb // 2, d)),
            whole((PHASES, nb // PHASES, d)),
            whole((nb // PHASES, 128)),
        ),
        scratch=[pltpu.VMEM((d // 128, nb + 16, 128), f32), pltpu.VMEM((d // 128, nb // 2, 128), f32)],
        flops=60 * nb * d,
        moved=20 * nb * d,
        vmem=20,
        name="gbst_forward",
    )(lo, emb, hi, msk, cw, sw, gain)


def gbst_backward_kernel(keep, recv, gb, dmid, gain, conv, aw, lo, emb, hi, msk, cw, sw, eg, small, dtok, dconv, pad, acc):
    byte_count, feats = emb.shape
    chunks = lane_chunks(feats)
    acc[...] = jnp.zeros_like(acc)
    fill_bytes(pad, lo, emb, hi)
    for c in range(len(chunks)):
        dconv[c, 0:16, :] = jnp.zeros((16, 128), f32)
        dconv[c, 16 + byte_count : 32 + byte_count, :] = jnp.zeros((16, 128), f32)

    def norm(t, _):
        at = pl.multiple_of(t * 16, 16)
        e = keep[pl.ds(at, 16), :] + recv[pl.ds(at, 16), :].astype(f32)
        v = gb[pl.ds(at, 16), :]
        r = lax.rsqrt(jnp.mean(v * v, axis=1, keepdims=True) + EPS)
        ge = gain[...] * e
        m = jnp.mean(ge * v, axis=1, keepdims=True)
        out = dmid[pl.ds(at, 16), :] + r * ge - v * (r * r * r * m)
        for c, cols in enumerate(chunks):
            dtok[c, pl.ds(at, 16), :] = out[:, cols]
        part = e * v * r
        acc[48:56, :] = acc[48:56, :] + part[0:8] + part[8:16]
        return 0

    lax.fori_loop(0, byte_count // 32, norm, 0)

    def step(g, _):
        rows = pl.ds(pl.multiple_of(8 * g, 8), 8)
        half = PHASES // 2

        def tok_rows(tok, c):
            return dtok[c, pl.ds(g * 8 * half + tok, 8, stride=half), :]

        inner = {}
        for tok in range(half):
            toks = [tok_rows(tok, c) for c in range(len(chunks))]
            for at in token_pairs(tok):
                dots = None
                for c, cols in enumerate(chunks):
                    term = toks[c] * conv[at, rows, cols]
                    dots = term if dots is None else dots + term
                inner[tok, at] = jnp.broadcast_to(jnp.sum(dots, axis=1, keepdims=True), (8, 128))
        tile = aw[rows, :]
        weights = [
            [jnp.broadcast_to(tile[:, 4 * p + size : 4 * p + size + 1], (8, 128)) for p in range(PHASES)]
            for size in range(4)
        ]
        coefs = mix_coefs(weights)
        dsize = [[None] * PHASES for _ in range(4)]
        for p in range(PHASES):
            cs = []
            for size in range(1, 5):
                total = None
                for at in block_of(size, p):
                    total = inner[p // 2, at] if total is None else total + inner[p // 2, at]
                cs.append(total * (0.5 / size))
            mean = sum(weights[s][p] * cs[s] for s in range(4))
            for s in range(4):
                dsize[s][p] = weights[s][p] * (cs[s] - mean)
        slopes = []
        for at in range(PHASES):
            e = None
            for size in range(1, 5):
                for p in block_of(size, at):
                    term = dsize[size - 1][p] * (1.0 / size)
                    e = term if e is None else e + term
            slopes.append(e)
        for c, cols in enumerate(chunks):
            toks = [tok_rows(tok, c) for tok in range(half)]
            score = acc[40:48, cols]
            for at in range(PHASES):
                out = slopes[at] * sw[:, cols]
                for tok in range(half):
                    if (tok, at) in coefs:
                        out = out + coefs[tok, at] * toks[tok]
                dconv[c, pl.ds(g * 8 * PHASES + 16 + at, 8, stride=PHASES), :] = out
                score = score + slopes[at] * conv[at, rows, cols]
            acc[40:48, cols] = score
        return 0

    lax.fori_loop(0, byte_count // (8 * PHASES), step, 0)

    def taps(t, _):
        masks = []
        for u in range(2):
            mask = msk[pl.ds(pl.multiple_of(t * 16 + 8 * u, 8), 8), :]
            masks.append({k: jnp.broadcast_to(mask[:, 4 - k : 5 - k], (8, 128)) for k in (0, 1, 3, 4)})
        for c, cols in enumerate(chunks):
            sums = [None] * CONV
            for u in range(2):
                at = pl.multiple_of(t * 16 + 8 * u, 8)
                x = pad[c, pl.ds(at, 8), :]
                out = None
                for k in range(CONV):
                    z = dconv[c, pl.ds(at + 8 + 2 - k, 8), :]
                    if k != 2:
                        z = z * masks[u][k]
                    term = z * cw[k : k + 1, cols]
                    out = term if out is None else out + term
                    sums[k] = z * x if sums[k] is None else sums[k] + z * x
                eg[pl.ds(at, 8), cols] = out
            for k in range(CONV):
                acc[8 * k : 8 * k + 8, cols] = acc[8 * k : 8 * k + 8, cols] + sums[k]
        return 0

    lax.fori_loop(0, (byte_count + 16) // 16, taps, 0)
    small[...] = jnp.zeros_like(small)
    for k in range(7):
        small[k : k + 1, :] = jnp.sum(acc[8 * k : 8 * k + 8, :], axis=0, keepdims=True)


def gbst_backward(keep, recv, gb, dmid, gain, conv, aw, lo, emb, hi, msk, cw, sw):
    nb, d = emb.shape
    args = (keep, recv, *in_hbm(gb, dmid, gain, conv, aw, lo, emb, hi, msk, cw, sw))
    return kernel_call(
        gbst_backward_kernel,
        (struct((nb + 16, d), f32), struct((8, d), f32)),
        ins=[whole(x.shape) for x in args],
        out_specs=(whole((nb + 16, d)), whole((8, d))),
        scratch=[
            pltpu.VMEM((d // 128, nb // 2, 128), f32),
            pltpu.VMEM((d // 128, nb + 32, 128), f32),
            pltpu.VMEM((d // 128, nb + 16, 128), f32),
            pltpu.VMEM((56, d), f32),
        ],
        flops=120 * nb * d,
        moved=24 * nb * d,
        vmem=28,
        name="gbst_backward",
    )(*args)


def halo_row(who, tok_dev, ext):
    return jnp.where(who >= 2, (who - 2) * tok_dev, ext - 2 * tok_dev + who * tok_dev)


def project_kernel(n_heads, info, *refs):
    own, far, w, cq, ck, (q, k, v, vt, wp) = refs[:4], refs[4:8], refs[8], refs[9], refs[10], refs[11:16]
    tok, _ = own[0].shape
    me = info[0]
    part = w.shape[2] // 3
    rows = w.shape[1]
    wp[...] = jnp.zeros_like(wp)
    for b in range(w.shape[0]):
        at = pl.ds(pl.multiple_of(info[1 + b] * rows, 16), rows)
        block = w[b]
        for j in range(3):
            wp[at, TILE * j : TILE * j + part] = block[:, part * j : part * (j + 1)]
    ext = k.shape[0]
    left = (ext - q.shape[0]) // 2
    for rel in range(4):
        who = me ^ rel
        out = dot(own[rel][...], wp[...])
        at = pl.ds(pl.multiple_of(who * tok, 128), tok)
        q[at, :] = out[:, :TILE].astype(bf16) + cq[at, :]
        edge = dot(far[rel][...], wp[:, TILE:])
        for at, ks, vs in (
            (left + who * tok, out[:, TILE : 2 * TILE], out[:, 2 * TILE :]),
            (halo_row(who, tok, ext), edge[:, :TILE], edge[:, TILE:]),
        ):
            at = pl.ds(pl.multiple_of(at, 128), tok)
            k[at, :] = ks.astype(bf16) + ck[at, :]
            v[at, :] = vs.astype(bf16)
            vt[:, at] = vs.T.astype(bf16)


def project(info, own, far, w, cq, ck, n_heads):
    tok, d = own[0].shape
    rows, ext = 4 * tok, 8 * tok
    args = (*own, *far, w, cq, ck)
    shapes = [(rows, TILE), (ext, TILE), (ext, TILE), (TILE, ext), (d, 3 * TILE)]
    return kernel_call(
        partial(project_kernel, n_heads),
        tuple(struct(x, bf16) for x in shapes),
        prefetch=1,
        ins=[whole(x.shape) for x in args],
        out_specs=tuple(whole(x) for x in shapes),
        flops=2 * ext * d * 3 * TILE,
        moved=2 * (ext * d + 2 * ext * TILE + d * d),
        vmem=30,
        name="project",
    )(info, *args)


def project_back_kernel(is_halo, me, dq, dk, dv, wp, keep0, keep2, send1, send3):
    tok = keep0.shape[0]
    ext = dk.shape[0]
    left = (ext - dq.shape[0]) // 2
    for rel, ref in ((3, send3), (1, send1), (2, keep2), (0, keep0)):
        who = me[0] ^ rel
        if is_halo:
            at = pl.multiple_of(halo_row(who, tok, ext), 128)
            out = dot(dk[pl.ds(at, tok), :], wp[:, TILE : 2 * TILE], ((1,), (1,)))
        else:
            at = pl.multiple_of(left + who * tok, 128)
            out = dot(dk[pl.ds(at, tok), :], wp[:, TILE : 2 * TILE], ((1,), (1,)))
            mine = pl.multiple_of(who * tok, 128)
            out = out + dot(dq[pl.ds(mine, tok), :], wp[:, :TILE], ((1,), (1,)))
        out = out + dot(dv[pl.ds(at, tok), :], wp[:, 2 * TILE :], ((1,), (1,)))
        ref[...] = out.astype(ref.dtype)


def project_back(is_halo, me, dq, dk, dv, wp):
    ext, d = dk.shape[0], wp.shape[0]
    tok = ext // 8
    args = (dq, dk, dv, wp)
    kinds = (f32, f32, bf16, bf16)
    return kernel_call(
        partial(project_back_kernel, is_halo),
        tuple(struct((tok, d), kind) for kind in kinds),
        prefetch=1,
        ins=[whole(x.shape) for x in args],
        out_specs=tuple(whole((tok, d)) for _ in kinds),
        flops=2 * ext // 2 * d * 3 * TILE,
        moved=4 * ext * d,
        vmem=20,
        name="project_back",
    )(me, *args)


def project_grad_kernel(info, *refs):
    own, far, (dq, dk, dv, mkeep, mrecv, mgot), out, flat = refs[:4], refs[4:8], refs[8:14], refs[14], refs[15]
    tok = own[0].shape[0]
    ext = dk.shape[0]
    me = info[0]
    left = (ext - dq.shape[0]) // 2
    part = mgot.shape[1]
    totals = [None] * 3

    def turned(ref, at):
        return ref[pl.ds(pl.multiple_of(at, 128), tok), :].astype(f32).T[:part].astype(bf16)

    for rel in range(4):
        who = me ^ rel
        at = left + who * tok
        edge = halo_row(who, tok, ext)
        terms = [
            dot(turned(dq, who * tok), own[rel][...]),
            dot(turned(dk, at), own[rel][...]) + dot(turned(dk, edge), far[rel][...]),
            dot(turned(dv, at), own[rel][...]) + dot(turned(dv, edge), far[rel][...]),
        ]
        totals = [t if x is None else x + t for x, t in zip(totals, terms)]
    for j in range(3):
        flat[:, part * j : part * (j + 1)] = totals[j].T.astype(bf16)
    merged = mkeep[0] + mrecv[0].astype(f32) + mgot[...].astype(f32)
    flat[:, 3 * part :] = merged.astype(bf16)
    rows = out.shape[1]
    for b in range(out.shape[0]):
        out[b] = flat[pl.ds(pl.multiple_of(info[1 + b] * rows, 16), rows), :]


def project_grad(info, own, far, dq, dk, dv, mkeep, mrecv, mgot, blocks):
    tok, d = own[0].shape
    args = (*in_hbm(*own, *far), dq, dk, dv, *in_hbm(mkeep, mrecv, mgot))
    shape = (blocks, d // blocks, 4 * mgot.shape[1])
    return kernel_call(
        project_grad_kernel,
        struct(shape, bf16),
        prefetch=1,
        ins=[whole(x.shape) for x in args],
        out_specs=whole(shape),
        scratch=[pltpu.VMEM((d, shape[2]), bf16)],
        flops=2 * 8 * tok * d * 3 * mgot.shape[1],
        moved=2 * 12 * tok * d,
        vmem=28,
        name="project_grad",
    )(info, *args)


def fill_bias(diag, bias):
    count = bias.shape[0]
    heads = diag.shape[0]

    def tile(t, _):
        seg = diag[:, pl.ds(pl.multiple_of((count - 1 - t) * TILE, TILE), 2 * TILE)]
        for h in range(heads):
            rows = jnp.broadcast_to(seg[h : h + 1, :], (TILE, 2 * TILE))
            turned = pltpu.roll(rows, TILE, axis=1, stride=1, stride_axis=0)
            bias[t, :, TILE * h : TILE * (h + 1)] = turned[:, :TILE]
        return 0

    lax.fori_loop(0, count, tile, 0)


def sum_diagonals(tiles, out):
    count, heads, _ = out.shape

    def tile(t, _):
        for h in range(heads):
            part = tiles[t, :, TILE * h : TILE * (h + 1)]
            cur = jnp.concatenate([part, jnp.zeros_like(part)], axis=1)
            rows = TILE
            while rows > 8:
                rows //= 2
                cur = cur[:rows] + pltpu.roll(cur[rows:], 2 * TILE - rows, axis=1)
            total = cur[0:1]
            for i in range(1, 8):
                total = total + pltpu.roll(cur[i : i + 1], 2 * TILE - i, axis=1)
            out[count - 1 - t, h : h + 1, :] = pltpu.roll(total, TILE, axis=1)
        return 0

    lax.fori_loop(0, count, tile, 0)


def lane_head(shape):
    return lax.broadcasted_iota(jnp.int32, shape, 1) // HEAD_DIM


def fill_queries(heads, q, q3):
    turned = q[...].astype(f32).T
    row = lax.broadcasted_iota(jnp.int32, (TILE, TILE), 0) // HEAD_DIM
    for h in range(heads):
        q3[:, TILE * h : TILE * (h + 1)] = jnp.where((row == h) | (row >= heads), turned, 0.0).astype(bf16)


def attend_kernel(heads, info, q, k, vt, diag, oa, ob, oloc, lse, bias, q3, sc, ac):
    i = pl.program_id(0)
    grid = pl.num_programs(0)
    me = info[2 * grid]
    ext = k.shape[0]
    wide = heads * TILE

    @pl.when(i == 0)
    def _():
        fill_bias(diag, bias)

    lo, hi = info[i], info[grid + i]
    away = (ext // TILE - grid) // 2
    fill_queries(heads, q, q3)
    ac[...] = jnp.zeros_like(ac)

    def scores(kt, top):
        at = pl.multiple_of(kt * TILE, TILE)
        s = dot(k[pl.ds(at, TILE), :], q3[...]) + bias[kt - i - away + 4]
        sc[kt - lo] = s
        return jnp.maximum(top, jnp.max(s.reshape(TILE // 8, 8, wide), axis=0))

    top = lax.fori_loop(lo, hi, scores, jnp.full((8, wide), -jnp.inf, f32))
    top = jnp.max(top, axis=0, keepdims=True)

    def gather(kt, total):
        at = pl.multiple_of(kt * TILE, TILE)
        p = jnp.exp(sc[kt - lo] - top)
        low = p.astype(bf16)
        for h in range(heads):
            cols = slice(TILE * h, TILE * (h + 1))
            head = slice(HEAD_DIM * h, HEAD_DIM * (h + 1))
            ac[head, :] = ac[head, :] + dot(vt[head, pl.ds(at, TILE)], low[:, cols])
        return total + jnp.sum(p.reshape(TILE // 8, 8, wide), axis=0)

    total = lax.fori_loop(lo, hi, gather, jnp.zeros((8, wide), f32))
    total = jnp.sum(total, axis=0, keepdims=True)
    inv = 1.0 / total
    lse[0] = jnp.broadcast_to(top + jnp.log(total), (8, wide))
    parts = []
    for h in range(heads):
        parts.append(ac[HEAD_DIM * h : HEAD_DIM * (h + 1), :] * inv[:, TILE * h : TILE * (h + 1)])
    turned = jnp.concatenate(parts, axis=0).astype(bf16)
    oloc[...] = turned
    per = oa.shape[1]
    for j in range(TILE // 128):
        chunk = i * (TILE // 128) + j
        rel = (chunk // per) ^ me
        piece = turned[:, 128 * j : 128 * (j + 1)]

        @pl.when(rel < 2)
        def _():
            oa[rel, chunk % per] = piece

        @pl.when(rel >= 2)
        def _():
            ob[rel - 2, chunk % per] = piece


def attend(info, q, k, vt, diag, heads, tok):
    rows, ext = q.shape[0], k.shape[0]
    grid = rows // TILE
    width = heads * HEAD_DIM
    sent = (2, tok // 128, width, 128)
    tile = pl.BlockSpec((TILE, TILE), lambda i, *_: (i, 0))
    return kernel_call(
        partial(attend_kernel, heads),
        (
            struct(sent, bf16),
            struct(sent, bf16),
            struct((width, rows), bf16),
            struct((grid, 8, heads * TILE), f32),
        ),
        grid=(grid,),
        prefetch=1,
        ins=[tile, whole(k.shape), whole(vt.shape), whole(diag.shape)],
        out_specs=(
            whole(sent),
            whole(sent),
            pl.BlockSpec((width, TILE), lambda i, *_: (0, i)),
            pl.BlockSpec((1, 8, heads * TILE), lambda i, *_: (i, 0, 0)),
        ),
        scratch=[
            pltpu.VMEM((9, TILE, heads * TILE), f32),
            pltpu.VMEM((TILE, heads * TILE), bf16),
            pltpu.VMEM((9, TILE, heads * TILE), f32),
            pltpu.VMEM((width, TILE), f32),
        ],
        flops=4 * rows * 1280 * TILE * heads,
        moved=8 * ext * TILE,
        vmem=30,
        name="attend",
    )(info, q, k, vt, diag)


def attend_back_kernel(
    heads, info, q, k, v, diag, oloc, lse, d0, d1, d2, d3,
    dq, dk, dv, sums,
    bias, tacc, kt_all, q3, g3, q3n, g3n, gall, dqa, dka, dva,
):
    i = pl.program_id(0)
    grid = pl.num_programs(0)
    me = info[2 * grid]
    ext = k.shape[0]
    per = d0.shape[0]
    width = heads * HEAD_DIM

    @pl.when(i == 0)
    def _():
        fill_bias(diag, bias)

        def turn(t, _):
            at = pl.ds(pl.multiple_of(t * TILE, TILE), TILE)
            kt_all[:, at] = k[at, :].astype(f32).T[:width].astype(bf16)
            return 0

        lax.fori_loop(0, ext // TILE, turn, 0)
        dka[...] = jnp.zeros_like(dka)
        dva[...] = jnp.zeros_like(dva)
        tacc[...] = jnp.zeros_like(tacc)
        for rel, piece in ((0, d0[...]), (2, d2[...]), (1, d1[...]), (3, d3[...])):
            gall[pl.ds((me ^ rel) * per, per)] = piece

    lo, hi = info[i], info[grid + i]
    away = (ext // TILE - grid) // 2
    where = lane_head((TILE, TILE))
    fill = jnp.zeros((TILE - width, TILE), f32)
    pieces = [gall[i * (TILE // 128) + j] for j in range(TILE // 128)]
    gt = jnp.concatenate(pieces, axis=1).astype(f32)
    grad = jnp.concatenate([gt, fill], axis=0).T
    prod = gt * oloc[...].astype(f32)
    deltas = []
    fill_queries(heads, q, q3)
    g3[...] = jnp.zeros_like(g3)
    for h in range(heads):
        rows = slice(TILE * h, TILE * (h + 1))
        head = slice(HEAD_DIM * h, HEAD_DIM * (h + 1))
        g3[head, rows] = gt[head, :].astype(bf16)
        q3n[rows, :] = jnp.where(where == h, q[...], jnp.zeros_like(q[...]))
        g3n[rows, :] = jnp.where(where == h, grad, 0.0).astype(bf16)
        deltas.append(jnp.sum(prod[HEAD_DIM * h : HEAD_DIM * (h + 1), :], axis=0, keepdims=True))
    delta = jnp.concatenate(deltas, axis=1)
    log = lse[0, 0:1, :]
    dqa[...] = jnp.zeros_like(dqa)

    def step(kt, _):
        at = pl.ds(pl.multiple_of(kt * TILE, TILE), TILE)
        rel = kt - i - away + 4
        s = dot(k[at, :], q3[...]) + bias[rel]
        p = jnp.exp(s - log)
        dp = dot(v[at, :], g3[...])
        ds = p * (dp - delta)
        tacc[rel] = tacc[rel] + ds
        low = ds.astype(bf16)
        dva[at, :] = dva[at, :] + dot(p.astype(bf16), g3n[...])
        dka[at, :] = dka[at, :] + dot(low, q3n[...])
        for h in range(heads):
            head = slice(HEAD_DIM * h, HEAD_DIM * (h + 1))
            dqa[head, :] = dqa[head, :] + dot(kt_all[head, at], low[:, TILE * h : TILE * (h + 1)])
        return 0

    lax.fori_loop(lo, hi, step, 0)
    dq[...] = jnp.concatenate([dqa[...], fill], axis=0).T.astype(bf16)

    @pl.when(i == grid - 1)
    def _():
        dk[...] = dka[...].astype(bf16)
        dv[...] = dva[...].astype(bf16)
        sum_diagonals(tacc, sums)


def attend_back(info, q, k, v, diag, oloc, lse, d0, d1, d2, d3, heads):
    rows, ext = q.shape[0], k.shape[0]
    grid = rows // TILE
    width = heads * HEAD_DIM
    tile = pl.BlockSpec((TILE, TILE), lambda i, *_: (i, 0))
    turned = pl.BlockSpec((width, TILE), lambda i, *_: (0, i))
    sums = (9, heads, 2 * TILE)
    return kernel_call(
        partial(attend_back_kernel, heads),
        (
            struct((rows, TILE), bf16),
            struct((ext, TILE), bf16),
            struct((ext, TILE), bf16),
            struct(sums, f32),
        ),
        grid=(grid,),
        prefetch=1,
        ins=[
            tile, whole(k.shape), whole(v.shape), whole(diag.shape),
            turned, pl.BlockSpec((1, 8, heads * TILE), lambda i, *_: (i, 0, 0)),
            whole(d0.shape), whole(d1.shape), whole(d2.shape), whole(d3.shape),
        ],
        out_specs=(tile, whole((ext, TILE)), whole((ext, TILE)), whole(sums)),
        scratch=[
            pltpu.VMEM((9, TILE, heads * TILE), f32),
            pltpu.VMEM((9, TILE, heads * TILE), f32),
            pltpu.VMEM((width, ext), bf16),
            pltpu.VMEM((TILE, heads * TILE), bf16),
            pltpu.VMEM((TILE, heads * TILE), bf16),
            pltpu.VMEM((heads * TILE, TILE), bf16),
            pltpu.VMEM((heads * TILE, TILE), bf16),
            pltpu.VMEM((rows // 128, width, 128), bf16),
            pltpu.VMEM((width, TILE), f32),
            pltpu.VMEM((ext, TILE), f32),
            pltpu.VMEM((ext, TILE), f32),
        ],
        flops=10 * rows * 1280 * TILE * heads,
        moved=16 * ext * TILE,
        vmem=44,
        name="attend_back",
    )(info, *in_hbm(q, k, v, diag, oloc, lse), d0, d1, d2, d3)


MERGE_ROWS = pl.BlockSpec((FORM, 144, TILE), lambda *a: (0, 4, 0), pipeline_mode=pl.Buffered(1))


def merge_rows(packed, src, part):
    span = FORM // 4
    low = 48 * part
    return packed[pl.ds(src * span, span), low : low + 48, :].reshape(48 * span, TILE)


def merge_kernel(info, a0, a1, a2, a3, packed, gb, gain, mid, nrm):
    per = a0.shape[0]
    for t in range(per):
        rows = slice(128 * t, 128 * (t + 1))
        total = [gb[rows, TILE * part : TILE * (part + 1)] for part in range(3)]
        for rel, piece in ((0, a0[t]), (2, a2[t]), (1, a1[t]), (3, a3[t])):
            flat = piece.astype(f32).T.astype(bf16)
            for part in range(3):
                total[part] = total[part] + dot(flat, merge_rows(packed, info[0] ^ rel, part))
        v = jnp.concatenate(total, axis=1)
        mid[rows, :] = v
        r = lax.rsqrt(jnp.mean(v * v, axis=1, keepdims=True) + EPS)
        nrm[rows, :] = (v * r * gain[...]).astype(bf16)


def merge(me, a0, a1, a2, a3, packed, gb, gain):
    tok, d = gb.shape
    args = (a0, a1, a2, a3, packed, gb, gain)
    specs = [MERGE_ROWS if x is packed else whole(x.shape) for x in args]
    args = in_hbm(*args)
    return kernel_call(
        merge_kernel,
        (struct((tok, d), f32), struct((tok, d), bf16)),
        prefetch=1,
        ins=specs,
        out_specs=(whole((tok, d)), whole((tok, d))),
        flops=2 * tok * d * d,
        moved=12 * tok * d,
        vmem=20,
        name="merge",
    )(me, *args)


def feed_kernel(nt, gr, wg, wu, wd, out, dn, hid, dg, du, osum, dsum):
    j = pl.program_id(0)

    @pl.when(j == 0)
    def _():
        osum[...] = jnp.zeros_like(osum)
        dsum[...] = jnp.zeros_like(dsum)

    wgt = wg[...].reshape(FORM * 48, TILE)
    wut = wu[...].reshape(FORM * 48, TILE)
    gate = dot(nt[...], wgt)
    up = dot(nt[...], wut)
    dh = None
    wds = []
    for part in range(3):
        wdt = wd[:, 64 * part : 64 * (part + 1), :].reshape(TILE, TILE)
        wds.append(wdt)
        term = dot(gr[:, TILE * part : TILE * (part + 1)], wdt, ((1,), (1,)))
        dh = term if dh is None else dh + term
    sq = gate * gate
    th = jnp.tanh(GELU_C * gate * (1.0 + GELU_A * sq))
    half = 0.5 * (1.0 + th)
    act = gate * half
    slope = half + 0.5 * gate * (1.0 - th * th) * (GELU_C * (1.0 + 3.0 * GELU_A * sq))
    h = (act * up).astype(bf16)
    g = (dh * up * slope).astype(bf16)
    u = (dh * act).astype(bf16)
    hid[...] = h
    dg[...] = g
    du[...] = u
    for part in range(3):
        cols = slice(TILE * part, TILE * (part + 1))
        osum[:, cols] = osum[:, cols] + dot(h, wds[part])
    dsum[...] = dsum[...] + dot(g, wgt, ((1,), (1,))) + dot(u, wut, ((1,), (1,)))

    @pl.when(j == pl.num_programs(0) - 1)
    def _():
        out[...] = osum[...].astype(out.dtype)
        dn[...] = dsum[...].astype(dn.dtype)


def feed(nt, gr, packed, units, kind):
    tok, d = nt.shape
    col = pl.BlockSpec((tok, TILE), lambda j: (0, j))
    full = whole((tok, d))
    return kernel_call(
        feed_kernel,
        (struct((tok, d), kind), struct((tok, d), kind)) + (struct((tok, units), bf16),) * 3,
        grid=(units // TILE,),
        ins=[
            full,
            full,
            pl.BlockSpec((FORM, 48, TILE), lambda j: (0, j, 0)),
            pl.BlockSpec((FORM, 48, TILE), lambda j: (0, 4 + j, 0)),
            pl.BlockSpec((4, 192, TILE), lambda j: (j, 2, 0)),
        ],
        out_specs=(full, full, col, col, col),
        scratch=[pltpu.VMEM((tok, d), f32), pltpu.VMEM((tok, d), f32)],
        flops=12 * tok * d * units,
        moved=2 * packed.size + 10 * tok * d + 6 * tok * units,
        vmem=24,
        name="feed",
    )(nt, gr, packed, packed, packed)


def middle_kernel(info, mid, da, db, og, gain, packed, dmid, dlow, ga, gb, gsum):
    tok, d = mid.shape
    gsum[...] = jnp.zeros_like(gsum)

    def norm(t, _):
        at = pl.ds(pl.multiple_of(t * 16, 16), 16)
        v = mid[at, :]
        e = da[at, :] + db[at, :].astype(f32)
        r = lax.rsqrt(jnp.mean(v * v, axis=1, keepdims=True) + EPS)
        ge = gain[...] * e
        m = jnp.mean(ge * v, axis=1, keepdims=True)
        out = og[at, :].astype(f32) + r * ge - v * (r * r * r * m)
        dmid[at, :] = out
        dlow[at, :] = out.astype(bf16)
        part = e * v * r
        gsum[...] = gsum[...] + part[0:8] + part[8:16]
        return 0

    lax.fori_loop(0, tok // 16, norm, 0)
    for rel in range(4):
        out = None
        for part in range(3):
            cols = slice(TILE * part, TILE * (part + 1))
            term = dot(merge_rows(packed, info[0] ^ rel, part), dlow[:, cols], ((1,), (1,)))
            out = term if out is None else out + term
        low = out.astype(bf16)
        for t in range(tok // 128):
            ref = ga if rel < 2 else gb
            ref[rel % 2, t] = low[:, 128 * t : 128 * (t + 1)]


def middle(me, mid, da, db, og, gain, packed):
    tok, d = mid.shape
    args = (mid, da, db, og, gain, packed)
    sent = (2, tok // 128, d // 4, 128)
    shapes = [((tok, d), f32), ((tok, d), bf16), (sent, bf16), (sent, bf16), ((8, d), f32)]
    return kernel_call(
        middle_kernel,
        tuple(struct(*s) for s in shapes),
        prefetch=1,
        ins=[MERGE_ROWS if x is packed else whole(x.shape) for x in args],
        out_specs=tuple(whole(s[0]) for s in shapes),
        flops=2 * tok * d * d,
        moved=30 * tok * d,
        vmem=24,
        name="middle",
    )(me, mid, da, db, *in_hbm(og, gain, packed))


def merge_grad_kernel(info, a0, a1, a2, a3, dlow, keep, send):
    per = a0.shape[0]
    width = a0.shape[1]
    me = info[0]
    for rel in range(4):
        pieces = [(a0[t], a1[t], a2[t], a3[t])[rel] for t in range(per)]
        left = jnp.concatenate(pieces, axis=1)
        rows = pl.ds(pl.multiple_of((me ^ rel) * width, 64), width)
        out = dot(left, dlow[...])
        for part in range(4):
            cols = out[:, width * part : width * (part + 1)]
            far = me ^ part

            @pl.when(far % 2 == 0)
            def _():
                keep[far // 2, rows, :] = cols

            @pl.when(far % 2 == 1)
            def _():
                send[far // 2, rows, :] = cols.astype(bf16)


def merge_grad(info, a0, a1, a2, a3, dlow):
    tok, d = dlow.shape
    args = (*in_hbm(a0, a1, a2, a3), dlow)
    shape = (2, d, d // 4)
    return kernel_call(
        merge_grad_kernel,
        (struct(shape, f32), struct(shape, bf16)),
        prefetch=1,
        ins=[whole(x.shape) for x in args],
        out_specs=(whole(shape), whole(shape)),
        flops=2 * tok * d * d,
        moved=4 * tok * d + 3 * d * d,
        vmem=20,
        name="merge_grad",
    )(info, *args)


def weight_kernel(na, nb, ga, gb, ha, dga, dua, hb, dgb, dub, out, nt):
    j = pl.program_id(0)
    tok, d = na.shape

    @pl.when(j == 0)
    def _():
        nt[:, :tok] = na[...].astype(f32).T.astype(bf16)
        nt[:, tok:] = nb[...].astype(f32).T.astype(bf16)

    for base, left, right in ((0, dga, dgb), (384, dua, dub)):
        grad = (dot(nt[:, :tok], left[...]) + dot(nt[:, tok:], right[...])).astype(bf16)
        for part in range(TILE // 128):
            at = pl.multiple_of(base + 48 * ((TILE // 128) * j + part), 16)
            out[:, pl.ds(at, 48), :] = grad[:, 128 * part : 128 * (part + 1)].reshape(FORM, 48, 128)
    grad = dot(ha[...].astype(f32).T.astype(bf16), ga[...]) + dot(hb[...].astype(f32).T.astype(bf16), gb[...])
    grad = grad.astype(bf16)
    for part in range(d // 128):
        low = 768 + 64 * part
        out[pl.ds(4 * j, 4), low : low + 64, :] = grad[:, 128 * part : 128 * (part + 1)].reshape(4, 64, 128)


def weight_grads(na, nb, ga, gb, left, right):
    tok, d = na.shape
    units = left[0].shape[1]
    args = (na, nb, ga, gb, *left, *right)
    col = pl.BlockSpec((tok, TILE), lambda j: (0, j))
    shape = (FORM, 1152, 128)
    return kernel_call(
        weight_kernel,
        struct(shape, bf16),
        grid=(units // TILE,),
        ins=[whole(x.shape) for x in args[:4]] + [col] * 6,
        out_specs=whole(shape),
        scratch=[pltpu.VMEM((d, 2 * tok), bf16)],
        flops=6 * 2 * tok * d * units,
        moved=12 * tok * units + 16 * tok * d,
        vmem=28,
        name="weight_grads",
    )(*args)


def regroup(stacked, parts, groups):
    count, _, width = stacked.shape
    if count == groups:
        return stacked
    pieces, low = [], 0
    for blocks, rows in parts:
        piece = stacked[:, low : low + blocks * rows].reshape(count, blocks, rows, width)
        low += blocks * rows
        piece = jnp.transpose(piece, (1, 0, 2, 3)).reshape(blocks, groups, count * rows // groups, width)
        pieces.append(jnp.transpose(piece, (1, 0, 2, 3)).reshape(groups, blocks * count * rows // groups, width))
    return jnp.concatenate(pieces, axis=1)


def to_blocks(mat, width):
    rows, cols = mat.shape
    return jnp.transpose(mat.reshape(rows, cols // width, width), (1, 0, 2)).reshape(-1, width)


def from_blocks(stacked, rows):
    blocks, width = stacked.shape[0] // rows, stacked.shape[1]
    return jnp.transpose(stacked.reshape(blocks, rows, width), (1, 0, 2)).reshape(rows, blocks * width)


def flip(x, bit):
    return lax.ppermute(x, ULY, [(i, i ^ bit) for i in range(4)])


def ordered(core, mine, theirs, axis):
    first = jnp.where(core == 0, mine, theirs)
    second = jnp.where(core == 0, theirs, mine)
    return jnp.concatenate([first, second], axis=axis)


def local(
    n_ctx,
    byte_embed,
    query_weight,
    key_weight,
    value_weight,
    merge_weight,
    gate_weight,
    up_weight,
    down_weight,
    conv_weight,
    score_weight,
    attn_gain,
    ffn_gain,
    bias_table,
    doc_lengths,
    rel_bucket,
    out_grad,
):
    nb, d = byte_embed.shape
    tok = out_grad.shape[0]
    n_dev = n_ctx * 4
    groups = n_ctx * 2
    rows_dev = query_weight.shape[0]
    rows_ctx = 4 * rows_dev
    down_dev = down_weight.shape[0]
    heads = HEADS // 4
    width = heads * HEAD_DIM
    group_len = tok * 4
    ext = 2 * group_len
    ff = gate_weight.shape[1]
    unit = ff // n_dev
    ctx_at = lax.axis_index("ctx")
    row_at = lax.axis_index("ux")
    core = lax.axis_index("uc")
    uly_at = lax.axis_index(ULY)
    dev_at = lax.axis_index(RING)
    me = uly_at.astype(jnp.int32).reshape(1)

    up_pairs = [(i, i + 1) for i in range(n_dev - 1)]
    down_pairs = [(i + 1, i) for i in range(n_dev - 1)]
    lo = lax.ppermute(byte_embed[nb - 8 :], RING, up_pairs)
    hi = lax.ppermute(byte_embed[:8], RING, down_pairs)

    count = doc_lengths.shape[0]
    order = lax.broadcasted_iota(jnp.int32, (count, count), 0)
    before = lax.broadcasted_iota(jnp.int32, (count, count), 1)
    starts = jnp.sum(jnp.where(before < order, doc_lengths[None, :], 0), axis=1)
    limit = jnp.sum(doc_lengths)

    shape = (nb + 16, 128)
    here = dev_at * nb - 8 + lax.broadcasted_iota(jnp.int32, shape, 0)
    there = here + lax.broadcasted_iota(jnp.int32, shape, 1) - 2
    between = jnp.sum(
        ((starts[None, None, :] <= here[:, :, None]) != (starts[None, None, :] <= there[:, :, None])).astype(jnp.int32),
        axis=2,
    )
    msk = ((between == 0) & (there >= 0) & (there < limit)).astype(f32)

    cw, sw = conv_weight, score_weight[None, :]
    gain_one, gain_two = attn_gain[None, :], ffn_gain[None, :]

    qkv_own = jnp.stack(
        [w.reshape(rows_dev, 4, width) for w in (query_weight, key_weight, value_weight)], axis=2
    ).reshape(rows_dev, 4, 3 * width)
    doubling = rows_ctx % 16 == 0
    take = lambda x, at, dim: lax.dynamic_index_in_dim(x, at, dim, keepdims=False)
    if doubling:
        cols = jnp.transpose(qkv_own, (1, 0, 2)).reshape(2, 2, rows_dev, 3 * width)
        got = flip(take(cols, 1 - core, 1), 1)
        cols = ordered(core, take(cols, core, 1), got, 1)
        got = flip(take(cols, 1 - row_at, 0), 2)
        qkv_w = ordered(row_at, take(cols, row_at, 0), got, 0)[None]
    else:
        qkv_send = jnp.broadcast_to(
            jnp.transpose(qkv_own, (1, 0, 2))[None], (n_ctx, 4, rows_dev, 3 * width)
        ).reshape(n_dev, rows_dev, 3 * width)
        qkv_w = lax.all_to_all(qkv_send, RING, 0, 0, tiled=True).reshape(8, d // 8, 3 * width)

    codes = [0]
    if doubling:
        bits_left = [1 << i for i in range(n_ctx.bit_length() - 1)][::-1]

        def double(qkv_w, bit):
            got = lax.ppermute(qkv_w, "ctx", [(i, i ^ bit) for i in range(n_ctx)])
            return jnp.concatenate([qkv_w, got], axis=0)

        qkv_w, lo, hi = lax.optimization_barrier((qkv_w, lo, hi))
        gbst, normed, conv, aw = gbst_forward(lo, byte_embed, hi, msk, cw, sw, gain_one)
        gate_in, up_in, merge_in = gate_weight, up_weight, merge_weight
        for i, bit in enumerate(bits_left):
            qkv_w = double(qkv_w, bit)
            codes = codes + [c ^ bit for c in codes]
            if i == 0:
                gate_in, up_in, merge_in, qkv_w, normed = lax.optimization_barrier(
                    (gate_in, up_in, merge_in, qkv_w, normed)
                )
        places = ctx_at ^ jnp.array(codes, jnp.int32)
    else:
        gbst, normed, conv, aw = gbst_forward(lo, byte_embed, hi, msk, cw, sw, gain_one)
        gate_in, up_in, merge_in = gate_weight, up_weight, merge_weight
        places = jnp.arange(8, dtype=jnp.int32)
    weight_info = jnp.concatenate([me, places.astype(jnp.int32)])
    chunk = jnp.concatenate([gate_in, up_in, merge_in], axis=1)
    chip = ordered(core, chunk, flip(chunk, 1), 0)

    def split(at):
        halves = [
            lax.dynamic_index_in_dim(
                chip[:, low : low + ff].reshape(2 * rows_dev, n_ctx, 2, 2 * unit), at, 2, keepdims=False
            ).reshape(2 * rows_dev, ff // 2)
            for low in (0, ff)
        ]
        return jnp.concatenate(halves + [chip[:, 2 * ff :]], axis=1)

    both = jnp.where(row_at == core, split(row_at), flip(split(1 - row_at), 2))
    packed_own = jnp.concatenate(
        [
            to_blocks(both[:, : ff // 2], TILE),
            to_blocks(both[:, ff // 2 : ff], TILE),
            to_blocks(down_weight, TILE),
            to_blocks(both[:, ff:], TILE),
        ],
        axis=0,
    )
    starts, limit, _ = lax.optimization_barrier((starts, limit, aw))

    tok_at = ctx_at * group_len - group_len // 2 + jnp.arange(ext, dtype=jnp.int32)
    tok_doc = jnp.sum((starts[None, :] <= 2 * tok_at[:, None]).astype(jnp.int32), axis=1) - 1
    tok_doc = jnp.where((tok_at >= 0) & (2 * tok_at < limit), tok_doc, -1)
    bits = count.bit_length()
    lane = jnp.arange(TILE, dtype=jnp.int32) - width

    def coded(docs, code, agree, value):
        bit_on = ((docs >> jnp.clip(code // 2, 0, 31)) & 1) == 1
        used = (code >= 0) & (code < 2 * bits)
        return jnp.where(used & ((bit_on == (code % 2 == 1)) == agree), value, 0.0).astype(bf16)

    code_k = coded(tok_doc[:, None], lane[None, :], True, 1.0)
    own_doc = tok_doc[group_len // 2 : group_len // 2 + group_len]
    code_q = coded(own_doc[:, None], lane[None, :], False, -BIG)
    tiles = group_len // TILE
    first = ctx_at * group_len + TILE * jnp.arange(tiles, dtype=jnp.int32)
    begin = jnp.max(jnp.where(starts[None, :] <= 2 * first[:, None], starts[None, :], 0), axis=1)
    last = 2 * (first + TILE - 1)
    end = jnp.min(jnp.where(starts[None, :] > last[:, None], starts[None, :], limit), axis=1)
    shift = group_len // 2 - ctx_at * group_len
    tile_lo = jnp.clip(((begin + 1) // 2 + shift) // TILE, 0, ext // TILE)
    tile_hi = jnp.clip(((end - 1) // 2 + shift) // TILE + 1, 0, ext // TILE)
    info = jnp.concatenate([tile_lo, tile_hi, me]).astype(jnp.int32)

    rel_count = rel_bucket.shape[0]
    diag_len = 2 * DOC_TOK + 2 * TILE
    bucket = jnp.pad(rel_bucket[::-1], (diag_len - TILE - rel_count, TILE), constant_values=-1)
    onehot = (bucket[None, :] == jnp.arange(NBUCK, dtype=jnp.int32)[:, None]).astype(f32)
    table_here = lax.dynamic_slice_in_dim(bias_table, uly_at * heads, heads, 1)
    diag = lax.dot_general(table_here, onehot, (((0,), (0,)), ((), ())), precision=highest)

    near = [(4 * c + u, 4 * (c + s) + u) for c in range(n_ctx) for u, s in ((0, -1), (1, -1), (2, 1), (3, 1)) if 0 <= c + s < n_ctx]
    far0 = lax.ppermute(normed, RING, near)
    own2 = flip(normed, 2)
    packed_own, qkv_w, far0, own2 = lax.optimization_barrier((packed_own, qkv_w, far0, own2))
    packed = lax.all_gather(packed_own, ("ctx", "uc"), axis=0, tiled=False)
    packed = packed.reshape(groups, packed_own.shape[0], TILE)
    packed = regroup(
        packed,
        ((4, 2 * rows_dev), (4, 2 * rows_dev), (3, down_dev), (3, 2 * rows_dev)),
        FORM,
    )


    own1 = flip(normed, 1)
    own3 = flip(own2, 1)
    far2 = flip(far0, 2)
    far1 = flip(far0, 1)
    far3 = flip(far2, 1)
    grad_in, far3 = lax.optimization_barrier((out_grad, far3))
    grad_other = flip(grad_in, 2)
    own = (normed, own1, own2, own3)
    far = (far0, far1, far2, far3)
    q, k, v, vt, wp = project(weight_info, own, far, qkv_w, code_q, code_k, heads)

    oa, ob, oloc, lse = attend(info, q, k, vt, diag, heads, tok)
    got2 = flip(ob, 2)
    got2, grad_other = lax.optimization_barrier((got2, grad_other))
    att = (oa[0], flip(oa[1], 1), got2[0], flip(got2[1], 1))
    mid, normed_two = merge(me, *att, packed, gbst, gain_two)

    normed_other = flip(normed_two, 2)
    out_a, dn_a, *left = feed(normed_two, out_grad, packed, ff // 2, f32)
    normed_other, dn_a = lax.optimization_barrier((normed_other, dn_a))
    out_b, dn_b, *right = feed(normed_other, grad_other, packed, ff // 2, bf16)
    dn_got = flip(dn_b, 2)
    grads = weight_grads(normed_two, normed_other, out_grad, grad_other, left, right)
    dn_got, grads = lax.optimization_barrier((dn_got, grads))
    parts16 = ((8, 48), (8, 48), (6, 64))
    grads = regroup(grads, parts16, groups)
    summed = lax.psum_scatter(grads, ("ctx", "uc"), scatter_dimension=0, tiled=False)
    dmid, dlow, ga, gb2, ffn_sum = middle(me, mid, dn_a, dn_got, out_grad, gain_two, packed)
    back2 = flip(gb2, 2)
    back1 = flip(ga[1], 1)
    back1, dlow = lax.optimization_barrier((back1, dlow))
    keep_m, send_m = merge_grad(me, *att, dlow)
    recv_m = flip(send_m, 1)
    back = (ga[0], back1, back2[0], flip(back2[1], 1))
    mid_m = (keep_m[1] + recv_m[1].astype(f32)).astype(bf16)

    out_b, mid_m, *back = lax.optimization_barrier((out_b, mid_m, *back))
    got_m = flip(mid_m, 2)
    out_got = flip(out_b, 2)
    dq, dk, dv, sums = attend_back(info, q, k, v, diag, oloc, lse, *back, heads)
    out_got, got_m, dk = lax.optimization_barrier((out_got, got_m, dk))
    layer_out = (mid + out_a + out_got.astype(f32)).astype(bf16)
    grad_info = jnp.concatenate([me, jnp.arange(8, dtype=jnp.int32)])
    hk0, hk2, hs1, hs3 = project_back(True, me, dq, dk, dv, wp)
    h_mid = (hk2 + flip(hs3, 1).astype(f32)).astype(bf16)
    h_mid, dq_g = lax.optimization_barrier((h_mid, dq))
    h_got2 = flip(h_mid, 2)
    part = project_grad(grad_info, own, far, dq_g, dk, dv, keep_m, recv_m, got_m, 8)
    dq_p, part, h_got2 = lax.optimization_barrier((dq_g, part, h_got2))
    ok0, ok2, os1, os3 = project_back(False, me, dq_p, dk, dv, wp)
    part = lax.psum_scatter(part.reshape(n_ctx, rows_ctx, 4 * width), "ctx", scatter_dimension=0, tiled=False)
    got = lax.all_to_all(part.reshape(4, rows_dev, 4 * width), ULY, 0, 0, tiled=True).astype(f32)
    h_got1 = flip(hs1, 1)
    o_got1 = flip(os1, 1)
    o_mid = (ok2 + flip(os3, 1).astype(f32)).astype(bf16)
    h_sum = (hk0 + h_got1.astype(f32) + h_got2.astype(f32)).astype(bf16)
    h_sum, o_mid = lax.optimization_barrier((h_sum, o_mid))
    h_back = lax.ppermute(h_sum, RING, [(b, a) for a, b in near])
    o_got2 = flip(o_mid, 2)
    o_sum = ok0 + o_got1.astype(f32) + o_got2.astype(f32)
    got = jnp.transpose(got.reshape(4, rows_dev, 4, width), (2, 1, 0, 3))
    query_grad, key_grad, value_grad, merge_g = (got[j].reshape(rows_dev, d) for j in range(4))

    sums, _ = lax.optimization_barrier((sums, h_sum))
    diag_parts = jnp.transpose(sums, (1, 0, 2))
    count_t = diag_parts.shape[1]
    low = diag_parts[:, :, :TILE].reshape(heads, count_t * TILE)
    high = diag_parts[:, :, TILE:].reshape(heads, count_t * TILE)
    diag_grad = jnp.pad(low, ((0, 0), (0, TILE))) + jnp.pad(high, ((0, 0), (TILE, 0)))
    table_local = lax.dot_general(onehot, diag_grad, (((1,), (1,)), ((), ())), precision=highest)
    table_grad = lax.dynamic_update_slice(jnp.zeros((NBUCK, HEADS), f32), table_local, (0, uly_at * heads))

    eg, small = gbst_backward(
        o_sum, h_back, gbst, dmid, gain_one, conv, aw, lo, byte_embed, hi, msk, cw, sw
    )
    from_prev = lax.ppermute(eg[nb + 8 :], RING, up_pairs)
    from_next = lax.ppermute(eg[:8], RING, down_pairs)
    main = eg[8 : nb + 8]
    embed_grad = jnp.concatenate(
        [main[:8] + from_prev, main[8 : nb - 8], main[nb - 8 :] + from_next], axis=0
    )

    rest = jnp.concatenate(
        [jnp.sum(ffn_sum, axis=0, keepdims=True), jnp.pad(table_grad.reshape(1, -1), ((0, 0), (0, d - NBUCK * HEADS)))],
        axis=0,
    )
    total = jnp.concatenate([small, jnp.pad(rest, ((0, 6), (0, 0)))], axis=0)
    for bit in (1, 2):
        total = total + flip(total, bit)
    bit = 1
    while bit < n_ctx:
        total = total + lax.ppermute(total, "ctx", [(i, i ^ bit) for i in range(n_ctx)])
        bit *= 2

    rows2 = 2 * rows_dev
    down_grad = from_blocks(summed[16 * rows2 :], down_dev).astype(f32)
    mine = jnp.concatenate(
        [from_blocks(summed[: 8 * rows2], rows2), from_blocks(summed[8 * rows2 : 16 * rows2], rows2)], axis=1
    )
    theirs = flip(mine, 2)
    sets = [jnp.where(row_at == at, mine, theirs).reshape(rows2, 2, n_ctx, 1, 2 * unit) for at in (0, 1)]
    full = jnp.concatenate(sets, axis=3).reshape(2, rows_dev, 2 * ff)
    given = flip(lax.dynamic_index_in_dim(full, 1 - core, 0, keepdims=False), 1)
    kept = lax.dynamic_index_in_dim(full, core, 0, keepdims=False)
    final = jnp.where(row_at == core, kept, given).astype(f32)
    return (
        layer_out,
        embed_grad,
        query_grad,
        key_grad,
        value_grad,
        merge_g,
        final[:, :ff],
        final[:, ff:],
        down_grad,
        total[:CONV],
        total[5],
        total[6],
        total[8],
        total[9, : NBUCK * HEADS].reshape(NBUCK, HEADS),
    )


def solution(mesh):
    n_ctx = mesh.shape["ctx"]
    inner = Mesh(mesh.devices.reshape(n_ctx, 2, 2), RING)
    row = P(RING, None)
    return jax.shard_map(
        partial(local, n_ctx),
        mesh=inner,
        in_specs=(row,) * 8 + (P(),) * 7 + (row,),
        out_specs=(row,) * 9 + (P(),) * 5,
        check_vma=False,
    )
```

time: 431 us -> 376 us (0.87)
  Pallas kernels: 179 us -> 130 us
  local copies, waits for them, and re-layouts: 49.4 us -> 40.8 us
  waiting for transfers between devices: 78 us -> 84 us
    all_to_all x2 -> x1, starting transfers between devices: 29.5 us -> 5.69 us  [local(): lax.all_to_all(part.reshape(4, rows_dev, 4 * width), ULY, 0, 0, tiled=True)]
    pallas_call x6 -> x5, Pallas kernels: 50.9 us -> 28.9 us  [the longest x2 12.6 us: feed(): kernel_call(feed_kernel, (struct((tok, d), kind), struct((tok, d), kind))...]
    ppermute x0 -> x3, waiting for transfers between devices: none -> 17.1 us  [double(): got = lax.ppermute(qkv_w, 'ctx', [(i, i ^ bit) for i in range(n_ctx)])]
    ppermute x25 -> x32, starting transfers between devices: 26.9 us -> 40.5 us  [flip(): return lax.ppermute(x, ULY, [(i, i ^ bit) for i in range(4)])]
    ppermute x25 -> x32, waiting for transfers between devices: 60.7 us -> 50.7 us  [flip(): return lax.ppermute(x, ULY, [(i, i ^ bit) for i in range(4)])]
    unnamed x84 -> x167, local copies, waits for them, and re-layouts: 10.3 us -> 19.3 us
    ppermute x1, waiting for transfers between devices: 11.4 us -> 3.78 us  [local(): h_back = lax.ppermute(h_sum, RING, [(b, a) for a, b in near])]
    pallas_call x1, Pallas kernels: 25.5 us -> 17.8 us  [attend(): kernel_call(partial(attend_kernel, heads), (struct(sent, bf16), struct(se...]
  transfers between devices with their start and end apart: 38 -> 48, of which waited for: 17 -> 19; matrix products, arithmetic and copies ran while one was open for 12% -> 12% of each run, Pallas kernels for 33% -> 32%
where the time goes in v1:
time: 376 us; the launch traced here: 372 us
  Pallas kernels  130 us (35%)
  waiting for transfers between devices  84 us (22%)
  starting transfers between devices  77 us (20%)
  local copies, waits for them, and re-layouts  40.8 us (11%)
  other arithmetic  24.2 us (6%)
  between operations  15.5 us (4%)
    ppermute x32, waiting for transfers between devices, flip(): return lax.ppermute(x, ULY, [(i, i ^ bit) for i in range(4)])  50.7 us
    ppermute x32, starting transfers between devices, flip(): return lax.ppermute(x, ULY, [(i, i ^ bit) for i in range(4)])  40.5 us
    pallas_call x1, Pallas kernels, attend_back(): kernel_call(partial(attend_back_kernel, heads), (struct((rows, TILE), bf1...  33.2 us
    unnamed x167, local copies, waits for them, and re-layouts  19.3 us
    pallas_call x1, Pallas kernels, attend(): kernel_call(partial(attend_kernel, heads), (struct(sent, bf16), struct(se...  17.8 us
    ppermute x3, waiting for transfers between devices, double(): got = lax.ppermute(qkv_w, 'ctx', [(i, i ^ bit) for i in range(n_ctx)])  17.1 us
    pallas_call x1, Pallas kernels, middle(): kernel_call(middle_kernel, tuple((struct(*s) for s in shapes)), prefetch=...  15.5 us
    pallas_call x1, Pallas kernels, gbst_backward(): kernel_call(gbst_backward_kernel, (struct((nb + 16, d), f32), struct((8,...  13.7 us
  transfers between devices with their start and end apart: 48, of which 19 were waited for; matrix products, arithmetic and copies ran while one was open for 12% of the time, Pallas kernels for 32%

profile of v1, /device:TPU:1, one launch (start us, length us, event | category | flops | bytes accessed | tf_op | source)
XLA Modules:
  0.0 372.1 jit_solution(4372293312658819875)
XLA Ops:
  11.0 4.5 %collective-permute-start.2 = (bf16[8,768]{1,0:T(8,128)(2,1)S(1)}, bf16[8,768]{1,0:T(8,128)(2,1)S(1)}, u32[]{:S(2)}, u32[]{:S(2)}) collective-permute-start(bf16[8,768]{1,0:T(8,128)(2,1)S(1)} %get-tuple-element.270), channel_id=1, source_target_pairs={{0,1},{1,2},{2,3},{3,4},{4,5},{5,6},{6,7},{7,8},{8,9},{9,10},{10,1... | collective-permute-start | bytes 36872 | tf_op jit(solution)/shard_map/ppermute | solution.py:1040
  25.3 7.0 %gbst_forward.1 = (f32[384,768]{1,0:T(8,128)S(1)}, bf16[384,768]{1,0:T(8,128)(2,1)S(1)}, f32[12,64,768]{2,1,0:T(8,128)S(1)}, f32[64,128]{1,0:T(8,128)S(1)}) custom-call(bf16[8,768]{1,0:T(8,128)(2,1)S(1)} %collective-permute-done.2.lo, bf16[768,768]{1,0:T(8,128)(2,1)S(1)} %copy-done.3, bf16[8,768]{1,0:T(8,128)(2,1)S(1)} %collective-permute-done.3.hi, ...), custom_call_target="tpu_custom_call" | custom-call | flops 35389440 | bytes 11796480 | tf_op jit(solution)/shard_map/gbst_forward/pallas_call | solution.py:179
  53.4 17.1 %collective-permute-done.9 = bf16[4,96,576]{2,1,0:T(8,128)(2,1)} collective-permute-done((bf16[4,96,576]{2,1,0:T(8,128)(2,1)S(1)}, bf16[4,96,576]{2,1,0:T(8,128)(2,1)}, u32[]{:S(2)}, u32[]{:S(2)}) %collective-permute-start.9) | collective-permute-done | bytes 442400 | tf_op jit(solution)/shard_map/ppermute | solution.py:1083
  77.9 9.5 %collective-permute-done.14.refs_6_ = bf16[384,768]{1,0:T(8,128)(2,1)S(1)} collective-permute-done((bf16[384,768]{1,0:T(8,128)(2,1)S(1)}, bf16[384,768]{1,0:T(8,128)(2,1)S(1)}, u32[]{:S(2)}, u32[]{:S(2)}) %collective-permute-start.14) | collective-permute-done | bytes 589856 | tf_op jit(solution)/shard_map/ppermute | solution.py:990
  91.6 4.2 %project.1 = (bf16[1536,256]{1,0:T(8,128)(2,1)S(1)}, bf16[3072,256]{1,0:T(8,128)(2,1)S(1)}, bf16[3072,256]{1,0:T(8,128)(2,1)S(1)}, bf16[256,3072]{1,0:T(8,128)(2,1)S(1)}, bf16[768,768]{1,0:T(8,128)(2,1)S(1)}) custom-call(s32[9]{0:T(128)S(1)} %pad_add_fusion.1.info, bf16[384,768]{1,0:T(8,128)(2,1)S(1)} %get-tuple-element.108.refs_0_, ...), custom_call_target="tpu_custom_call" | custom-call | flops 3623878656 | bytes 9043968 | tf_op jit(solution)/shard_map/project/pallas_call | solution.py:372
  95.9 17.8 %attend.1 = (bf16[2,3,192,128]{3,2,1,0:T(8,128)(2,1)S(1)}, bf16[2,3,192,128]{3,2,1,0:T(8,128)(2,1)S(1)}, bf16[192,1536]{1,0:T(8,128)(2,1)S(1)}, f32[6,8,768]{2,1,0:T(8,128)S(1)}) custom-call(s32[13]{0:T(128)S(1)} %pad_add_fusion.info, bf16[1536,256]{1,0:T(8,128)(2,1)S(1)} %get-tuple-element.117.q, bf16[3072,256]{1,0:T(8,128)(2,1)S(1)} %get-tuple-element.118.k, ...), custom_call_target="tpu_custom_call" | custom-call | flops 6039797760 | bytes 6291456 | tf_op jit(solution)/shard_map/attend/pallas_call | solution.py:581
  117.5 5.0 %collective-permute-done.17 = bf16[2,3,192,128]{3,2,1,0:T(8,128)(2,1)S(1)} collective-permute-done((bf16[2,3,192,128]{3,2,1,0:T(8,128)(2,1)S(1)}, bf16[2,3,192,128]{3,2,1,0:T(8,128)(2,1)S(1)}, u32[]{:S(2)}, u32[]{:S(2)}) %collective-permute-start.17) | collective-permute-done | bytes 294944 | tf_op jit(solution)/shard_map/ppermute | solution.py:990
  126.4 5.5 %all-gather.3.cloned.1.call-done = bf16[11520,256]{1,0:T(8,128)(2,1)} async-done(((bf16[720,256]{1,0:T(8,128)(2,1)}), bf16[11520,256]{1,0:T(8,128)(2,1)}) %all-gather.3.cloned.1.call-update) | async-done | bytes 5898256 | tf_op jit(solution)/shard_map/all_gather | solution.py:1161
  136.1 5.9 %feed.2 = (f32[384,768]{1,0:T(8,128)S(1)}, f32[384,768]{1,0:T(8,128)S(1)}, bf16[384,1024]{1,0:T(8,128)(2,1)S(1)}, bf16[384,1024]{1,0:T(8,128)(2,1)S(1)}, bf16[384,1024]{1,0:T(8,128)(2,1)S(1)}) custom-call(bf16[384,768]{1,0:T(8,128)(2,1)S(1)} %get-tuple-element.127.nt.na, bf16[384,768]{1,0:T(8,128)(2,1)S(1)} %copy-done.10, ...), custom_call_target="tpu_custom_call" | custom-call | flops 3623878656 | bytes 11206656 | tf_op jit(solution)/shard_map/feed/pallas_call | solution.py:817
  143.0 6.8 %collective-permute-done.20.nt.nb = bf16[384,768]{1,0:T(8,128)(2,1)S(1)} collective-permute-done((bf16[384,768]{1,0:T(8,128)(2,1)S(1)}, bf16[384,768]{1,0:T(8,128)(2,1)S(1)}, u32[]{:S(2)}, u32[]{:S(2)}) %collective-permute-start.20) | collective-permute-done | bytes 589856 | tf_op jit(solution)/shard_map/ppermute | solution.py:990
  149.8 6.7 %feed.3 = (bf16[384,768]{1,0:T(8,128)(2,1)}, bf16[384,768]{1,0:T(8,128)(2,1)}, bf16[384,1024]{1,0:T(8,128)(2,1)S(1)}, bf16[384,1024]{1,0:T(8,128)(2,1)S(1)}, bf16[384,1024]{1,0:T(8,128)(2,1)S(1)}) custom-call(bf16[384,768]{1,0:T(8,128)(2,1)S(1)} %collective-permute-done.20.nt.nb, bf16[384,768]{1,0:T(8,128)(2,1)S(1)} %copy-done.30, ...), custom_call_target="tpu_custom_call" | custom-call | flops 3623878656 | bytes 11206656 | tf_op jit(solution)/shard_map/feed/pallas_call | solution.py:817
  157.5 6.7 %weight_grads.1 = bf16[16,1152,128]{2,1,0:T(8,128)(2,1)S(1)} custom-call(bf16[384,768]{1,0:T(8,128)(2,1)S(1)} %get-tuple-element.127.nt.na, bf16[384,768]{1,0:T(8,128)(2,1)S(1)} %collective-permute-done.20.nt.nb, bf16[384,768]{1,0:T(8,128)(2,1)S(1)} %copy-done.10, bf16[384,768]{1,0:T(8,128)(2,1)S(1)} %copy-done.30, ...), custom_call_target="tpu_custom_call" | custom-call | flops 3623878656 | bytes 9437184 | tf_op jit(solution)/shard_map/weight_grads/pallas_call | solution.py:952
  166.4 4.1 %collective-permute-done.21.db = bf16[384,768]{1,0:T(8,128)(2,1)S(1)} collective-permute-done((bf16[384,768]{1,0:T(8,128)(2,1)}, bf16[384,768]{1,0:T(8,128)(2,1)S(1)}, u32[]{:S(2)}, u32[]{:S(2)}) %collective-permute-start.21) | collective-permute-done | bytes 589856 | tf_op jit(solution)/shard_map/ppermute | solution.py:990
  170.6 15.5 %middle.1 = (f32[384,768]{1,0:T(8,128)S(1)}, bf16[384,768]{1,0:T(8,128)(2,1)S(1)}, bf16[2,3,192,128]{3,2,1,0:T(8,128)(2,1)S(1)}, bf16[2,3,192,128]{3,2,1,0:T(8,128)(2,1)S(1)}, f32[8,768]{1,0:T(8,128)S(1)}) custom-call(s32[1]{0:T(128)} %bitcast.info.me, f32[384,768]{1,0:T(8,128)S(1)} %get-tuple-element.126.mid, f32[384,768]{1,0:T(8,128)S(1)} %get-tuple-element.133.da, ...), custom_call_target="tpu_custom_call" | custom-call | flops 452984832 | bytes 8847360 | tf_op jit(solution)/shard_map/middle/pallas_call | solution.py:873
  197.2 7.7 %collective-permute-done.24 = bf16[2,3,192,128]{3,2,1,0:T(8,128)(2,1)S(1)} collective-permute-done((bf16[2,3,192,128]{3,2,1,0:T(8,128)(2,1)}, bf16[2,3,192,128]{3,2,1,0:T(8,128)(2,1)S(1)}, u32[]{:S(2)}, u32[]{:S(2)}) %collective-permute-start.24) | collective-permute-done | bytes 294944 | tf_op jit(solution)/shard_map/ppermute | solution.py:990
  213.8 33.2 %attend_back.1 = (bf16[1536,256]{1,0:T(8,128)(2,1)S(1)}, bf16[3072,256]{1,0:T(8,128)(2,1)S(1)}, bf16[3072,256]{1,0:T(8,128)(2,1)S(1)}, f32[9,3,512]{2,1,0:T(4,128)S(1)}) custom-call(s32[13]{0:T(128)S(1)} %pad_add_fusion.info, bf16[1536,256]{1,0:T(8,128)(2,1)} %copy-done.54, bf16[3072,256]{1,0:T(8,128)(2,1)} %copy-done.52, bf16[3072,256]{1,0:T(8,128)(2,1)} %copy-done.53, ...), custom_call_target="tpu_custom_call" | custom-call | flops 15099494400 | bytes 12582912 | tf_op jit(solution)/shard_map/attend_back/pallas_call | solution.py:694
  254.9 8.4 %project_grad.1 = bf16[8,96,768]{2,1,0:T(8,128)(2,1)} custom-call(s32[9]{0:T(128)S(1)} %pad_add_fusion.2.info, bf16[384,768]{1,0:T(8,128)(2,1)} %copy-done.21, bf16[384,768]{1,0:T(8,128)(2,1)} %copy-done.25, bf16[384,768]{1,0:T(8,128)(2,1)} %copy-done.23, bf16[384,768]{1,0:T(8,128)(2,1)} %copy-done.27, bf16[384,768]{1,0:T(8,128)(2,1)} %copy-done.22, ...), custom_call_target="tpu_custom_call" | custom-call | flops 2717908992 | bytes 7077888 | tf_op jit(solution)/shard_map/project_grad/pallas_call | solution.py:456
  263.2 4.7 %collective-permute-done.29 = bf16[384,768]{1,0:T(8,128)(2,1)} collective-permute-done((bf16[384,768]{1,0:T(8,128)(2,1)}, bf16[384,768]{1,0:T(8,128)(2,1)}, u32[]{:S(2)}, u32[]{:S(2)}) %collective-permute-start.29) | collective-permute-done | bytes 589856 | tf_op jit(solution)/shard_map/ppermute | solution.py:990
  278.5 5.2 %collective-permute-start.34 = (bf16[384,768]{1,0:T(8,128)(2,1)}, bf16[384,768]{1,0:T(8,128)(2,1)S(1)}, u32[]{:S(2)}, u32[]{:S(2)}) collective-permute-start(bf16[384,768]{1,0:T(8,128)(2,1)} %add_convert_fusion.1), channel_id=1, source_target_pairs={{6,2},{7,3},{0,4},{1,5},{10,6},{11,7},{4,8},{5,9},{14,10},{15,11},... | collective-permute-start | bytes 1769480 | tf_op jit(solution)/shard_map/ppermute | solution.py:1227
  284.6 7.7 %collective-permute-done.33 = bf16[384,768]{1,0:T(8,128)(2,1)} collective-permute-done((bf16[384,768]{1,0:T(8,128)(2,1)}, bf16[384,768]{1,0:T(8,128)(2,1)}, u32[]{:S(2)}, u32[]{:S(2)}) %collective-permute-start.33) | collective-permute-done | bytes 589856 | tf_op jit(solution)/shard_map/ppermute | solution.py:990
  293.7 3.8 %collective-permute-done.34.recv = bf16[384,768]{1,0:T(8,128)(2,1)S(1)} collective-permute-done((bf16[384,768]{1,0:T(8,128)(2,1)}, bf16[384,768]{1,0:T(8,128)(2,1)S(1)}, u32[]{:S(2)}, u32[]{:S(2)}) %collective-permute-start.34) | collective-permute-done | bytes 589856 | tf_op jit(solution)/shard_map/ppermute | solution.py:1227
  297.5 13.7 %gbst_backward.1 = (f32[784,768]{1,0:T(8,128)S(1)}, f32[8,768]{1,0:T(8,128)S(1)}) custom-call(f32[384,768]{1,0:T(8,128)S(1)} %convert_add_fusion.keep, bf16[384,768]{1,0:T(8,128)(2,1)S(1)} %collective-permute-done.34.recv, f32[384,768]{1,0:T(8,128)} %copy-done.4, f32[384,768]{1,0:T(8,128)} %copy-done.14, f32[1,768]{1,0:T(1,128)} %copy-done.40, ...), custom_call_target="tpu_custom_call" | custom-call | flops 70778880 | bytes 14155776 | tf_op jit(solution)/shard_map/gbst_backward/pallas_call | solution.py:315
  317.7 9.7 %collective-permute-start.40 = (f32[16,768]{1,0:T(8,128)S(1)}, f32[16,768]{1,0:T(8,128)S(1)}, u32[]{:S(2)}, u32[]{:S(2)}) collective-permute-start(f32[16,768]{1,0:T(8,128)S(1)} %fusion.33), channel_id=1, source_target_pairs={{0,2},{1,3},{2,0},{3,1},{4,6},{5,7},{6,4},{7,5},{8,10},{9,11},{10,... | collective-permute-start | bytes 147464 | tf_op jit(solution)/shard_map/ppermute | solution.py:990
  348.6 5.7 %all-to-all-start = ((bf16[4,24,768]{2,1,0:T(8,128)(2,1)}), bf16[4,24,768]{2,1,0:T(8,128)(2,1)S(1)}, u32[]{:S(2)}, u32[]{:S(2)}) async-start(bf16[4,24,768]{2,1,0:T(8,128)(2,1)} %bitcast.142), calls=%async_computation.1 | async-start | bytes 294912 | tf_op jit(solution)/shard_map/all_to_all | solution.py:1221
  (374 shorter events, 140.4 us)
Async XLA Ops:
  7.2 124.7 %all-gather.3.cloned.1.call-start = ((), (), s32[]{:S(2)}) async-start(), calls=%async_computation.5 | async-start | bytes 6266880 | tf_op jit(solution)/shard_map/all_gather | solution.py:1161
  11.0 11.0 %collective-permute-start.2 = (bf16[8,768]{1,0:T(8,128)(2,1)S(1)}, bf16[8,768]{1,0:T(8,128)(2,1)S(1)}, u32[]{:S(2)}, u32[]{:S(2)}) collective-permute-start(bf16[8,768]{1,0:T(8,128)(2,1)S(1)} %get-tuple-element.270), channel_id=1, source_target_pairs={{0,1},{1,2},{2,3},{3,4},{4,5},{5,6},{6,7},{7,8},{8,9},{9,10},{10,1... | collective-permute-start | bytes 36872 | tf_op jit(solution)/shard_map/ppermute | solution.py:1040
  22.0 12.7 %collective-permute-start.4 = (bf16[1,96,576]{2,1,0:T(8,128)(2,1)S(1)}, bf16[1,96,576]{2,1,0:T(8,128)(2,1)S(1)}, u32[]{:S(2)}, u32[]{:S(2)}) collective-permute-start(bf16[1,96,576]{2,1,0:T(8,128)(2,1)S(1)} %maximum_bitcast_fusion), channel_id=1, source_target_pairs={{0,16},{4,20},{8,24},{12,28},{16,0},{20,4},{24,8},{28,12},{1,17},{... | collective-permute-start | bytes 331784 | tf_op jit(solution)/shard_map/ppermute | solution.py:1083
  43.7 28.0 %collective-permute-start.10 = (bf16[384,768]{1,0:T(8,128)(2,1)S(1)}, bf16[384,768]{1,0:T(8,128)(2,1)S(1)}, u32[]{:S(2)}, u32[]{:S(2)}) collective-permute-start(bf16[384,768]{1,0:T(8,128)(2,1)S(1)} %get-tuple-element.108.refs_0_), channel_id=1, source_target_pairs={{2,6},{3,7},{4,0},{5,1},{6,10},{7,11},{8,4},{9,5},{10,14},{11,15},... | collective-permute-start | bytes 1769480 | tf_op jit(solution)/shard_map/ppermute | solution.py:1158
  45.0 26.7 %collective-permute-start.11 = (bf16[384,768]{1,0:T(8,128)(2,1)S(1)}, bf16[384,768]{1,0:T(8,128)(2,1)S(1)}, u32[]{:S(2)}, u32[]{:S(2)}) collective-permute-start(bf16[384,768]{1,0:T(8,128)(2,1)S(1)} %get-tuple-element.108.refs_0_), channel_id=1, source_target_pairs={{0,2},{1,3},{2,0},{3,1},{4,6},{5,7},{6,4},{7,5},{8,10},{9,11},{10,... | collective-permute-start | bytes 1769480 | tf_op jit(solution)/shard_map/ppermute | solution.py:990
  47.2 23.2 %collective-permute-start.9 = (bf16[4,96,576]{2,1,0:T(8,128)(2,1)S(1)}, bf16[4,96,576]{2,1,0:T(8,128)(2,1)}, u32[]{:S(2)}, u32[]{:S(2)}) collective-permute-start(bf16[4,96,576]{2,1,0:T(8,128)(2,1)S(1)} %pad_maximum_fusion.2), channel_id=1, source_target_pairs={{0,4},{4,0},{8,12},{12,8},{16,20},{20,16},{24,28},{28,24},{1,5},{5... | collective-permute-start | bytes 1327112 | tf_op jit(solution)/shard_map/ppermute | solution.py:1083
  71.7 274.8 %reduce-scatter.5.cloned.1.call-start = ((), (), s32[]{:S(2)}) async-start(), calls=%async_computation.4 | async-start | bytes 5013504 | tf_op jit(solution)/shard_map/reduce_scatter | solution.py:1196
  74.1 13.4 %collective-permute-start.14 = (bf16[384,768]{1,0:T(8,128)(2,1)S(1)}, bf16[384,768]{1,0:T(8,128)(2,1)S(1)}, u32[]{:S(2)}, u32[]{:S(2)}) collective-permute-start(bf16[384,768]{1,0:T(8,128)(2,1)S(1)} %collective-permute-done.10.refs_4_), channel_id=1, source_target_pairs={{0,2},{1,3},{2,0},{3,1},{4,6},{5,7},{6,4},{7,5},{8,10},{9,11},{10,... | collective-permute-start | bytes 1769480 | tf_op jit(solution)/shard_map/ppermute | solution.py:990
  75.9 15.7 %collective-permute-start.5 = (bf16[384,768]{1,0:T(8,128)(2,1)S(1)}, bf16[384,768]{1,0:T(8,128)(2,1)S(1)}, u32[]{:S(2)}, u32[]{:S(2)}) collective-permute-start(bf16[384,768]{1,0:T(8,128)(2,1)S(1)} %get-tuple-element.108.refs_0_), channel_id=1, source_target_pairs={{0,1},{1,0},{2,3},{3,2},{4,5},{5,4},{6,7},{7,6},{8,9},{9,8},{10,11... | collective-permute-start | bytes 1769480 | tf_op jit(solution)/shard_map/ppermute | solution.py:990
  77.4 14.1 %collective-permute-start.13 = (bf16[384,768]{1,0:T(8,128)(2,1)S(1)}, bf16[384,768]{1,0:T(8,128)(2,1)S(1)}, u32[]{:S(2)}, u32[]{:S(2)}) collective-permute-start(bf16[384,768]{1,0:T(8,128)(2,1)S(1)} %collective-permute-done.10.refs_4_), channel_id=1, source_target_pairs={{0,1},{1,0},{2,3},{3,2},{4,5},{5,4},{6,7},{7,6},{8,9},{9,8},{10,11... | collective-permute-start | bytes 1769480 | tf_op jit(solution)/shard_map/ppermute | solution.py:990
  77.5 14.0 %collective-permute-start.12 = (bf16[384,768]{1,0:T(8,128)(2,1)S(1)}, bf16[384,768]{1,0:T(8,128)(2,1)S(1)}, u32[]{:S(2)}, u32[]{:S(2)}) collective-permute-start(bf16[384,768]{1,0:T(8,128)(2,1)S(1)} %collective-permute-done.11.refs_2_), channel_id=1, source_target_pairs={{0,1},{1,0},{2,3},{3,2},{4,5},{5,4},{6,7},{7,6},{8,9},{9,8},{10,11... | collective-permute-start | bytes 1769480 | tf_op jit(solution)/shard_map/ppermute | solution.py:990
  91.5 31.0 %collective-permute-start.18 = (bf16[384,768]{1,0:T(8,128)(2,1)S(1)}, bf16[384,768]{1,0:T(8,128)(2,1)S(1)}, u32[]{:S(2)}, u32[]{:S(2)}) collective-permute-start(bf16[384,768]{1,0:T(8,128)(2,1)S(1)} %copy-done.10), channel_id=1, source_target_pairs={{0,2},{1,3},{2,0},{3,1},{4,6},{5,7},{6,4},{7,5},{8,10},{9,11},{10,... | collective-permute-start | bytes 1769480 | tf_op jit(solution)/shard_map/ppermute | solution.py:990
  135.0 14.8 %collective-permute-start.20 = (bf16[384,768]{1,0:T(8,128)(2,1)S(1)}, bf16[384,768]{1,0:T(8,128)(2,1)S(1)}, u32[]{:S(2)}, u32[]{:S(2)}) collective-permute-start(bf16[384,768]{1,0:T(8,128)(2,1)S(1)} %get-tuple-element.127.nt.na), channel_id=1, source_target_pairs={{0,2},{1,3},{2,0},{3,1},{4,6},{5,7},{6,4},{7,5},{8,10},{9,11},{10,... | collective-permute-start | bytes 1769480 | tf_op jit(solution)/shard_map/ppermute | solution.py:990
  156.5 14.0 %collective-permute-start.21 = (bf16[384,768]{1,0:T(8,128)(2,1)}, bf16[384,768]{1,0:T(8,128)(2,1)S(1)}, u32[]{:S(2)}, u32[]{:S(2)}) collective-permute-start(bf16[384,768]{1,0:T(8,128)(2,1)} %get-tuple-element.134), channel_id=1, source_target_pairs={{0,2},{1,3},{2,0},{3,1},{4,6},{5,7},{6,4},{7,5},{8,10},{9,11},{10,... | collective-permute-start | bytes 1769480 | tf_op jit(solution)/shard_map/ppermute | solution.py:990
  170.5 178.0 %reduce-scatter.3.cloned.1.call-start = ((), (), s32[]{:S(2)}) async-start(), calls=%async_computation.3 | async-start | bytes 1327104 | tf_op jit(solution)/shard_map/reduce_scatter | solution.py:1220
  209.6 37.4 %collective-permute-start.26 = (bf16[384,768]{1,0:T(8,128)(2,1)}, bf16[384,768]{1,0:T(8,128)(2,1)S(1)}, u32[]{:S(2)}, u32[]{:S(2)}) collective-permute-start(bf16[384,768]{1,0:T(8,128)(2,1)} %get-tuple-element.149), channel_id=1, source_target_pairs={{0,2},{1,3},{2,0},{3,1},{4,6},{5,7},{6,4},{7,5},{8,10},{9,11},{10,... | collective-permute-start | bytes 1769480 | tf_op jit(solution)/shard_map/ppermute | solution.py:990
  210.6 36.4 %collective-permute-start.27 = (bf16[768,192]{1,0:T(8,128)(2,1)S(1)}, bf16[768,192]{1,0:T(8,128)(2,1)S(1)}, u32[]{:S(2)}, u32[]{:S(2)}) collective-permute-start(bf16[768,192]{1,0:T(8,128)(2,1)S(1)} %fusion.7), channel_id=1, source_target_pairs={{0,2},{1,3},{2,0},{3,1},{4,6},{5,7},{6,4},{7,5},{8,10},{9,11},{10,... | collective-permute-start | bytes 884744 | tf_op jit(solution)/shard_map/ppermute | solution.py:990
  253.1 14.9 %collective-permute-start.29 = (bf16[384,768]{1,0:T(8,128)(2,1)}, bf16[384,768]{1,0:T(8,128)(2,1)}, u32[]{:S(2)}, u32[]{:S(2)}) collective-permute-start(bf16[384,768]{1,0:T(8,128)(2,1)} %add_convert_fusion.2), channel_id=1, source_target_pairs={{0,2},{1,3},{2,0},{3,1},{4,6},{5,7},{6,4},{7,5},{8,10},{9,11},{10,... | collective-permute-start | bytes 1769480 | tf_op jit(solution)/shard_map/ppermute | solution.py:990
  254.2 19.9 %collective-permute-start.31 = (bf16[384,768]{1,0:T(8,128)(2,1)}, bf16[384,768]{1,0:T(8,128)(2,1)}, u32[]{:S(2)}, u32[]{:S(2)}) collective-permute-start(bf16[384,768]{1,0:T(8,128)(2,1)} %get-tuple-element.173), channel_id=1, source_target_pairs={{0,1},{1,0},{2,3},{3,2},{4,5},{5,4},{6,7},{7,6},{8,9},{9,8},{10,11... | collective-permute-start | bytes 1769480 | tf_op jit(solution)/shard_map/ppermute | solution.py:990
  277.4 14.8 %collective-permute-start.33 = (bf16[384,768]{1,0:T(8,128)(2,1)}, bf16[384,768]{1,0:T(8,128)(2,1)}, u32[]{:S(2)}, u32[]{:S(2)}) collective-permute-start(bf16[384,768]{1,0:T(8,128)(2,1)} %add_convert_fusion), channel_id=1, source_target_pairs={{0,2},{1,3},{2,0},{3,1},{4,6},{5,7},{6,4},{7,5},{8,10},{9,11},{10,... | collective-permute-start | bytes 1769480 | tf_op jit(solution)/shard_map/ppermute | solution.py:990
  278.5 19.0 %collective-permute-start.34 = (bf16[384,768]{1,0:T(8,128)(2,1)}, bf16[384,768]{1,0:T(8,128)(2,1)S(1)}, u32[]{:S(2)}, u32[]{:S(2)}) collective-permute-start(bf16[384,768]{1,0:T(8,128)(2,1)} %add_convert_fusion.1), channel_id=1, source_target_pairs={{6,2},{7,3},{0,4},{1,5},{10,6},{11,7},{4,8},{5,9},{14,10},{15,11},... | collective-permute-start | bytes 1769480 | tf_op jit(solution)/shard_map/ppermute | solution.py:1227
  315.5 11.9 %collective-permute-start.35 = (f32[8,768]{1,0:T(8,128)S(1)}, f32[8,768]{1,0:T(8,128)S(1)}, u32[]{:S(2)}, u32[]{:S(2)}) collective-permute-start(f32[8,768]{1,0:T(8,128)S(1)} %slice.150), channel_id=1, source_target_pairs={{0,1},{1,2},{2,3},{3,4},{4,5},{5,6},{6,7},{7,8},{8,9},{9,10},{10,1... | collective-permute-start | bytes 73736 | tf_op jit(solution)/shard_map/ppermute | solution.py:1245
  317.7 12.6 %collective-permute-start.40 = (f32[16,768]{1,0:T(8,128)S(1)}, f32[16,768]{1,0:T(8,128)S(1)}, u32[]{:S(2)}, u32[]{:S(2)}) collective-permute-start(f32[16,768]{1,0:T(8,128)S(1)} %fusion.33), channel_id=1, source_target_pairs={{0,2},{1,3},{2,0},{3,1},{4,6},{5,7},{6,4},{7,5},{8,10},{9,11},{10,... | collective-permute-start | bytes 147464 | tf_op jit(solution)/shard_map/ppermute | solution.py:990
  328.1 11.5 %collective-permute-start.36 = (f32[8,768]{1,0:T(8,128)S(1)}, f32[8,768]{1,0:T(8,128)S(1)}, u32[]{:S(2)}, u32[]{:S(2)}) collective-permute-start(f32[8,768]{1,0:T(8,128)S(1)} %get-tuple-element.268), channel_id=1, source_target_pairs={{1,0},{2,1},{3,2},{4,3},{5,4},{6,5},{7,6},{8,7},{9,8},{10,9},{11,1... | collective-permute-start | bytes 73736 | tf_op jit(solution)/shard_map/ppermute | solution.py:1246
  (101 other events, 1002.4 us)
Sparse Core Ops, SparseCore 0:
  71.8 60.0 all-gather.2
  170.7 74.2 reduce-scatter.4
  278.6 64.1 reduce-scatter.2

commit v2 on v1

--- a/solution.py
+++ b/solution.py
@@ -46,7 +46,7 @@
             scratch_shapes=list(scratch),
         ),
         compiler_params=params,
-        cost_estimate=pl.CostEstimate(flops=int(flops), bytes_accessed=int(moved), transcendentals=0),
+        cost_estimate=pl.CostEstimate(flops=int(flops) // 8, bytes_accessed=int(moved) // 8, transcendentals=0),
         name=name,
     )
 
@@ -467,6 +467,27 @@
     )(info, *args)
 
 
+def spread_kernel(got, *outs):
+    width = got.shape[2] // 4
+    for j, out in enumerate(outs):
+        for u in range(4):
+            out[:, width * u : width * (u + 1)] = got[u, :, width * j : width * (j + 1)].astype(f32)
+
+
+def spread(got):
+    _, rows, d = got.shape
+    return kernel_call(
+        spread_kernel,
+        (struct((rows, d), f32),) * 4,
+        ins=[whole(got.shape)],
+        out_specs=(whole((rows, d)),) * 4,
+        flops=8 * 10**11,
+        moved=24 * rows * d,
+        vmem=8,
+        name="spread",
+    )(got)
+
+
 def fill_bias(diag, bias):
     count = bias.shape[0]
     heads = diag.shape[0]
@@ -483,7 +504,7 @@
 
 
 def sum_diagonals(tiles, out):
-    count, heads, _ = out.shape
+    count, heads, _, _ = out.shape
 
     def tile(t, _):
         for h in range(heads):
@@ -493,10 +514,7 @@
             while rows > 8:
                 rows //= 2
                 cur = cur[:rows] + pltpu.roll(cur[rows:], 2 * TILE - rows, axis=1)
-            total = cur[0:1]
-            for i in range(1, 8):
-                total = total + pltpu.roll(cur[i : i + 1], 2 * TILE - i, axis=1)
-            out[count - 1 - t, h : h + 1, :] = pltpu.roll(total, TILE, axis=1)
+            out[count - 1 - t, h] = cur
         return 0
 
     lax.fori_loop(0, count, tile, 0)
@@ -690,7 +708,7 @@
     width = heads * HEAD_DIM
     tile = pl.BlockSpec((TILE, TILE), lambda i, *_: (i, 0))
     turned = pl.BlockSpec((width, TILE), lambda i, *_: (0, i))
-    sums = (9, heads, 2 * TILE)
+    sums = (9, heads, 8, 2 * TILE)
     return kernel_call(
         partial(attend_back_kernel, heads),
         (
@@ -1083,11 +1101,11 @@
             got = lax.ppermute(qkv_w, "ctx", [(i, i ^ bit) for i in range(n_ctx)])
             return jnp.concatenate([qkv_w, got], axis=0)
 
-        qkv_w, lo, hi = lax.optimization_barrier((qkv_w, lo, hi))
         gbst, normed, conv, aw = gbst_forward(lo, byte_embed, hi, msk, cw, sw, gain_one)
         gate_in, up_in, merge_in = gate_weight, up_weight, merge_weight
         for i, bit in enumerate(bits_left):
-            qkv_w = double(qkv_w, bit)
+            if i < len(bits_left) - 1:
+                qkv_w = double(qkv_w, bit)
             codes = codes + [c ^ bit for c in codes]
             if i == 0:
                 gate_in, up_in, merge_in, qkv_w, normed = lax.optimization_barrier(
@@ -1157,7 +1175,7 @@
     near = [(4 * c + u, 4 * (c + s) + u) for c in range(n_ctx) for u, s in ((0, -1), (1, -1), (2, 1), (3, 1)) if 0 <= c + s < n_ctx]
     far0 = lax.ppermute(normed, RING, near)
     own2 = flip(normed, 2)
-    packed_own, qkv_w, far0, own2 = lax.optimization_barrier((packed_own, qkv_w, far0, own2))
+    packed_own, far0, own2, qkv_w = lax.optimization_barrier((packed_own, far0, own2, qkv_w))
     packed = lax.all_gather(packed_own, ("ctx", "uc"), axis=0, tiled=False)
     packed = packed.reshape(groups, packed_own.shape[0], TILE)
     packed = regroup(
@@ -1174,6 +1192,10 @@
     far3 = flip(far2, 1)
     grad_in, far3 = lax.optimization_barrier((out_grad, far3))
     grad_other = flip(grad_in, 2)
+    if doubling:
+        qkv_got = lax.ppermute(qkv_w, "ctx", [(i, i ^ bits_left[-1]) for i in range(n_ctx)])
+        qkv_got, far2 = lax.optimization_barrier((qkv_got, far2))
+        qkv_w = jnp.concatenate([qkv_w, qkv_got], axis=0)
     own = (normed, own1, own2, own3)
     far = (far0, far1, far2, far3)
     q, k, v, vt, wp = project(weight_info, own, far, qkv_w, code_q, code_k, heads)
@@ -1215,10 +1237,10 @@
     h_mid, dq_g = lax.optimization_barrier((h_mid, dq))
     h_got2 = flip(h_mid, 2)
     part = project_grad(grad_info, own, far, dq_g, dk, dv, keep_m, recv_m, got_m, 8)
-    dq_p, part, h_got2 = lax.optimization_barrier((dq_g, part, h_got2))
+    dq_p, part, h_got2, summed = lax.optimization_barrier((dq_g, part, h_got2, summed))
     ok0, ok2, os1, os3 = project_back(False, me, dq_p, dk, dv, wp)
     part = lax.psum_scatter(part.reshape(n_ctx, rows_ctx, 4 * width), "ctx", scatter_dimension=0, tiled=False)
-    got = lax.all_to_all(part.reshape(4, rows_dev, 4 * width), ULY, 0, 0, tiled=True).astype(f32)
+    got = lax.all_to_all(part.reshape(4, rows_dev, 4 * width), ULY, 0, 0, tiled=True)
     h_got1 = flip(hs1, 1)
     o_got1 = flip(os1, 1)
     o_mid = (ok2 + flip(os3, 1).astype(f32)).astype(bf16)
@@ -1227,11 +1249,11 @@
     h_back = lax.ppermute(h_sum, RING, [(b, a) for a, b in near])
     o_got2 = flip(o_mid, 2)
     o_sum = ok0 + o_got1.astype(f32) + o_got2.astype(f32)
-    got = jnp.transpose(got.reshape(4, rows_dev, 4, width), (2, 1, 0, 3))
-    query_grad, key_grad, value_grad, merge_g = (got[j].reshape(rows_dev, d) for j in range(4))
 
     sums, _ = lax.optimization_barrier((sums, h_sum))
-    diag_parts = jnp.transpose(sums, (1, 0, 2))
+    twice = jnp.concatenate([sums, sums], axis=3)
+    moved = sum(twice[:, :, r, r + TILE : r + 3 * TILE] for r in range(8))
+    diag_parts = jnp.transpose(moved, (1, 0, 2))
     count_t = diag_parts.shape[1]
     low = diag_parts[:, :, :TILE].reshape(heads, count_t * TILE)
     high = diag_parts[:, :, TILE:].reshape(heads, count_t * TILE)
@@ -1260,6 +1282,9 @@
     while bit < n_ctx:
         total = total + lax.ppermute(total, "ctx", [(i, i ^ bit) for i in range(n_ctx)])
         bit *= 2
+
+    got, total = lax.optimization_barrier((got, total))
+    query_grad, key_grad, value_grad, merge_g = spread(got)
 
     rows2 = 2 * rows_dev
     down_grad = from_blocks(summed[16 * rows2 :], down_dev).astype(f32)

time: 376 us -> 366 us (0.973)
  Pallas kernels: 130 us -> 117 us
  starting transfers between devices: 77 us -> 81.7 us
    ppermute x3 -> x2, waiting for transfers between devices: 17.1 us -> 0.01 us  [double(): got = lax.ppermute(qkv_w, 'ctx', [(i, i ^ bit) for i in range(n_ctx)])]
    ppermute x0 -> x1, waiting for transfers between devices: none -> 12.7 us  [local(): lax.ppermute(qkv_w, 'ctx', [(i, i ^ bits_left[-1]) for i in range(n_ctx)])]
    ppermute x32, starting transfers between devices: 40.5 us -> 29.3 us  [flip(): return lax.ppermute(x, ULY, [(i, i ^ bit) for i in range(4)])]
    reduce_scatter x1, starting transfers between devices: 0.04 us -> 10.9 us  [local(): lax.psum_scatter(part.reshape(n_ctx, rows_ctx, 4 * width), 'ctx', scatter...]
    pallas_call x1, Pallas kernels: 15.5 us -> 5.09 us  [middle(): kernel_call(middle_kernel, tuple((struct(*s) for s in shapes)), prefetch=...]
    ppermute x1, waiting for transfers between devices: 0.01 us -> 6.46 us  [local(): far0 = lax.ppermute(normed, RING, near)]
    all_gather x1, waiting for transfers between devices: 5.54 us -> 0.01 us  [local(): packed = lax.all_gather(packed_own, ('ctx', 'uc'), axis=0, tiled=False)]
    unnamed x167 -> x165, local copies, waits for them, and re-layouts: 19.3 us -> 20.3 us
  transfers between devices with their start and end apart: 48 -> 48, of which waited for: 19 -> 20; matrix products, arithmetic and copies ran while one was open for 12% -> 12% of each run, Pallas kernels for 32% -> 29%
where the time goes in v2:
time: 366 us; the launch traced here: 362 us
  Pallas kernels  117 us (32%)
  waiting for transfers between devices  84.3 us (23%)
  starting transfers between devices  81.7 us (22%)
  local copies, waits for them, and re-layouts  38.6 us (11%)
  other arithmetic  23.4 us (6%)
  between operations  15.6 us (4%)
    ppermute x32, waiting for transfers between devices, flip(): return lax.ppermute(x, ULY, [(i, i ^ bit) for i in range(4)])  52.9 us
    pallas_call x1, Pallas kernels, attend_back(): kernel_call(partial(attend_back_kernel, heads), (struct((rows, TILE), bf1...  31.2 us
    ppermute x32, starting transfers between devices, flip(): return lax.ppermute(x, ULY, [(i, i ^ bit) for i in range(4)])  29.3 us
    unnamed x165, local copies, waits for them, and re-layouts  20.3 us
    pallas_call x1, Pallas kernels, attend(): kernel_call(partial(attend_kernel, heads), (struct(sent, bf16), struct(se...  17.8 us
    pallas_call x1, Pallas kernels, gbst_backward(): kernel_call(gbst_backward_kernel, (struct((nb + 16, d), f32), struct((8,...  13.5 us
    ppermute x1, waiting for transfers between devices, local(): lax.ppermute(qkv_w, 'ctx', [(i, i ^ bits_left[-1]) for i in range(n_ctx)])  12.7 us
    pallas_call x2, Pallas kernels, feed(): kernel_call(feed_kernel, (struct((tok, d), kind), struct((tok, d), kind))...  12.6 us
  transfers between devices with their start and end apart: 48, of which 20 were waited for; matrix products, arithmetic and copies ran while one was open for 12% of the time, Pallas kernels for 29%

profile of v2, /device:TPU:1, one launch (start us, length us, event | category | flops | bytes accessed | tf_op | source)
XLA Modules:
  0.0 362.0 jit_solution(15854703184772232642)
XLA Ops:
  8.0 4.5 %collective-permute-start = (bf16[8,768]{1,0:T(8,128)(2,1)S(1)}, bf16[8,768]{1,0:T(8,128)(2,1)S(1)}, u32[]{:S(2)}, u32[]{:S(2)}) collective-permute-start(bf16[8,768]{1,0:T(8,128)(2,1)S(1)} %get-tuple-element.282), channel_id=1, source_target_pairs={{0,1},{1,2},{2,3},{3,4},{4,5},{5,6},{6,7},{7,8},{8,9},{9,10},{10,1... | collective-permute-start | bytes 36872 | tf_op jit(solution)/shard_map/ppermute | solution.py:1058
  28.0 7.0 %gbst_forward.1 = (f32[384,768]{1,0:T(8,128)S(1)}, bf16[384,768]{1,0:T(8,128)(2,1)S(1)}, f32[12,64,768]{2,1,0:T(8,128)S(1)}, f32[64,128]{1,0:T(8,128)S(1)}) custom-call(bf16[8,768]{1,0:T(8,128)(2,1)S(1)} %collective-permute-done.lo, bf16[768,768]{1,0:T(8,128)(2,1)S(1)} %copy-done.8, bf16[8,768]{1,0:T(8,128)(2,1)S(1)} %collective-permute-done.1.hi, ...), custom_call_target="tpu_custom_call" | custom-call | flops 4423680 | bytes 1474560 | tf_op jit(solution)/shard_map/gbst_forward/pallas_call | solution.py:179
  54.3 6.5 %collective-permute-done.8.refs_4_ = bf16[384,768]{1,0:T(8,128)(2,1)S(1)} collective-permute-done((bf16[384,768]{1,0:T(8,128)(2,1)S(1)}, bf16[384,768]{1,0:T(8,128)(2,1)S(1)}, u32[]{:S(2)}, u32[]{:S(2)}) %collective-permute-start.8) | collective-permute-done | bytes 589856 | tf_op jit(solution)/shard_map/ppermute | solution.py:1176
  60.7 4.0 %collective-permute-done.9.refs_2_ = bf16[384,768]{1,0:T(8,128)(2,1)S(1)} collective-permute-done((bf16[384,768]{1,0:T(8,128)(2,1)S(1)}, bf16[384,768]{1,0:T(8,128)(2,1)S(1)}, u32[]{:S(2)}, u32[]{:S(2)}) %collective-permute-start.9) | collective-permute-done | bytes 589856 | tf_op jit(solution)/shard_map/ppermute | solution.py:1008
  70.6 9.7 %collective-permute-done.14.refs_6_ = bf16[384,768]{1,0:T(8,128)(2,1)S(1)} collective-permute-done((bf16[384,768]{1,0:T(8,128)(2,1)S(1)}, bf16[384,768]{1,0:T(8,128)(2,1)S(1)}, u32[]{:S(2)}, u32[]{:S(2)}) %collective-permute-start.14) | collective-permute-done | bytes 589856 | tf_op jit(solution)/shard_map/ppermute | solution.py:1008
  84.7 12.7 %collective-permute-done.13 = bf16[4,96,576]{2,1,0:T(8,128)(2,1)S(1)} collective-permute-done((bf16[4,96,576]{2,1,0:T(8,128)(2,1)S(1)}, bf16[4,96,576]{2,1,0:T(8,128)(2,1)S(1)}, u32[]{:S(2)}, u32[]{:S(2)}) %collective-permute-start.13) | collective-permute-done | bytes 442400 | tf_op jit(solution)/shard_map/ppermute | solution.py:1196
  97.6 4.2 %project.1 = (bf16[1536,256]{1,0:T(8,128)(2,1)S(1)}, bf16[3072,256]{1,0:T(8,128)(2,1)S(1)}, bf16[3072,256]{1,0:T(8,128)(2,1)S(1)}, bf16[256,3072]{1,0:T(8,128)(2,1)S(1)}, bf16[768,768]{1,0:T(8,128)(2,1)S(1)}) custom-call(s32[9]{0:T(128)S(1)} %pad_add_fusion.1.info, bf16[384,768]{1,0:T(8,128)(2,1)S(1)} %get-tuple-element.111.refs_0_, ...), custom_call_target="tpu_custom_call" | custom-call | flops 452984832 | bytes 1130496 | tf_op jit(solution)/shard_map/project/pallas_call | solution.py:372
  103.1 17.8 %attend.1 = (bf16[2,3,192,128]{3,2,1,0:T(8,128)(2,1)S(1)}, bf16[2,3,192,128]{3,2,1,0:T(8,128)(2,1)S(1)}, bf16[192,1536]{1,0:T(8,128)(2,1)S(1)}, f32[6,8,768]{2,1,0:T(8,128)S(1)}) custom-call(s32[13]{0:T(128)S(1)} %pad_add_fusion.info, bf16[1536,256]{1,0:T(8,128)(2,1)S(1)} %get-tuple-element.122.q, bf16[3072,256]{1,0:T(8,128)(2,1)S(1)} %get-tuple-element.123.k, ...), custom_call_target="tpu_custom_call" | custom-call | flops 754974720 | bytes 786432 | tf_op jit(solution)/shard_map/attend/pallas_call | solution.py:599
  123.3 4.8 %collective-permute-done.17 = bf16[2,3,192,128]{3,2,1,0:T(8,128)(2,1)S(1)} collective-permute-done((bf16[2,3,192,128]{3,2,1,0:T(8,128)(2,1)S(1)}, bf16[2,3,192,128]{3,2,1,0:T(8,128)(2,1)S(1)}, u32[]{:S(2)}, u32[]{:S(2)}) %collective-permute-start.17) | collective-permute-done | bytes 294944 | tf_op jit(solution)/shard_map/ppermute | solution.py:1008
  136.5 5.9 %feed.2 = (f32[384,768]{1,0:T(8,128)S(1)}, f32[384,768]{1,0:T(8,128)S(1)}, bf16[384,1024]{1,0:T(8,128)(2,1)S(1)}, bf16[384,1024]{1,0:T(8,128)(2,1)S(1)}, bf16[384,1024]{1,0:T(8,128)(2,1)S(1)}) custom-call(bf16[384,768]{1,0:T(8,128)(2,1)S(1)} %get-tuple-element.132.nt.na, bf16[384,768]{1,0:T(8,128)(2,1)S(1)} %copy-done.7, ...), custom_call_target="tpu_custom_call" | custom-call | flops 452984832 | bytes 1400832 | tf_op jit(solution)/shard_map/feed/pallas_call | solution.py:835
  144.4 6.1 %collective-permute-done.20.nt.nb = bf16[384,768]{1,0:T(8,128)(2,1)S(1)} collective-permute-done((bf16[384,768]{1,0:T(8,128)(2,1)S(1)}, bf16[384,768]{1,0:T(8,128)(2,1)S(1)}, u32[]{:S(2)}, u32[]{:S(2)}) %collective-permute-start.20) | collective-permute-done | bytes 589856 | tf_op jit(solution)/shard_map/ppermute | solution.py:1008
  150.5 6.8 %feed.3 = (bf16[384,768]{1,0:T(8,128)(2,1)}, bf16[384,768]{1,0:T(8,128)(2,1)}, bf16[384,1024]{1,0:T(8,128)(2,1)S(1)}, bf16[384,1024]{1,0:T(8,128)(2,1)S(1)}, bf16[384,1024]{1,0:T(8,128)(2,1)S(1)}) custom-call(bf16[384,768]{1,0:T(8,128)(2,1)S(1)} %collective-permute-done.20.nt.nb, bf16[384,768]{1,0:T(8,128)(2,1)S(1)} %collective-permute-done.18.gr.gb, ...), custom_call_target="tpu_custom_call" | custom-call | flops 452984832 | bytes 1400832 | tf_op jit(solution)/shard_map/feed/pallas_call | solution.py:835
  157.3 6.7 %weight_grads.1 = bf16[16,1152,128]{2,1,0:T(8,128)(2,1)S(1)} custom-call(bf16[384,768]{1,0:T(8,128)(2,1)S(1)} %get-tuple-element.132.nt.na, bf16[384,768]{1,0:T(8,128)(2,1)S(1)} %collective-permute-done.20.nt.nb, bf16[384,768]{1,0:T(8,128)(2,1)S(1)} %copy-done.7, bf16[384,768]{1,0:T(8,128)(2,1)S(1)} %collective-permute-done.18.gr.gb, ...), custom_call_target="tpu_custom_call" | custom-call | flops 452984832 | bytes 1179648 | tf_op jit(solution)/shard_map/weight_grads/pallas_call | solution.py:970
  166.2 4.9 %collective-permute-done.21.db = bf16[384,768]{1,0:T(8,128)(2,1)S(1)} collective-permute-done((bf16[384,768]{1,0:T(8,128)(2,1)}, bf16[384,768]{1,0:T(8,128)(2,1)S(1)}, u32[]{:S(2)}, u32[]{:S(2)}) %collective-permute-start.21) | collective-permute-done | bytes 589856 | tf_op jit(solution)/shard_map/ppermute | solution.py:1008
  171.1 10.9 %reduce-scatter.5.cloned.1.call-start = ((), (), s32[]{:S(2)}) async-start(), calls=%async_computation.4 | async-start | bytes 1327104 | tf_op jit(solution)/shard_map/reduce_scatter | solution.py:1242
  182.1 5.1 %middle.1 = (f32[384,768]{1,0:T(8,128)S(1)}, bf16[384,768]{1,0:T(8,128)(2,1)S(1)}, bf16[2,3,192,128]{3,2,1,0:T(8,128)(2,1)S(1)}, bf16[2,3,192,128]{3,2,1,0:T(8,128)(2,1)S(1)}, f32[8,768]{1,0:T(8,128)S(1)}) custom-call(s32[1]{0:T(128)} %bitcast.info.me, f32[384,768]{1,0:T(8,128)S(1)} %get-tuple-element.131.mid, f32[384,768]{1,0:T(8,128)S(1)} %copy-done.38, ...), custom_call_target="tpu_custom_call" | custom-call | flops 56623104 | bytes 1105920 | tf_op jit(solution)/shard_map/middle/pallas_call | solution.py:891
  195.9 8.6 %collective-permute-done.24 = bf16[2,3,192,128]{3,2,1,0:T(8,128)(2,1)S(1)} collective-permute-done((bf16[2,3,192,128]{3,2,1,0:T(8,128)(2,1)}, bf16[2,3,192,128]{3,2,1,0:T(8,128)(2,1)S(1)}, u32[]{:S(2)}, u32[]{:S(2)}) %collective-permute-start.24) | collective-permute-done | bytes 294944 | tf_op jit(solution)/shard_map/ppermute | solution.py:1008
  210.7 31.2 %attend_back.1 = (bf16[1536,256]{1,0:T(8,128)(2,1)S(1)}, bf16[3072,256]{1,0:T(8,128)(2,1)S(1)}, bf16[3072,256]{1,0:T(8,128)(2,1)S(1)}, f32[9,3,8,512]{3,2,1,0:T(8,128)S(1)}) custom-call(s32[13]{0:T(128)S(1)} %pad_add_fusion.info, bf16[1536,256]{1,0:T(8,128)(2,1)} %copy-done.39, bf16[3072,256]{1,0:T(8,128)(2,1)} %copy-done.28, bf16[3072,256]{1,0:T(8,128)(2,1)} %copy-done.49, ...), custom_call_target="tpu_custom_call" | custom-call | flops 1887436800 | bytes 1572864 | tf_op jit(solution)/shard_map/attend_back/pallas_call | solution.py:712
  251.5 7.4 %project_grad.1 = bf16[8,96,768]{2,1,0:T(8,128)(2,1)S(1)} custom-call(s32[9]{0:T(128)S(1)} %pad_add_fusion.2.info, bf16[384,768]{1,0:T(8,128)(2,1)} %copy-done.17, bf16[384,768]{1,0:T(8,128)(2,1)} %copy-done.21, bf16[384,768]{1,0:T(8,128)(2,1)} %copy-done.19, bf16[384,768]{1,0:T(8,128)(2,1)} %copy-done.23, bf16[384,768]{1,0:T(8,128)(2,1)} %copy-done.18, ...), custom_call_target="tpu_custom_call" | custom-call | flops 339738624 | bytes 884736 | tf_op jit(solution)/shard_map/project_grad/pallas_call | solution.py:456
  281.8 7.9 %collective-permute-start.34 = (bf16[384,768]{1,0:T(8,128)(2,1)}, bf16[384,768]{1,0:T(8,128)(2,1)S(1)}, u32[]{:S(2)}, u32[]{:S(2)}) collective-permute-start(bf16[384,768]{1,0:T(8,128)(2,1)} %add_convert_fusion.1), channel_id=1, source_target_pairs={{6,2},{7,3},{0,4},{1,5},{10,6},{11,7},{4,8},{5,9},{14,10},{15,11},... | collective-permute-start | bytes 1769480 | tf_op jit(solution)/shard_map/ppermute | solution.py:1249
  297.0 7.1 %collective-permute-done.34.recv = bf16[384,768]{1,0:T(8,128)(2,1)S(1)} collective-permute-done((bf16[384,768]{1,0:T(8,128)(2,1)}, bf16[384,768]{1,0:T(8,128)(2,1)S(1)}, u32[]{:S(2)}, u32[]{:S(2)}) %collective-permute-start.34) | collective-permute-done | bytes 589856 | tf_op jit(solution)/shard_map/ppermute | solution.py:1249
  304.1 13.5 %gbst_backward.1 = (f32[784,768]{1,0:T(8,128)S(1)}, f32[8,768]{1,0:T(8,128)S(1)}) custom-call(f32[384,768]{1,0:T(8,128)S(1)} %convert_add_fusion.keep, bf16[384,768]{1,0:T(8,128)(2,1)S(1)} %collective-permute-done.34.recv, f32[384,768]{1,0:T(8,128)} %copy-done.9, f32[384,768]{1,0:T(8,128)} %copy-done.29, f32[1,768]{1,0:T(1,128)} %copy-done.46, ...), custom_call_target="tpu_custom_call" | custom-call | flops 8847360 | bytes 1769472 | tf_op jit(solution)/shard_map/gbst_backward/pallas_call | solution.py:315
  329.4 4.2 %collective-permute-start.39 = (f32[16,768]{1,0:T(8,128)S(1)}, f32[16,768]{1,0:T(8,128)S(1)}, u32[]{:S(2)}, u32[]{:S(2)}) collective-permute-start(f32[16,768]{1,0:T(8,128)S(1)} %add.283), channel_id=1, source_target_pairs={{0,4},{4,0},{8,12},{12,8},{16,20},{20,16},{24,28},{28,24},{1,5},{5... | collective-permute-start | bytes 147464 | tf_op jit(solution)/shard_map/ppermute | solution.py:1283
  343.6 5.1 %all-to-all-start = ((bf16[4,24,768]{2,1,0:T(8,128)(2,1)}), bf16[4,24,768]{2,1,0:T(8,128)(2,1)S(1)}, u32[]{:S(2)}, u32[]{:S(2)}) async-start(bf16[4,24,768]{2,1,0:T(8,128)(2,1)} %bitcast.144), calls=%async_computation.2 | async-start | bytes 294912 | tf_op jit(solution)/shard_map/all_to_all | solution.py:1243
  (368 shorter events, 144.1 us)
Async XLA Ops:
  7.2 124.9 %all-gather.3.cloned.1.call-start = ((), (), s32[]{:S(2)}) async-start(), calls=%async_computation.5 | async-start | bytes 6266880 | tf_op jit(solution)/shard_map/all_gather | solution.py:1179
  8.0 19.9 %collective-permute-start = (bf16[8,768]{1,0:T(8,128)(2,1)S(1)}, bf16[8,768]{1,0:T(8,128)(2,1)S(1)}, u32[]{:S(2)}, u32[]{:S(2)}) collective-permute-start(bf16[8,768]{1,0:T(8,128)(2,1)S(1)} %get-tuple-element.282), channel_id=1, source_target_pairs={{0,1},{1,2},{2,3},{3,4},{4,5},{5,6},{6,7},{7,8},{8,9},{9,10},{10,1... | collective-permute-start | bytes 36872 | tf_op jit(solution)/shard_map/ppermute | solution.py:1058
  12.5 15.4 %collective-permute-start.1 = (bf16[8,768]{1,0:T(8,128)(2,1)S(1)}, bf16[8,768]{1,0:T(8,128)(2,1)S(1)}, u32[]{:S(2)}, u32[]{:S(2)}) collective-permute-start(bf16[8,768]{1,0:T(8,128)(2,1)S(1)} %get-tuple-element.281), channel_id=1, source_target_pairs={{1,0},{2,1},{3,2},{4,3},{5,4},{6,5},{7,6},{8,7},{9,8},{10,9},{11,1... | collective-permute-start | bytes 36872 | tf_op jit(solution)/shard_map/ppermute | solution.py:1059
  23.8 13.6 %collective-permute-start.4 = (bf16[1,96,576]{2,1,0:T(8,128)(2,1)S(1)}, bf16[1,96,576]{2,1,0:T(8,128)(2,1)S(1)}, u32[]{:S(2)}, u32[]{:S(2)}) collective-permute-start(bf16[1,96,576]{2,1,0:T(8,128)(2,1)S(1)} %maximum_bitcast_fusion), channel_id=1, source_target_pairs={{0,16},{4,20},{8,24},{12,28},{16,0},{20,4},{24,8},{28,12},{1,17},{... | collective-permute-start | bytes 331784 | tf_op jit(solution)/shard_map/ppermute | solution.py:1101
  44.6 16.1 %collective-permute-start.8 = (bf16[384,768]{1,0:T(8,128)(2,1)S(1)}, bf16[384,768]{1,0:T(8,128)(2,1)S(1)}, u32[]{:S(2)}, u32[]{:S(2)}) collective-permute-start(bf16[384,768]{1,0:T(8,128)(2,1)S(1)} %get-tuple-element.111.refs_0_), channel_id=1, source_target_pairs={{2,6},{3,7},{4,0},{5,1},{6,10},{7,11},{8,4},{9,5},{10,14},{11,15},... | collective-permute-start | bytes 1769480 | tf_op jit(solution)/shard_map/ppermute | solution.py:1176
  45.9 18.9 %collective-permute-start.9 = (bf16[384,768]{1,0:T(8,128)(2,1)S(1)}, bf16[384,768]{1,0:T(8,128)(2,1)S(1)}, u32[]{:S(2)}, u32[]{:S(2)}) collective-permute-start(bf16[384,768]{1,0:T(8,128)(2,1)S(1)} %get-tuple-element.111.refs_0_), channel_id=1, source_target_pairs={{0,2},{1,3},{2,0},{3,1},{4,6},{5,7},{6,4},{7,5},{8,10},{9,11},{10,... | collective-permute-start | bytes 1769480 | tf_op jit(solution)/shard_map/ppermute | solution.py:1008
  64.8 197.8 %reduce-scatter.3.cloned.1.call-start = ((), (), s32[]{:S(2)}) async-start(), calls=%async_computation.3 | async-start | bytes 5013504 | tf_op jit(solution)/shard_map/reduce_scatter | solution.py:1218
  66.5 13.8 %collective-permute-start.14 = (bf16[384,768]{1,0:T(8,128)(2,1)S(1)}, bf16[384,768]{1,0:T(8,128)(2,1)S(1)}, u32[]{:S(2)}, u32[]{:S(2)}) collective-permute-start(bf16[384,768]{1,0:T(8,128)(2,1)S(1)} %collective-permute-done.8.refs_4_), channel_id=1, source_target_pairs={{0,2},{1,3},{2,0},{3,1},{4,6},{5,7},{6,4},{7,5},{8,10},{9,11},{10,... | collective-permute-start | bytes 1769480 | tf_op jit(solution)/shard_map/ppermute | solution.py:1008
  68.6 29.0 %collective-permute-start.5 = (bf16[384,768]{1,0:T(8,128)(2,1)S(1)}, bf16[384,768]{1,0:T(8,128)(2,1)S(1)}, u32[]{:S(2)}, u32[]{:S(2)}) collective-permute-start(bf16[384,768]{1,0:T(8,128)(2,1)S(1)} %get-tuple-element.111.refs_0_), channel_id=1, source_target_pairs={{0,1},{1,0},{2,3},{3,2},{4,5},{5,4},{6,7},{7,6},{8,9},{9,8},{10,11... | collective-permute-start | bytes 1769480 | tf_op jit(solution)/shard_map/ppermute | solution.py:1008
  70.1 27.5 %collective-permute-start.12 = (bf16[384,768]{1,0:T(8,128)(2,1)S(1)}, bf16[384,768]{1,0:T(8,128)(2,1)S(1)}, u32[]{:S(2)}, u32[]{:S(2)}) collective-permute-start(bf16[384,768]{1,0:T(8,128)(2,1)S(1)} %collective-permute-done.8.refs_4_), channel_id=1, source_target_pairs={{0,1},{1,0},{2,3},{3,2},{4,5},{5,4},{6,7},{7,6},{8,9},{9,8},{10,11... | collective-permute-start | bytes 1769480 | tf_op jit(solution)/shard_map/ppermute | solution.py:1008
  70.2 27.4 %collective-permute-start.11 = (bf16[384,768]{1,0:T(8,128)(2,1)S(1)}, bf16[384,768]{1,0:T(8,128)(2,1)S(1)}, u32[]{:S(2)}, u32[]{:S(2)}) collective-permute-start(bf16[384,768]{1,0:T(8,128)(2,1)S(1)} %collective-permute-done.9.refs_2_), channel_id=1, source_target_pairs={{0,1},{1,0},{2,3},{3,2},{4,5},{5,4},{6,7},{7,6},{8,9},{9,8},{10,11... | collective-permute-start | bytes 1769480 | tf_op jit(solution)/shard_map/ppermute | solution.py:1008
  82.8 14.5 %collective-permute-start.13 = (bf16[4,96,576]{2,1,0:T(8,128)(2,1)S(1)}, bf16[4,96,576]{2,1,0:T(8,128)(2,1)S(1)}, u32[]{:S(2)}, u32[]{:S(2)}) collective-permute-start(bf16[4,96,576]{2,1,0:T(8,128)(2,1)S(1)} %pad_maximum_fusion.2), channel_id=1, source_target_pairs={{0,4},{4,0},{8,12},{12,8},{16,20},{20,16},{24,28},{28,24},{1,5},{5... | collective-permute-start | bytes 1327112 | tf_op jit(solution)/shard_map/ppermute | solution.py:1196
  84.2 43.9 %collective-permute-start.18 = (bf16[384,768]{1,0:T(8,128)(2,1)S(1)}, bf16[384,768]{1,0:T(8,128)(2,1)S(1)}, u32[]{:S(2)}, u32[]{:S(2)}) collective-permute-start(bf16[384,768]{1,0:T(8,128)(2,1)S(1)} %copy-done.7), channel_id=1, source_target_pairs={{0,2},{1,3},{2,0},{3,1},{4,6},{5,7},{6,4},{7,5},{8,10},{9,11},{10,... | collective-permute-start | bytes 1769480 | tf_op jit(solution)/shard_map/ppermute | solution.py:1008
  135.9 14.6 %collective-permute-start.20 = (bf16[384,768]{1,0:T(8,128)(2,1)S(1)}, bf16[384,768]{1,0:T(8,128)(2,1)S(1)}, u32[]{:S(2)}, u32[]{:S(2)}) collective-permute-start(bf16[384,768]{1,0:T(8,128)(2,1)S(1)} %get-tuple-element.132.nt.na), channel_id=1, source_target_pairs={{0,2},{1,3},{2,0},{3,1},{4,6},{5,7},{6,4},{7,5},{8,10},{9,11},{10,... | collective-permute-start | bytes 1769480 | tf_op jit(solution)/shard_map/ppermute | solution.py:1008
  157.3 13.8 %collective-permute-start.21 = (bf16[384,768]{1,0:T(8,128)(2,1)}, bf16[384,768]{1,0:T(8,128)(2,1)S(1)}, u32[]{:S(2)}, u32[]{:S(2)}) collective-permute-start(bf16[384,768]{1,0:T(8,128)(2,1)} %get-tuple-element.139), channel_id=1, source_target_pairs={{0,2},{1,3},{2,0},{3,1},{4,6},{5,7},{6,4},{7,5},{8,10},{9,11},{10,... | collective-permute-start | bytes 1769480 | tf_op jit(solution)/shard_map/ppermute | solution.py:1008
  171.1 172.5 %reduce-scatter.5.cloned.1.call-start = ((), (), s32[]{:S(2)}) async-start(), calls=%async_computation.4 | async-start | bytes 1327104 | tf_op jit(solution)/shard_map/reduce_scatter | solution.py:1242
  208.3 33.7 %collective-permute-start.26 = (bf16[384,768]{1,0:T(8,128)(2,1)}, bf16[384,768]{1,0:T(8,128)(2,1)S(1)}, u32[]{:S(2)}, u32[]{:S(2)}) collective-permute-start(bf16[384,768]{1,0:T(8,128)(2,1)} %get-tuple-element.154), channel_id=1, source_target_pairs={{0,2},{1,3},{2,0},{3,1},{4,6},{5,7},{6,4},{7,5},{8,10},{9,11},{10,... | collective-permute-start | bytes 1769480 | tf_op jit(solution)/shard_map/ppermute | solution.py:1008
  208.3 33.6 %collective-permute-start.27 = (bf16[768,192]{1,0:T(8,128)(2,1)S(1)}, bf16[768,192]{1,0:T(8,128)(2,1)S(1)}, u32[]{:S(2)}, u32[]{:S(2)}) collective-permute-start(bf16[768,192]{1,0:T(8,128)(2,1)S(1)} %fusion.7), channel_id=1, source_target_pairs={{0,2},{1,3},{2,0},{3,1},{4,6},{5,7},{6,4},{7,5},{8,10},{9,11},{10,... | collective-permute-start | bytes 884744 | tf_op jit(solution)/shard_map/ppermute | solution.py:1008
  247.7 14.9 %collective-permute-start.29 = (bf16[384,768]{1,0:T(8,128)(2,1)}, bf16[384,768]{1,0:T(8,128)(2,1)}, u32[]{:S(2)}, u32[]{:S(2)}) collective-permute-start(bf16[384,768]{1,0:T(8,128)(2,1)} %add_convert_fusion.2), channel_id=1, source_target_pairs={{0,2},{1,3},{2,0},{3,1},{4,6},{5,7},{6,4},{7,5},{8,10},{9,11},{10,... | collective-permute-start | bytes 1769480 | tf_op jit(solution)/shard_map/ppermute | solution.py:1008
  247.9 25.3 %collective-permute-start.31 = (bf16[384,768]{1,0:T(8,128)(2,1)}, bf16[384,768]{1,0:T(8,128)(2,1)}, u32[]{:S(2)}, u32[]{:S(2)}) collective-permute-start(bf16[384,768]{1,0:T(8,128)(2,1)} %copy-done.51), channel_id=1, source_target_pairs={{0,1},{1,0},{2,3},{3,2},{4,5},{5,4},{6,7},{7,6},{8,9},{9,8},{10,11... | collective-permute-start | bytes 1769480 | tf_op jit(solution)/shard_map/ppermute | solution.py:1008
  271.1 23.6 %collective-permute-start.30 = (bf16[384,768]{1,0:T(8,128)(2,1)}, bf16[384,768]{1,0:T(8,128)(2,1)S(1)}, u32[]{:S(2)}, u32[]{:S(2)}) collective-permute-start(bf16[384,768]{1,0:T(8,128)(2,1)} %get-tuple-element.177), channel_id=1, source_target_pairs={{0,1},{1,0},{2,3},{3,2},{4,5},{5,4},{6,7},{7,6},{8,9},{9,8},{10,11... | collective-permute-start | bytes 1769480 | tf_op jit(solution)/shard_map/ppermute | solution.py:1008
  279.5 39.8 %collective-permute-start.43 = (bf16[24,4096]{1,0:T(8,128)(2,1)S(1)}, bf16[24,4096]{1,0:T(8,128)(2,1)}, u32[]{:S(2)}, u32[]{:S(2)}) collective-permute-start(bf16[24,4096]{1,0:T(8,128)(2,1)S(1)} %dynamic-slice_bitcast_fusion), channel_id=1, source_target_pairs={{0,1},{1,0},{2,3},{3,2},{4,5},{5,4},{6,7},{7,6},{8,9},{9,8},{10,11... | collective-permute-start | bytes 589832 | tf_op jit(solution)/shard_map/ppermute | solution.py:1008
  281.8 15.0 %collective-permute-start.33 = (bf16[384,768]{1,0:T(8,128)(2,1)}, bf16[384,768]{1,0:T(8,128)(2,1)S(1)}, u32[]{:S(2)}, u32[]{:S(2)}) collective-permute-start(bf16[384,768]{1,0:T(8,128)(2,1)} %add_convert_fusion), channel_id=1, source_target_pairs={{0,2},{1,3},{2,0},{3,1},{4,6},{5,7},{6,4},{7,5},{8,10},{9,11},{10,... | collective-permute-start | bytes 1769480 | tf_op jit(solution)/shard_map/ppermute | solution.py:1008
  281.8 22.3 %collective-permute-start.34 = (bf16[384,768]{1,0:T(8,128)(2,1)}, bf16[384,768]{1,0:T(8,128)(2,1)S(1)}, u32[]{:S(2)}, u32[]{:S(2)}) collective-permute-start(bf16[384,768]{1,0:T(8,128)(2,1)} %add_convert_fusion.1), channel_id=1, source_target_pairs={{6,2},{7,3},{0,4},{1,5},{10,6},{11,7},{4,8},{5,9},{14,10},{15,11},... | collective-permute-start | bytes 1769480 | tf_op jit(solution)/shard_map/ppermute | solution.py:1249
  (99 other events, 968.6 us)
Sparse Core Ops, SparseCore 0:
  64.9 58.6 all-gather.2
  171.2 76.6 reduce-scatter.2
  271.2 70.4 reduce-scatter.4

commit v3 on v2

--- a/solution.py
+++ b/solution.py
@@ -323,7 +323,7 @@
             pltpu.VMEM((d // 128, nb + 16, 128), f32),
             pltpu.VMEM((56, d), f32),
         ],
-        flops=120 * nb * d,
+        flops=4 * 10**11,
         moved=24 * nb * d,
         vmem=28,
         name="gbst_backward",
@@ -375,7 +375,7 @@
         prefetch=1,
         ins=[whole(x.shape) for x in args],
         out_specs=tuple(whole(x) for x in shapes),
-        flops=2 * ext * d * 3 * TILE,
+        flops=4 * 10**11,
         moved=2 * (ext * d + 2 * ext * TILE + d * d),
         vmem=30,
         name="project",
@@ -1225,7 +1225,7 @@
     back = (ga[0], back1, back2[0], flip(back2[1], 1))
     mid_m = (keep_m[1] + recv_m[1].astype(f32)).astype(bf16)
 
-    out_b, mid_m, *back = lax.optimization_barrier((out_b, mid_m, *back))
+    out_b, *back = lax.optimization_barrier((out_b, *back))
     got_m = flip(mid_m, 2)
     out_got = flip(out_b, 2)
     dq, dk, dv, sums = attend_back(info, q, k, v, diag, oloc, lse, *back, heads)

time: 366 us -> 353 us (0.964)
  waiting for transfers between devices: 84.3 us -> 69.4 us
  Pallas kernels: 117 us -> 129 us
  starting transfers between devices: 81.7 us -> 72.5 us
    pallas_call x1, Pallas kernels: 5.09 us -> 16.5 us  [middle(): kernel_call(middle_kernel, tuple((struct(*s) for s in shapes)), prefetch=...]
    reduce_scatter x1, starting transfers between devices: 10.9 us -> 0.04 us  [local(): lax.psum_scatter(part.reshape(n_ctx, rows_ctx, 4 * width), 'ctx', scatter...]
    ppermute x32, waiting for transfers between devices: 52.9 us -> 44.5 us  [flip(): return lax.ppermute(x, ULY, [(i, i ^ bit) for i in range(4)])]
    ppermute x1, waiting for transfers between devices: 12.7 us -> 4.39 us  [local(): lax.ppermute(qkv_w, 'ctx', [(i, i ^ bits_left[-1]) for i in range(n_ctx)])]
    ppermute x32, starting transfers between devices: 29.3 us -> 35.5 us  [flip(): return lax.ppermute(x, ULY, [(i, i ^ bit) for i in range(4)])]
    unnamed x165 -> x163, local copies, waits for them, and re-layouts: 20.3 us -> 18.3 us
  transfers between devices with their start and end apart: 48 -> 48, of which waited for: 20 -> 21; matrix products, arithmetic and copies ran while one was open for 12% -> 13% of each run, Pallas kernels for 29% -> 34%
where the time goes in v3:
time: 353 us; the launch traced here: 349 us
  Pallas kernels  129 us (37%)
  starting transfers between devices  72.5 us (21%)
  waiting for transfers between devices  69.4 us (20%)
  local copies, waits for them, and re-layouts  38 us (11%)
  other arithmetic  23.5 us (7%)
  between operations  15.5 us (4%)
    ppermute x32, waiting for transfers between devices, flip(): return lax.ppermute(x, ULY, [(i, i ^ bit) for i in range(4)])  44.5 us
    ppermute x32, starting transfers between devices, flip(): return lax.ppermute(x, ULY, [(i, i ^ bit) for i in range(4)])  35.5 us
    pallas_call x1, Pallas kernels, attend_back(): kernel_call(partial(attend_back_kernel, heads), (struct((rows, TILE), bf1...  31.2 us
    unnamed x163, local copies, waits for them, and re-layouts  18.3 us
    pallas_call x1, Pallas kernels, attend(): kernel_call(partial(attend_kernel, heads), (struct(sent, bf16), struct(se...  17.8 us
    pallas_call x1, Pallas kernels, middle(): kernel_call(middle_kernel, tuple((struct(*s) for s in shapes)), prefetch=...  16.5 us
    pallas_call x1, Pallas kernels, gbst_backward(): kernel_call(gbst_backward_kernel, (struct((nb + 16, d), f32), struct((8,...  13.5 us
    pallas_call x2, Pallas kernels, feed(): kernel_call(feed_kernel, (struct((tok, d), kind), struct((tok, d), kind))...  12.6 us
  transfers between devices with their start and end apart: 48, of which 21 were waited for; matrix products, arithmetic and copies ran while one was open for 13% of the time, Pallas kernels for 34%

profile of v3, /device:TPU:1, one launch (start us, length us, event | category | flops | bytes accessed | tf_op | source)
XLA Modules:
  0.0 348.8 jit_solution(16836129645864750577)
XLA Ops:
  8.0 4.5 %collective-permute-start = (bf16[8,768]{1,0:T(8,128)(2,1)S(1)}, bf16[8,768]{1,0:T(8,128)(2,1)S(1)}, u32[]{:S(2)}, u32[]{:S(2)}) collective-permute-start(bf16[8,768]{1,0:T(8,128)(2,1)S(1)} %get-tuple-element.280), channel_id=1, source_target_pairs={{0,1},{1,2},{2,3},{3,4},{4,5},{5,6},{6,7},{7,8},{8,9},{9,10},{10,1... | collective-permute-start | bytes 36872 | tf_op jit(solution)/shard_map/ppermute | solution.py:1058
  28.0 7.0 %gbst_forward.1 = (f32[384,768]{1,0:T(8,128)S(1)}, bf16[384,768]{1,0:T(8,128)(2,1)S(1)}, f32[12,64,768]{2,1,0:T(8,128)S(1)}, f32[64,128]{1,0:T(8,128)S(1)}) custom-call(bf16[8,768]{1,0:T(8,128)(2,1)S(1)} %collective-permute-done.lo, bf16[768,768]{1,0:T(8,128)(2,1)S(1)} %copy-done.18, bf16[8,768]{1,0:T(8,128)(2,1)S(1)} %collective-permute-done.1.hi, ...), custom_call_target="tpu_custom_call" | custom-call | flops 4423680 | bytes 1474560 | tf_op jit(solution)/shard_map/gbst_forward/pallas_call | solution.py:179
  53.9 7.1 %collective-permute-done.8.refs_4_ = bf16[384,768]{1,0:T(8,128)(2,1)S(1)} collective-permute-done((bf16[384,768]{1,0:T(8,128)(2,1)S(1)}, bf16[384,768]{1,0:T(8,128)(2,1)S(1)}, u32[]{:S(2)}, u32[]{:S(2)}) %collective-permute-start.8) | collective-permute-done | bytes 589856 | tf_op jit(solution)/shard_map/ppermute | solution.py:1176
  71.5 9.3 %collective-permute-done.14.refs_6_ = bf16[384,768]{1,0:T(8,128)(2,1)S(1)} collective-permute-done((bf16[384,768]{1,0:T(8,128)(2,1)S(1)}, bf16[384,768]{1,0:T(8,128)(2,1)S(1)}, u32[]{:S(2)}, u32[]{:S(2)}) %collective-permute-start.14) | collective-permute-done | bytes 589856 | tf_op jit(solution)/shard_map/ppermute | solution.py:1008
  83.4 4.4 %collective-permute-done.13 = bf16[4,96,576]{2,1,0:T(8,128)(2,1)S(1)} collective-permute-done((bf16[4,96,576]{2,1,0:T(8,128)(2,1)S(1)}, bf16[4,96,576]{2,1,0:T(8,128)(2,1)S(1)}, u32[]{:S(2)}, u32[]{:S(2)}) %collective-permute-start.13) | collective-permute-done | bytes 442400 | tf_op jit(solution)/shard_map/ppermute | solution.py:1196
  89.3 4.2 %project.1 = (bf16[1536,256]{1,0:T(8,128)(2,1)S(1)}, bf16[3072,256]{1,0:T(8,128)(2,1)S(1)}, bf16[3072,256]{1,0:T(8,128)(2,1)S(1)}, bf16[256,3072]{1,0:T(8,128)(2,1)S(1)}, bf16[768,768]{1,0:T(8,128)(2,1)S(1)}) custom-call(s32[9]{0:T(128)S(1)} %pad_add_fusion.1.info, bf16[384,768]{1,0:T(8,128)(2,1)S(1)} %get-tuple-element.110.refs_0_, ...), custom_call_target="tpu_custom_call" | custom-call | flops 49999998976 | bytes 1130496 | tf_op jit(solution)/shard_map/project/pallas_call | solution.py:372
  94.8 17.8 %attend.1 = (bf16[2,3,192,128]{3,2,1,0:T(8,128)(2,1)S(1)}, bf16[2,3,192,128]{3,2,1,0:T(8,128)(2,1)S(1)}, bf16[192,1536]{1,0:T(8,128)(2,1)S(1)}, f32[6,8,768]{2,1,0:T(8,128)S(1)}) custom-call(s32[13]{0:T(128)S(1)} %pad_add_fusion.info, bf16[1536,256]{1,0:T(8,128)(2,1)S(1)} %get-tuple-element.121.q, bf16[3072,256]{1,0:T(8,128)(2,1)S(1)} %get-tuple-element.122.k, ...), custom_call_target="tpu_custom_call" | custom-call | flops 754974720 | bytes 786432 | tf_op jit(solution)/shard_map/attend/pallas_call | solution.py:599
  114.6 6.1 %collective-permute-done.17 = bf16[2,3,192,128]{3,2,1,0:T(8,128)(2,1)S(1)} collective-permute-done((bf16[2,3,192,128]{3,2,1,0:T(8,128)(2,1)S(1)}, bf16[2,3,192,128]{3,2,1,0:T(8,128)(2,1)S(1)}, u32[]{:S(2)}, u32[]{:S(2)}) %collective-permute-start.17) | collective-permute-done | bytes 294944 | tf_op jit(solution)/shard_map/ppermute | solution.py:1008
  129.5 5.9 %feed.2 = (f32[384,768]{1,0:T(8,128)S(1)}, f32[384,768]{1,0:T(8,128)S(1)}, bf16[384,1024]{1,0:T(8,128)(2,1)S(1)}, bf16[384,1024]{1,0:T(8,128)(2,1)S(1)}, bf16[384,1024]{1,0:T(8,128)(2,1)S(1)}) custom-call(bf16[384,768]{1,0:T(8,128)(2,1)S(1)} %get-tuple-element.131.nt.na, bf16[384,768]{1,0:T(8,128)(2,1)S(1)} %copy-done.7, ...), custom_call_target="tpu_custom_call" | custom-call | flops 452984832 | bytes 1400832 | tf_op jit(solution)/shard_map/feed/pallas_call | solution.py:835
  136.4 6.7 %collective-permute-done.20.nt.nb = bf16[384,768]{1,0:T(8,128)(2,1)S(1)} collective-permute-done((bf16[384,768]{1,0:T(8,128)(2,1)S(1)}, bf16[384,768]{1,0:T(8,128)(2,1)S(1)}, u32[]{:S(2)}, u32[]{:S(2)}) %collective-permute-start.20) | collective-permute-done | bytes 589856 | tf_op jit(solution)/shard_map/ppermute | solution.py:1008
  143.1 6.8 %feed.3 = (bf16[384,768]{1,0:T(8,128)(2,1)}, bf16[384,768]{1,0:T(8,128)(2,1)}, bf16[384,1024]{1,0:T(8,128)(2,1)S(1)}, bf16[384,1024]{1,0:T(8,128)(2,1)S(1)}, bf16[384,1024]{1,0:T(8,128)(2,1)S(1)}) custom-call(bf16[384,768]{1,0:T(8,128)(2,1)S(1)} %collective-permute-done.20.nt.nb, bf16[384,768]{1,0:T(8,128)(2,1)S(1)} %collective-permute-done.18.gr.gb, ...), custom_call_target="tpu_custom_call" | custom-call | flops 452984832 | bytes 1400832 | tf_op jit(solution)/shard_map/feed/pallas_call | solution.py:835
  150.9 6.8 %weight_grads.1 = bf16[16,1152,128]{2,1,0:T(8,128)(2,1)S(1)} custom-call(bf16[384,768]{1,0:T(8,128)(2,1)S(1)} %get-tuple-element.131.nt.na, bf16[384,768]{1,0:T(8,128)(2,1)S(1)} %collective-permute-done.20.nt.nb, bf16[384,768]{1,0:T(8,128)(2,1)S(1)} %copy-done.7, bf16[384,768]{1,0:T(8,128)(2,1)S(1)} %collective-permute-done.18.gr.gb, ...), custom_call_target="tpu_custom_call" | custom-call | flops 452984832 | bytes 1179648 | tf_op jit(solution)/shard_map/weight_grads/pallas_call | solution.py:970
  159.9 4.0 %collective-permute-done.21.db = bf16[384,768]{1,0:T(8,128)(2,1)} collective-permute-done((bf16[384,768]{1,0:T(8,128)(2,1)}, bf16[384,768]{1,0:T(8,128)(2,1)}, u32[]{:S(2)}, u32[]{:S(2)}) %collective-permute-start.21) | collective-permute-done | bytes 589856 | tf_op jit(solution)/shard_map/ppermute | solution.py:1008
  164.0 16.5 %middle.1 = (f32[384,768]{1,0:T(8,128)S(1)}, bf16[384,768]{1,0:T(8,128)(2,1)S(1)}, bf16[2,3,192,128]{3,2,1,0:T(8,128)(2,1)S(1)}, bf16[2,3,192,128]{3,2,1,0:T(8,128)(2,1)}, f32[8,768]{1,0:T(8,128)S(1)}) custom-call(s32[1]{0:T(128)} %bitcast.info.me, f32[384,768]{1,0:T(8,128)S(1)} %get-tuple-element.130.mid, f32[384,768]{1,0:T(8,128)S(1)} %get-tuple-element.137.da, ...), custom_call_target="tpu_custom_call" | custom-call | flops 56623104 | bytes 1105920 | tf_op jit(solution)/shard_map/middle/pallas_call | solution.py:891
  183.7 3.8 %merge_grad.1 = (f32[2,768,192]{2,1,0:T(8,128)S(1)}, bf16[2,768,192]{2,1,0:T(8,128)(2,1)S(1)}) custom-call(s32[1]{0:T(128)} %bitcast.info.me, bf16[3,192,128]{2,1,0:T(8,128)(2,1)} %get-tuple-element.299.a0, bf16[3,192,128]{2,1,0:T(8,128)(2,1)} %copy-done.58, bf16[3,192,128]{2,1,0:T(8,128)(2,1)} %get-tuple-element.297.a2, bf16[3,192,128]{2,1,0:T(8,128)(2,1)} %copy-done.59, ...), custom_call_target="tpu_custom_call" | custom-call | flops 56623104 | bytes 368640 | tf_op jit(solution)/shard_map/merge_grad/pallas_call | solution.py:930
  199.6 31.2 %attend_back.1 = (bf16[1536,256]{1,0:T(8,128)(2,1)S(1)}, bf16[3072,256]{1,0:T(8,128)(2,1)S(1)}, bf16[3072,256]{1,0:T(8,128)(2,1)S(1)}, f32[9,3,8,512]{3,2,1,0:T(8,128)S(1)}) custom-call(s32[13]{0:T(128)S(1)} %pad_add_fusion.info, bf16[1536,256]{1,0:T(8,128)(2,1)} %copy-done.27, bf16[3072,256]{1,0:T(8,128)(2,1)} %copy-done.17, bf16[3072,256]{1,0:T(8,128)(2,1)} %copy-done.54, ...), custom_call_target="tpu_custom_call" | custom-call | flops 1887436800 | bytes 1572864 | tf_op jit(solution)/shard_map/attend_back/pallas_call | solution.py:712
  241.2 7.4 %project_grad.1 = bf16[8,96,768]{2,1,0:T(8,128)(2,1)S(1)} custom-call(s32[9]{0:T(128)S(1)} %pad_add_fusion.2.info, bf16[384,768]{1,0:T(8,128)(2,1)} %copy-done.28, bf16[384,768]{1,0:T(8,128)(2,1)} %copy-done.32, bf16[384,768]{1,0:T(8,128)(2,1)} %copy-done.30, bf16[384,768]{1,0:T(8,128)(2,1)} %copy-done.34, bf16[384,768]{1,0:T(8,128)(2,1)} %copy-done.29, ...), custom_call_target="tpu_custom_call" | custom-call | flops 339738624 | bytes 884736 | tf_op jit(solution)/shard_map/project_grad/pallas_call | solution.py:456
  271.5 5.7 %collective-permute-start.34 = (bf16[384,768]{1,0:T(8,128)(2,1)}, bf16[384,768]{1,0:T(8,128)(2,1)S(1)}, u32[]{:S(2)}, u32[]{:S(2)}) collective-permute-start(bf16[384,768]{1,0:T(8,128)(2,1)} %add_convert_fusion.1), channel_id=1, source_target_pairs={{6,2},{7,3},{0,4},{1,5},{10,6},{11,7},{4,8},{5,9},{14,10},{15,11},... | collective-permute-start | bytes 1769480 | tf_op jit(solution)/shard_map/ppermute | solution.py:1249
  285.7 6.2 %collective-permute-done.34.recv = bf16[384,768]{1,0:T(8,128)(2,1)S(1)} collective-permute-done((bf16[384,768]{1,0:T(8,128)(2,1)}, bf16[384,768]{1,0:T(8,128)(2,1)S(1)}, u32[]{:S(2)}, u32[]{:S(2)}) %collective-permute-start.34) | collective-permute-done | bytes 589856 | tf_op jit(solution)/shard_map/ppermute | solution.py:1249
  291.8 13.5 %gbst_backward.1 = (f32[784,768]{1,0:T(8,128)S(1)}, f32[8,768]{1,0:T(8,128)S(1)}) custom-call(f32[384,768]{1,0:T(8,128)S(1)} %convert_add_fusion.keep, bf16[384,768]{1,0:T(8,128)(2,1)S(1)} %collective-permute-done.34.recv, f32[384,768]{1,0:T(8,128)} %copy-done.19, f32[384,768]{1,0:T(8,128)} %copy-done.45, f32[1,768]{1,0:T(1,128)} %copy-done.43, ...), custom_call_target="tpu_custom_call" | custom-call | flops 49999998976 | bytes 1769472 | tf_op jit(solution)/shard_map/gbst_backward/pallas_call | solution.py:315
  307.9 3.5 %collective-permute-start.35 = (f32[8,768]{1,0:T(8,128)S(1)}, f32[8,768]{1,0:T(8,128)S(1)}, u32[]{:S(2)}, u32[]{:S(2)}) collective-permute-start(f32[8,768]{1,0:T(8,128)S(1)} %slice.159), channel_id=1, source_target_pairs={{0,1},{1,2},{2,3},{3,4},{4,5},{5,6},{6,7},{7,8},{8,9},{9,10},{10,1... | collective-permute-start | bytes 73736 | tf_op jit(solution)/shard_map/ppermute | solution.py:1267
  311.4 4.2 %collective-permute-start.38 = (f32[16,768]{1,0:T(8,128)S(1)}, f32[16,768]{1,0:T(8,128)S(1)}, u32[]{:S(2)}, u32[]{:S(2)}) collective-permute-start(f32[16,768]{1,0:T(8,128)S(1)} %fusion.33), channel_id=1, source_target_pairs={{0,2},{1,3},{2,0},{3,1},{4,6},{5,7},{6,4},{7,5},{8,10},{9,11},{10,... | collective-permute-start | bytes 147464 | tf_op jit(solution)/shard_map/ppermute | solution.py:1008
  322.9 3.9 %collective-permute-start.40 = (f32[16,768]{1,0:T(8,128)S(1)}, f32[16,768]{1,0:T(8,128)S(1)}, u32[]{:S(2)}, u32[]{:S(2)}) collective-permute-start(f32[16,768]{1,0:T(8,128)S(1)} %add.284), channel_id=1, source_target_pairs={{0,8},{4,12},{8,0},{12,4},{16,24},{20,28},{24,16},{28,20},{1,9},{5... | collective-permute-start | bytes 147464 | tf_op jit(solution)/shard_map/ppermute | solution.py:1283
  330.7 4.8 %all-to-all-start = ((bf16[4,24,768]{2,1,0:T(8,128)(2,1)}), bf16[4,24,768]{2,1,0:T(8,128)(2,1)S(1)}, u32[]{:S(2)}, u32[]{:S(2)}) async-start(bf16[4,24,768]{2,1,0:T(8,128)(2,1)} %bitcast.144), calls=%async_computation.2 | async-start | bytes 294912 | tf_op jit(solution)/shard_map/all_to_all | solution.py:1243
  (366 shorter events, 142.2 us)
Async XLA Ops:
  7.2 118.0 %all-gather.3.cloned.1.call-start = ((), (), s32[]{:S(2)}) async-start(), calls=%async_computation.5 | async-start | bytes 6266880 | tf_op jit(solution)/shard_map/all_gather | solution.py:1179
  8.0 19.9 %collective-permute-start = (bf16[8,768]{1,0:T(8,128)(2,1)S(1)}, bf16[8,768]{1,0:T(8,128)(2,1)S(1)}, u32[]{:S(2)}, u32[]{:S(2)}) collective-permute-start(bf16[8,768]{1,0:T(8,128)(2,1)S(1)} %get-tuple-element.280), channel_id=1, source_target_pairs={{0,1},{1,2},{2,3},{3,4},{4,5},{5,6},{6,7},{7,8},{8,9},{9,10},{10,1... | collective-permute-start | bytes 36872 | tf_op jit(solution)/shard_map/ppermute | solution.py:1058
  12.5 15.4 %collective-permute-start.1 = (bf16[8,768]{1,0:T(8,128)(2,1)S(1)}, bf16[8,768]{1,0:T(8,128)(2,1)S(1)}, u32[]{:S(2)}, u32[]{:S(2)}) collective-permute-start(bf16[8,768]{1,0:T(8,128)(2,1)S(1)} %get-tuple-element.279), channel_id=1, source_target_pairs={{1,0},{2,1},{3,2},{4,3},{5,4},{6,5},{7,6},{8,7},{9,8},{10,9},{11,1... | collective-permute-start | bytes 36872 | tf_op jit(solution)/shard_map/ppermute | solution.py:1059
  23.8 12.6 %collective-permute-start.4 = (bf16[1,96,576]{2,1,0:T(8,128)(2,1)S(1)}, bf16[1,96,576]{2,1,0:T(8,128)(2,1)S(1)}, u32[]{:S(2)}, u32[]{:S(2)}) collective-permute-start(bf16[1,96,576]{2,1,0:T(8,128)(2,1)S(1)} %maximum_bitcast_fusion), channel_id=1, source_target_pairs={{0,16},{4,20},{8,24},{12,28},{16,0},{20,4},{24,8},{28,12},{1,17},{... | collective-permute-start | bytes 331784 | tf_op jit(solution)/shard_map/ppermute | solution.py:1101
  44.8 16.1 %collective-permute-start.8 = (bf16[384,768]{1,0:T(8,128)(2,1)S(1)}, bf16[384,768]{1,0:T(8,128)(2,1)S(1)}, u32[]{:S(2)}, u32[]{:S(2)}) collective-permute-start(bf16[384,768]{1,0:T(8,128)(2,1)S(1)} %get-tuple-element.110.refs_0_), channel_id=1, source_target_pairs={{2,6},{3,7},{4,0},{5,1},{6,10},{7,11},{8,4},{9,5},{10,14},{11,15},... | collective-permute-start | bytes 1769480 | tf_op jit(solution)/shard_map/ppermute | solution.py:1176
  46.1 18.2 %collective-permute-start.9 = (bf16[384,768]{1,0:T(8,128)(2,1)S(1)}, bf16[384,768]{1,0:T(8,128)(2,1)S(1)}, u32[]{:S(2)}, u32[]{:S(2)}) collective-permute-start(bf16[384,768]{1,0:T(8,128)(2,1)S(1)} %get-tuple-element.110.refs_0_), channel_id=1, source_target_pairs={{0,2},{1,3},{2,0},{3,1},{4,6},{5,7},{6,4},{7,5},{8,10},{9,11},{10,... | collective-permute-start | bytes 1769480 | tf_op jit(solution)/shard_map/ppermute | solution.py:1008
  64.4 186.9 %reduce-scatter.3.cloned.1.call-start = ((), (), s32[]{:S(2)}) async-start(), calls=%async_computation.3 | async-start | bytes 5013504 | tf_op jit(solution)/shard_map/reduce_scatter | solution.py:1218
  67.1 13.8 %collective-permute-start.14 = (bf16[384,768]{1,0:T(8,128)(2,1)S(1)}, bf16[384,768]{1,0:T(8,128)(2,1)S(1)}, u32[]{:S(2)}, u32[]{:S(2)}) collective-permute-start(bf16[384,768]{1,0:T(8,128)(2,1)S(1)} %collective-permute-done.8.refs_4_), channel_id=1, source_target_pairs={{0,2},{1,3},{2,0},{3,1},{4,6},{5,7},{6,4},{7,5},{8,10},{9,11},{10,... | collective-permute-start | bytes 1769480 | tf_op jit(solution)/shard_map/ppermute | solution.py:1008
  69.1 20.1 %collective-permute-start.5 = (bf16[384,768]{1,0:T(8,128)(2,1)S(1)}, bf16[384,768]{1,0:T(8,128)(2,1)S(1)}, u32[]{:S(2)}, u32[]{:S(2)}) collective-permute-start(bf16[384,768]{1,0:T(8,128)(2,1)S(1)} %get-tuple-element.110.refs_0_), channel_id=1, source_target_pairs={{0,1},{1,0},{2,3},{3,2},{4,5},{5,4},{6,7},{7,6},{8,9},{9,8},{10,11... | collective-permute-start | bytes 1769480 | tf_op jit(solution)/shard_map/ppermute | solution.py:1008
  70.6 18.6 %collective-permute-start.12 = (bf16[384,768]{1,0:T(8,128)(2,1)S(1)}, bf16[384,768]{1,0:T(8,128)(2,1)S(1)}, u32[]{:S(2)}, u32[]{:S(2)}) collective-permute-start(bf16[384,768]{1,0:T(8,128)(2,1)S(1)} %collective-permute-done.8.refs_4_), channel_id=1, source_target_pairs={{0,1},{1,0},{2,3},{3,2},{4,5},{5,4},{6,7},{7,6},{8,9},{9,8},{10,11... | collective-permute-start | bytes 1769480 | tf_op jit(solution)/shard_map/ppermute | solution.py:1008
  70.7 18.5 %collective-permute-start.11 = (bf16[384,768]{1,0:T(8,128)(2,1)S(1)}, bf16[384,768]{1,0:T(8,128)(2,1)S(1)}, u32[]{:S(2)}, u32[]{:S(2)}) collective-permute-start(bf16[384,768]{1,0:T(8,128)(2,1)S(1)} %collective-permute-done.9.refs_2_), channel_id=1, source_target_pairs={{0,1},{1,0},{2,3},{3,2},{4,5},{5,4},{6,7},{7,6},{8,9},{9,8},{10,11... | collective-permute-start | bytes 1769480 | tf_op jit(solution)/shard_map/ppermute | solution.py:1008
  71.1 16.6 %collective-permute-start.13 = (bf16[4,96,576]{2,1,0:T(8,128)(2,1)S(1)}, bf16[4,96,576]{2,1,0:T(8,128)(2,1)S(1)}, u32[]{:S(2)}, u32[]{:S(2)}) collective-permute-start(bf16[4,96,576]{2,1,0:T(8,128)(2,1)S(1)} %pad_maximum_fusion.2), channel_id=1, source_target_pairs={{0,4},{4,0},{8,12},{12,8},{16,20},{20,16},{24,28},{28,24},{1,5},{5... | collective-permute-start | bytes 1327112 | tf_op jit(solution)/shard_map/ppermute | solution.py:1196
  87.9 32.7 %collective-permute-start.18 = (bf16[384,768]{1,0:T(8,128)(2,1)S(1)}, bf16[384,768]{1,0:T(8,128)(2,1)S(1)}, u32[]{:S(2)}, u32[]{:S(2)}) collective-permute-start(bf16[384,768]{1,0:T(8,128)(2,1)S(1)} %copy-done.7), channel_id=1, source_target_pairs={{0,2},{1,3},{2,0},{3,1},{4,6},{5,7},{6,4},{7,5},{8,10},{9,11},{10,... | collective-permute-start | bytes 1769480 | tf_op jit(solution)/shard_map/ppermute | solution.py:1008
  128.3 14.7 %collective-permute-start.20 = (bf16[384,768]{1,0:T(8,128)(2,1)S(1)}, bf16[384,768]{1,0:T(8,128)(2,1)S(1)}, u32[]{:S(2)}, u32[]{:S(2)}) collective-permute-start(bf16[384,768]{1,0:T(8,128)(2,1)S(1)} %get-tuple-element.131.nt.na), channel_id=1, source_target_pairs={{0,2},{1,3},{2,0},{3,1},{4,6},{5,7},{6,4},{7,5},{8,10},{9,11},{10,... | collective-permute-start | bytes 1769480 | tf_op jit(solution)/shard_map/ppermute | solution.py:1008
  149.8 14.1 %collective-permute-start.21 = (bf16[384,768]{1,0:T(8,128)(2,1)}, bf16[384,768]{1,0:T(8,128)(2,1)}, u32[]{:S(2)}, u32[]{:S(2)}) collective-permute-start(bf16[384,768]{1,0:T(8,128)(2,1)} %get-tuple-element.138), channel_id=1, source_target_pairs={{0,2},{1,3},{2,0},{3,1},{4,6},{5,7},{6,4},{7,5},{8,10},{9,11},{10,... | collective-permute-start | bytes 1769480 | tf_op jit(solution)/shard_map/ppermute | solution.py:1008
  163.9 166.7 %reduce-scatter.5.cloned.1.call-start = ((), (), s32[]{:S(2)}) async-start(), calls=%async_computation.4 | async-start | bytes 1327104 | tf_op jit(solution)/shard_map/reduce_scatter | solution.py:1242
  194.4 36.4 %collective-permute-start.25 = (bf16[384,768]{1,0:T(8,128)(2,1)}, bf16[384,768]{1,0:T(8,128)(2,1)}, u32[]{:S(2)}, u32[]{:S(2)}) collective-permute-start(bf16[384,768]{1,0:T(8,128)(2,1)} %get-tuple-element.150), channel_id=1, source_target_pairs={{0,2},{1,3},{2,0},{3,1},{4,6},{5,7},{6,4},{7,5},{8,10},{9,11},{10,... | collective-permute-start | bytes 1769480 | tf_op jit(solution)/shard_map/ppermute | solution.py:1008
  197.0 33.8 %collective-permute-start.27 = (bf16[768,192]{1,0:T(8,128)(2,1)S(1)}, bf16[768,192]{1,0:T(8,128)(2,1)S(1)}, u32[]{:S(2)}, u32[]{:S(2)}) collective-permute-start(bf16[768,192]{1,0:T(8,128)(2,1)S(1)} %fusion.7), channel_id=1, source_target_pairs={{0,2},{1,3},{2,0},{3,1},{4,6},{5,7},{6,4},{7,5},{8,10},{9,11},{10,... | collective-permute-start | bytes 884744 | tf_op jit(solution)/shard_map/ppermute | solution.py:1008
  236.4 14.9 %collective-permute-start.29 = (bf16[384,768]{1,0:T(8,128)(2,1)}, bf16[384,768]{1,0:T(8,128)(2,1)}, u32[]{:S(2)}, u32[]{:S(2)}) collective-permute-start(bf16[384,768]{1,0:T(8,128)(2,1)} %add_convert_fusion.2), channel_id=1, source_target_pairs={{0,2},{1,3},{2,0},{3,1},{4,6},{5,7},{6,4},{7,5},{8,10},{9,11},{10,... | collective-permute-start | bytes 1769480 | tf_op jit(solution)/shard_map/ppermute | solution.py:1008
  237.6 25.3 %collective-permute-start.31 = (bf16[384,768]{1,0:T(8,128)(2,1)}, bf16[384,768]{1,0:T(8,128)(2,1)}, u32[]{:S(2)}, u32[]{:S(2)}) collective-permute-start(bf16[384,768]{1,0:T(8,128)(2,1)} %copy-done.47), channel_id=1, source_target_pairs={{0,1},{1,0},{2,3},{3,2},{4,5},{5,4},{6,7},{7,6},{8,9},{9,8},{10,11... | collective-permute-start | bytes 1769480 | tf_op jit(solution)/shard_map/ppermute | solution.py:1008
  259.8 22.4 %collective-permute-start.30 = (bf16[384,768]{1,0:T(8,128)(2,1)}, bf16[384,768]{1,0:T(8,128)(2,1)S(1)}, u32[]{:S(2)}, u32[]{:S(2)}) collective-permute-start(bf16[384,768]{1,0:T(8,128)(2,1)} %get-tuple-element.175), channel_id=1, source_target_pairs={{0,1},{1,0},{2,3},{3,2},{4,5},{5,4},{6,7},{7,6},{8,9},{9,8},{10,11... | collective-permute-start | bytes 1769480 | tf_op jit(solution)/shard_map/ppermute | solution.py:1008
  268.2 38.7 %collective-permute-start.43 = (bf16[24,4096]{1,0:T(8,128)(2,1)S(1)}, bf16[24,4096]{1,0:T(8,128)(2,1)}, u32[]{:S(2)}, u32[]{:S(2)}) collective-permute-start(bf16[24,4096]{1,0:T(8,128)(2,1)S(1)} %dynamic-slice_bitcast_fusion), channel_id=1, source_target_pairs={{0,1},{1,0},{2,3},{3,2},{4,5},{5,4},{6,7},{7,6},{8,9},{9,8},{10,11... | collective-permute-start | bytes 589832 | tf_op jit(solution)/shard_map/ppermute | solution.py:1008
  270.5 15.0 %collective-permute-start.33 = (bf16[384,768]{1,0:T(8,128)(2,1)}, bf16[384,768]{1,0:T(8,128)(2,1)S(1)}, u32[]{:S(2)}, u32[]{:S(2)}) collective-permute-start(bf16[384,768]{1,0:T(8,128)(2,1)} %add_convert_fusion), channel_id=1, source_target_pairs={{0,2},{1,3},{2,0},{3,1},{4,6},{5,7},{6,4},{7,5},{8,10},{9,11},{10,... | collective-permute-start | bytes 1769480 | tf_op jit(solution)/shard_map/ppermute | solution.py:1008
  271.5 20.3 %collective-permute-start.34 = (bf16[384,768]{1,0:T(8,128)(2,1)}, bf16[384,768]{1,0:T(8,128)(2,1)S(1)}, u32[]{:S(2)}, u32[]{:S(2)}) collective-permute-start(bf16[384,768]{1,0:T(8,128)(2,1)} %add_convert_fusion.1), channel_id=1, source_target_pairs={{6,2},{7,3},{0,4},{1,5},{10,6},{11,7},{4,8},{5,9},{14,10},{15,11},... | collective-permute-start | bytes 1769480 | tf_op jit(solution)/shard_map/ppermute | solution.py:1249
  (98 other events, 872.6 us)
Sparse Core Ops, SparseCore 0:
  64.5 60.6 all-gather.2
  164.0 74.4 reduce-scatter.2
  259.9 68.9 reduce-scatter.4
